TPU v7x, 256 devices: a whole 4x4x8 slice. The times are simulated.
256 devices in a mesh: dp: 32 (over x, z), tensor: 8 (over y, core).
Axes of the slice: x: 4, y: 4, z: 8, core: 2. Of those that a mesh axis runs over, the one named last changes fastest.
Arguments:
- context: bfloat16 [2, 32768, 3072], P(None, 'dp', 'tensor'), may hold values from -6 to 6
- out_grad: bfloat16 [2, 32768, 3072], P(None, ('dp', 'tensor')), may hold values from -0.1875 to 0.1875
- error_in: bfloat16 [2, 98304, 3072], P(None, 'dp', 'tensor'), may hold values from -6 to 6
- right_init: float32 [2, 64, 3072], P(None, None, 'tensor'), may hold values from -6 to 6
Outputs:
- summed_update: bfloat16 [2, 3072, 3072], P(None, 'dp', 'tensor')
- error_out: bfloat16 [2, 98304, 3072], P(None, 'dp', 'tensor')
All inputs are finite; a program needn't handle non-finite values.
Results may differ from a plain program's by a relative error of at most 0.015.
Values may be sent and summed in bfloat16 or wider, within the bound.
No kernel may reach another device: no remote copies, remote signals or barrier semaphores. Data moves between devices by JAX's collectives and lax.ppermute only.
A program may use at most 128 MiB of HBM per device.

v0:
```python
import jax
import jax.numpy as jnp
from jax import lax
from jax.sharding import Mesh
from jax.sharding import PartitionSpec as P

TENSOR = ("tensor_0", "tensor_1")
DP_TENSOR = ("dp_0", "dp_1", "tensor_0", "tensor_1")
DP = ("dp_0", "dp_1")


def cut_along(x, dim, devices):
    dims = x.shape
    parts = x.reshape(*dims[:dim], devices, dims[dim] // devices, *dims[dim + 1 :])
    return jnp.moveaxis(parts, dim, 0)


def sent_and_summed(x, axis, dim):
    devices = lax.axis_size(axis)
    parts = lax.all_to_all(cut_along(x, dim, devices), axis, 0, 0, tiled=True)
    return jnp.sum(parts, axis=0)


def sum_in_two_steps(x, axes, dim):
    far, near = axes
    own = sent_and_summed(cut_along(x, dim, lax.axis_size(far)), near, dim + 1)
    return jnp.sum(lax.all_to_all(own, far, 0, 0, tiled=True), axis=0)


def filled_up(lines, devices):
    spare = -lines.shape[0] % devices
    if not spare:
        return lines
    return jnp.concatenate([lines, jnp.zeros((spare, *lines.shape[1:]), lines.dtype)])


def copy_for_each(x, axis):
    devices = lax.axis_size(axis)
    return lax.all_to_all(jnp.broadcast_to(x[None], (devices, *x.shape)), axis, 0, 0, tiled=True)


def joined_along(parts, dim):
    dims = list(parts.shape[1:])
    dims[dim] *= parts.shape[0]
    return jnp.moveaxis(parts, 0, dim).reshape(dims)


def gathered_by_axis(x, axes, dim):
    far, near = axes
    initial = copy_for_each(x, far)
    parts = jnp.swapaxes(copy_for_each(initial, near), 0, 1)
    return joined_along(parts.reshape(-1, *x.shape), dim)


def nested_sum(x, axes):
    lines = x.reshape(-1)
    own = sum_in_two_steps(
        filled_up(lines, lax.axis_size(axes[0]) * lax.axis_size(axes[1])), axes, 0
    )
    whole = gathered_by_axis(own, axes, 0)
    return whole[: len(lines)].reshape(x.shape)


def gathered_copies(x, axis, dim):
    return joined_along(copy_for_each(x, axis), dim)


def summed_on_arrival(x, axis, dim):
    parts = cut_along(x, dim, lax.axis_size(axis))
    arrived = lax.all_to_all(parts, axis, split_axis=0, concat_axis=0, tiled=True)
    return arrived.astype(jnp.float32).sum(axis=0)


def nested_sum_2(x, axes):
    lines = x.reshape(-1, x.shape[-1])
    padded = filled_up(lines, lax.axis_size(axes))
    whole = gathered_copies(summed_on_arrival(padded, axes, 0).astype(jnp.bfloat16), axes, 0)
    return lax.slice_in_dim(whole, 0, len(lines)).reshape(x.shape).astype(jnp.float32)


def solve_rows(gram_matrix, left_factor):
    ridge_term = 1e-06 * jnp.mean(jnp.diagonal(gram_matrix, axis1=1, axis2=2), axis=1)
    eye_matrix = jnp.eye(gram_matrix.shape[1], dtype=gram_matrix.dtype)
    gram_matrix = gram_matrix + ridge_term[:, None, None] * eye_matrix
    factor_low = jnp.linalg.cholesky(gram_matrix)

    def one_solve(low_part, rhs_part):
        return jax.scipy.linalg.solve_triangular(low_part, rhs_part, lower=True)

    return jax.vmap(one_solve)(factor_low, left_factor)


def gram_of(left_factor):
    return jnp.einsum("lrd,lsd->lrs", left_factor, left_factor, precision=lax.Precision.HIGHEST)


def compress(context, out_grad, error_in, right_init):
    out_width = out_grad.shape[2]
    moment = jnp.einsum(
        "ltd,lte->lde",
        lax.all_gather(out_grad, TENSOR, axis=1, tiled=True),
        context,
        preferred_element_type=jnp.float32,
    )
    moment = moment + error_in.astype(jnp.float32)
    left_factor = jnp.einsum("lre,lde->lrd", right_init, moment, precision=lax.Precision.HIGHEST)
    left_factor = nested_sum(left_factor, (("dp_0", "dp_1"), ("tensor_0", "tensor_1")))
    ortho_basis = solve_rows(gram_of(left_factor), left_factor)
    right_terms = jnp.einsum("lrd,lde->lre", ortho_basis, moment, precision=lax.Precision.HIGHEST)
    right_factor = nested_sum_2(right_terms.astype(jnp.bfloat16), DP)
    replicas = lax.axis_size(DP)
    row_share = out_width // replicas
    own_basis = lax.dynamic_slice_in_dim(ortho_basis, lax.axis_index(DP) * row_share, row_share, 2)
    summed = jnp.einsum("lrd,lre->lde", own_basis, right_factor, precision=lax.Precision.HIGHEST)
    mean_part = jnp.einsum(
        "lrd,lre->lde", ortho_basis, right_factor / replicas, precision=lax.Precision.HIGHEST
    )
    new_error = (moment - mean_part).astype(jnp.bfloat16)
    return (summed.astype(jnp.bfloat16), new_error)


def body(context, out_grad, error_in, right_init):
    return compress(context, out_grad, error_in, right_init)


def solution(mesh):
    finer = Mesh(mesh.devices.reshape(4, 8, 4, 2), ("dp_0", "dp_1", "tensor_0", "tensor_1"))
    return jax.shard_map(
        body,
        mesh=finer,
        in_specs=(
            P(None, DP, TENSOR),
            P(None, DP_TENSOR, None),
            P(None, DP, TENSOR),
            P(None, None, TENSOR),
        ),
        out_specs=(P(None, DP, TENSOR), P(None, DP, TENSOR)),
        check_vma=False,
    )
```

profile of v0, /device:TPU:2, one launch (start us, length us, event | category | flops | bytes accessed | tf_op | source)
XLA Modules:
  0.0 293.3 jit_solution(1838412830930112913)
XLA Ops:
  7.2 0.0 copy-start
  7.2 0.0 all-gather.2.cloned.1.call-start
  7.2 2.7 copy.16
  9.9 0.0 all-gather.2.cloned.1.call-update
  9.9 0.0 copy-start.3
  9.9 77.6 %all-gather.2.cloned.1.call-done = bf16[2,1024,3072]{1,2,0:T(8,128)(2,1)} async-done(((bf16[2,128,3072]{1,2,0:T(8,128)(2,1)}), bf16[2,1024,3072]{1,2,0:T(8,128)(2,1)}) %all-gather.2.cloned.1.call-update) | async-done | bytes 12582928 | tf_op jit(solution)/shard_map/all_gather | solution.py:101
  87.5 0.0 copy-done
  87.5 10.4 %convert_add_fusion = f32[2,3072,384]{2,1,0:T(8,128)S(1)} fusion(bf16[2,3072,384]{2,1,0:T(8,128)(2,1)} %param.6, bf16[2,1024,3072]{1,2,0:T(8,128)(2,1)} %all-gather.2.cloned.1.call-done, bf16[2,1024,384]{2,1,0:T(8,128)(2,1)S(1)} %copy-done), kind=kOutput, calls=%fused_computation.2 | convolution fusion | flops 4836556800 | bytes 28311552 | tf_op jit(solution)/shard_map/ltd,lte->lde/dot_general | solution.py:99
  97.9 0.0 copy-start.1
  97.9 3.6 %copy-done.1 = f32[2,3072,384]{2,1,0:T(8,128)} copy-done((f32[2,3072,384]{2,1,0:T(8,128)}, f32[2,3072,384]{2,1,0:T(8,128)S(1)}, u32[]{:S(2)}) %copy-start.1) | copy-done | bytes 9437208
  101.6 0.0 copy-done.3
  101.6 10.7 %convolution_bitcast_fusion = f32[2,64,3072]{2,1,0:T(8,128)} fusion(f32[2,3072,384]{2,1,0:T(8,128)S(1)} %convert_add_fusion, f32[2,64,384]{2,1,0:T(8,128)S(1)} %copy-done.3), kind=kOutput, calls=%fused_computation.3 | convolution fusion | flops 1811939328 | bytes 11206656 | tf_op jit(solution)/shard_map/lre,lde->lrd/dot_general | solution.py:106
  112.3 1.7 reshape_reshape_reshape.6
  114.0 0.9 copy.26
  114.9 25.4 %all_to_all.35 = f32[8,32,1536]{2,1,0:T(8,128)S(1)} all-to-all(f32[8,32,1536]{2,1,0:T(8,128)S(1)} %bitcast.34), channel_id=1, replica_groups=mesh['dp_0'=4,'dp_1'=8,'tensor_0'=4,'tensor_1'=2] {'tensor_0','tensor_1'}, dimensions={0} | all-to-all | bytes 3145728 | tf_op jit(solution)/shard_map/all_to_all | solution.py:20
  140.3 0.1 reduce_sum.39
  140.4 0.1 all_to_all.23
  140.5 19.7 %all_to_all.36 = f32[32,1,1536]{2,1,0:T(1,128)S(1)} all-to-all(f32[32,1,1536]{2,1,0:T(1,128)S(1)} %all_to_all.23), channel_id=1, replica_groups=mesh['dp_0'=4,'dp_1'=8,'tensor_0'=4,'tensor_1'=2] {'dp_0','dp_1'}, dimensions={0} | all-to-all | bytes 393216 | tf_op jit(solution)/shard_map/all_to_all | solution.py:27
  160.2 0.1 reduce_sum.40
  160.4 0.1 broadcast_in_dim.14
  160.5 14.6 %all_to_all.37 = f32[32,1,1536]{2,1,0:T(1,128)S(1)} all-to-all(f32[32,1,1536]{2,1,0:T(1,128)S(1)} %broadcast_in_dim.14), channel_id=1, replica_groups=mesh['dp_0'=4,'dp_1'=8,'tensor_0'=4,'tensor_1'=2] {'dp_0','dp_1'}, dimensions={0} | all-to-all | bytes 393216 | tf_op jit(solution)/shard_map/all_to_all | solution.py:39
  175.1 1.3 broadcast_in_dim.18
  176.4 3.6 %all-to-all-start.3 = ((f32[8,32,1536]{2,1,0:T(8,128)}), f32[8,32,1536]{2,1,0:T(8,128)S(1)}, u32[]{:S(2)}, u32[]{:S(2)}) async-start(f32[8,32,1536]{2,1,0:T(8,128)} %broadcast_in_dim.18), calls=%async_computation.3 | async-start | bytes 3145728 | tf_op jit(solution)/shard_map/all_to_all | solution.py:39
  180.1 21.4 %all-to-all-done.3 = f32[8,32,1536]{2,1,0:T(8,128)S(1)} async-done(((f32[8,32,1536]{2,1,0:T(8,128)}), f32[8,32,1536]{2,1,0:T(8,128)S(1)}, u32[]{:S(2)}, u32[]{:S(2)}) %all-to-all-start.3) | async-done | bytes 1572896 | tf_op jit(solution)/shard_map/all_to_all | solution.py:39
  201.5 2.1 copy.18
  203.5 1.8 reshape_reshape_reshape.7
  205.3 1.6 fusion.12
  206.9 2.0 copy.19
  208.9 0.1 copy.20
  209.0 1.6 gather_fusion
  210.7 0.1 fusion.6
  210.7 11.7 %custom-call.8 = f32[2,64,64]{2,1,0:T(8,128)S(1)} custom-call(f32[2,64,64]{2,1,0:T(8,128)S(1)} %fusion.6), custom_call_target="Cholesky" | custom-call | tf_op jit(solution)/shard_map/jit(cholesky)/cholesky | solution.py:85
  222.5 0.1 compare_reduce_fusion
  222.6 0.1 select_bitcast_fusion
  222.7 9.8 %custom-call.9 = f32[2,1,64,64]{2,3,1,0:T(8,128)S(1)} custom-call(f32[2,1,64,64]{3,2,1,0:T(8,128)S(1)} %select_bitcast_fusion), custom_call_target="InvertDiagBlocksLowerTriangular" | custom-call | tf_op jit(solution)/shard_map/vmap(jit(_solve_triangular))/triangular_solve | solution.py:88
  232.5 1.5 fusion.3
  234.1 0.0 copy-start.2
  234.1 1.2 copy-done.2
  235.2 8.2 %convolution_convert_fusion.1 = bf16[2,64,384]{2,1,0:T(8,128)(2,1)S(1)} fusion(f32[2,64,3072]{2,1,0:T(8,128)S(1)} %fusion.3, f32[2,3072,384]{2,1,0:T(8,128)} %copy-done.1), kind=kOutput, calls=%fused_computation.6 | convolution fusion | flops 1811988480 | bytes 11108352 | tf_op jit(solution)/shard_map/lrd,lde->lre/dot_general | solution.py:109
  243.4 14.0 %all_to_all.38 = bf16[32,4,384]{2,1,0:T(4,128)(2,1)S(1)} all-to-all(bf16[32,4,384]{2,1,0:T(4,128)(2,1)S(1)} %reshape_reshape.6), channel_id=1, replica_groups=mesh['dp_0'=4,'dp_1'=8,'tensor_0'=4,'tensor_1'=2] {'dp_0','dp_1'}, dimensions={0} | all-to-all | bytes 196608 | tf_op jit(solution)/shard_map/all_to_all | solution.py:70
  257.5 0.1 reduce_sum.42
  257.5 0.7 broadcast_in_dim.19
  258.2 5.0 %all-to-all-start.5 = ((bf16[32,4,384]{2,1,0:T(4,128)(2,1)}), bf16[32,4,384]{2,1,0:T(4,128)(2,1)S(1)}, u32[]{:S(2)}, u32[]{:S(2)}) async-start(bf16[32,4,384]{2,1,0:T(4,128)(2,1)} %broadcast_in_dim.19), calls=%async_computation.5 | async-start | bytes 196608 | tf_op jit(solution)/shard_map/all_to_all | solution.py:39
  263.2 9.1 %all-to-all-done.5 = bf16[32,4,384]{2,1,0:T(4,128)(2,1)S(1)} async-done(((bf16[32,4,384]{2,1,0:T(4,128)(2,1)}), bf16[32,4,384]{2,1,0:T(4,128)(2,1)S(1)}, u32[]{:S(2)}, u32[]{:S(2)}) %all-to-all-start.5) | async-done | bytes 98336 | tf_op jit(solution)/shard_map/all_to_all | solution.py:39
  272.3 12.1 %subtract_convert_fusion = bf16[2,3072,384]{2,1,0:T(8,128)(2,1)} fusion(f32[2,3072,384]{2,1,0:T(8,128)} %copy-done.1, f32[2,64,3072]{2,1,0:T(8,128)} %copy-done.2, bf16[2,64,384]{2,1,0:T(8,128)(2,1)S(1)} %reshape_reshape.7), kind=kOutput, calls=%fused_computation.1 | convolution fusion | flops 1816756224 | bytes 15826944 | tf_op jit(solution)/shard_map/lrd,lre->lde/dot_general | solution.py:115
  284.5 2.0 convolution_convert_fusion
  (10 shorter events, 0.2 us)
Async XLA Ops:
  7.2 80.4 %copy-start = (bf16[2,1024,384]{2,1,0:T(8,128)(2,1)S(1)}, bf16[2,1024,384]{2,1,0:T(8,128)(2,1)}, u32[]{:S(2)}) copy-start(bf16[2,1024,384]{2,1,0:T(8,128)(2,1)} %param.4) | copy-start | bytes 4718596
  7.2 80.3 %all-gather.2.cloned.1.call-start = ((), (), s32[]{:S(2)}) async-start(), calls=%async_computation.6 | async-start | bytes 14155776 | tf_op jit(solution)/shard_map/all_gather | solution.py:101
  9.9 91.6 %copy-start.3 = (f32[2,64,384]{2,1,0:T(8,128)S(1)}, f32[2,64,384]{2,1,0:T(8,128)}, u32[]{:S(2)}) copy-start(f32[2,64,384]{2,1,0:T(8,128)} %param.7) | copy-start | bytes 589828
  97.9 3.6 %copy-start.1 = (f32[2,3072,384]{2,1,0:T(8,128)}, f32[2,3072,384]{2,1,0:T(8,128)S(1)}, u32[]{:S(2)}) copy-start(f32[2,3072,384]{2,1,0:T(8,128)S(1)} %convert_add_fusion) | copy-start | bytes 28311556
  176.4 25.1 %all-to-all-start.3 = ((f32[8,32,1536]{2,1,0:T(8,128)}), f32[8,32,1536]{2,1,0:T(8,128)S(1)}, u32[]{:S(2)}, u32[]{:S(2)}) async-start(f32[8,32,1536]{2,1,0:T(8,128)} %broadcast_in_dim.18), calls=%async_computation.3 | async-start | bytes 3145728 | tf_op jit(solution)/shard_map/all_to_all | solution.py:39
  234.1 1.2 copy-start.2
  258.2 14.1 %all-to-all-start.5 = ((bf16[32,4,384]{2,1,0:T(4,128)(2,1)}), bf16[32,4,384]{2,1,0:T(4,128)(2,1)S(1)}, u32[]{:S(2)}, u32[]{:S(2)}) async-start(bf16[32,4,384]{2,1,0:T(4,128)(2,1)} %broadcast_in_dim.19), calls=%async_computation.5 | async-start | bytes 196608 | tf_op jit(solution)/shard_map/all_to_all | solution.py:39
Sparse Core Ops, SparseCore 0:
  10.4 77.0 all-gather.1
where the time goes:
time: 294 us; the launch traced here: 293 us
  waiting for transfers between devices  108 us (37%)
  blocking collectives  73.7 us (25%)
  matrix products  46.4 us (16%)
  other arithmetic  22.2 us (8%)
  local copies, waits for them, and re-layouts  20 us (7%)
  between operations  14.2 us (5%)
  starting transfers between devices  8.59 us (3%)
    all_gather x1, waiting for transfers between devices, compress(): lax.all_gather(out_grad, TENSOR, axis=1, tiled=True)  77.6 us
    all_to_all x2, waiting for transfers between devices, copy_for_each(): lax.all_to_all(jnp.broadcast_to(x[None], (devices, *x.shape)), axis, 0, 0...  30.5 us
    all_to_all x1, blocking collectives, sent_and_summed(): parts = lax.all_to_all(cut_along(x, dim, devices), axis, 0, 0, tiled=True)  25.4 us
    all_to_all x1, blocking collectives, sum_in_two_steps(): return jnp.sum(lax.all_to_all(own, far, 0, 0, tiled=True), axis=0)  19.7 us
    all_to_all x1, blocking collectives, copy_for_each(): lax.all_to_all(jnp.broadcast_to(x[None], (devices, *x.shape)), axis, 0, 0...  14.6 us
    all_to_all x1, blocking collectives, summed_on_arrival(): lax.all_to_all(parts, axis, split_axis=0, concat_axis=0, tiled=True)  14 us
    dot_general x1, matrix products, compress(): jnp.einsum('lrd,lre->lde', ortho_basis, right_factor / replicas, precisio...  12.1 us
    another operation x4, other arithmetic, solve_rows(): factor_low = jnp.linalg.cholesky(gram_matrix)  11.9 us
  transfers between devices with their start and end apart: 3, of which 3 were waited for; matrix products, arithmetic and copies ran while one was open for 0% of the time, Pallas kernels for 0%

commit v1 on v0

v1 whole, which is shorter than its diff:
```python
import functools

import jax
import jax.numpy as jnp
from jax import lax
from jax.experimental import pallas as pl
from jax.experimental.pallas import tpu as pltpu
from jax.sharding import Mesh
from jax.sharding import PartitionSpec as P

TENSOR = ("tensor_0", "tensor_1")
DP_TENSOR = ("dp_0", "dp_1", "tensor_0", "tensor_1")
DP = ("dp_0", "dp_1")
WIDE = ("dp_0", "dp_1", "tensor_0")
F32, BF16 = jnp.float32, jnp.bfloat16
HIGHEST = lax.Precision.HIGHEST
VMEM = pl.BlockSpec(memory_space=pltpu.VMEM)
SMEM = pl.BlockSpec(memory_space=pltpu.SMEM)


def room(mib):
    return pltpu.CompilerParams(vmem_limit_bytes=mib * 1024 * 1024)


def cost(flops, nbytes):
    return pl.CostEstimate(flops=int(flops), bytes_accessed=int(nbytes), transcendentals=0)


def two_parts(x):
    high = x.astype(BF16)
    return high, (x - high.astype(F32)).astype(BF16)


def dot(a, b, dims, **kw):
    return lax.dot_general(a, b, (dims, ((), ())), preferred_element_type=F32, **kw)


def sketch_kernel(r_ref, x_ref, o_ref):
    rank = r_ref.shape[1]
    for layer in range(r_ref.shape[0]):
        stacked = jnp.concatenate(two_parts(r_ref[layer]), axis=0)
        z = dot(stacked, x_ref[layer], ((1,), (1,)))
        z = (z[:rank] + z[rank:]).astype(BF16)
        for j in range(o_ref.shape[0]):
            o_ref[j, layer] = z[:, j * 128 : (j + 1) * 128]


def sketch(right_init, context):
    layers, rank, _ = right_init.shape
    tokens = context.shape[1]
    return pl.pallas_call(
        sketch_kernel,
        out_shape=jax.ShapeDtypeStruct((tokens // 128, layers, rank, 128), BF16),
        in_specs=[VMEM, VMEM],
        out_specs=VMEM,
        cost_estimate=cost(4e8, 2e6),
        name="sketch",
        compiler_params=room(6),
    )(right_init, context)


def error_sketch_kernel(r_ref, e_ref, o_ref):
    rank = r_ref.shape[1]
    stacked = jnp.concatenate(two_parts(r_ref[0]), axis=0)
    z = dot(stacked, e_ref[0], ((1,), (1,)))
    o_ref[0] = z[:rank] + z[rank:]


def error_sketch(right_init, error_in):
    layers, rank, width = right_init.shape
    rows = error_in.shape[1]
    step = 768
    return pl.pallas_call(
        error_sketch_kernel,
        out_shape=jax.ShapeDtypeStruct((layers, rank, rows), F32),
        grid=(layers, rows // step),
        in_specs=[
            pl.BlockSpec((1, rank, width), lambda l, d: (l, 0, 0)),
            pl.BlockSpec((1, step, width), lambda l, d: (l, d, 0)),
        ],
        out_specs=pl.BlockSpec((1, rank, step), lambda l, d: (l, 0, d)),
        cost_estimate=cost(6e8, 7e6),
        name="error_sketch",
        compiler_params=room(6),
    )(right_init, error_in)


def left_term_kernel(core_ref, z_ref, y_ref, e_ref, send_ref, keep_ref):
    rank = z_ref.shape[2]
    core = core_ref[0]
    for which, out in ((1 - core, send_ref), (core, keep_ref)):
        z = z_ref[0, which].astype(F32)
        for j in range(1, z_ref.shape[0]):
            z = z + z_ref[j, which].astype(F32)
        t = dot(jnp.concatenate(two_parts(z), axis=0), y_ref[which], ((1,), (0,)))
        out[...] = (t[:rank] + t[rank:] + e_ref[which]).astype(BF16)


def left_term(core, z, own_grad, error_part):
    rank, rows = error_part.shape[1:]
    shape = jax.ShapeDtypeStruct((rank, rows), BF16)
    return pl.pallas_call(
        left_term_kernel,
        out_shape=(shape, shape),
        in_specs=[SMEM, VMEM, VMEM, VMEM],
        out_specs=(VMEM, VMEM),
        cost_estimate=cost(2e8, 5e6),
        name="left_term",
        compiler_params=room(12),
    )(core, z, own_grad, error_part)


def cut_kernel(a_ref, b_ref, o_ref):
    bands, lanes = a_ref.shape[0] // 16, a_ref.shape[1] // 128
    for i in range(bands):
        for j in range(lanes):
            rows, cols = slice(i * 16, i * 16 + 16), slice(j * 128, j * 128 + 128)
            both = a_ref[rows, cols].astype(F32) + b_ref[rows, cols].astype(F32)
            o_ref[i * lanes + j] = both.astype(BF16)
    for p in range(bands * lanes, o_ref.shape[0]):
        o_ref[p] = jnp.zeros(o_ref.shape[1:], BF16)


def cut(a, b, pieces):
    return pl.pallas_call(
        cut_kernel,
        out_shape=jax.ShapeDtypeStruct((pieces, 16, 128), BF16),
        in_specs=[VMEM, VMEM],
        out_specs=VMEM,
        cost_estimate=cost(4e5, 1.2e6),
        name="cut",
        compiler_params=room(4),
    )(a, b)


def sum_copies_kernel(x_ref, o_ref):
    parts = [x_ref[p].astype(F32) for p in range(4)]
    for p in range(4, x_ref.shape[0], 4):
        for q in range(4):
            parts[q] = parts[q] + x_ref[p + q].astype(F32)
    total = ((parts[0] + parts[1]) + (parts[2] + parts[3])).astype(BF16)
    for p in range(o_ref.shape[0]):
        o_ref[p] = total


def sum_copies(x):
    return pl.pallas_call(
        sum_copies_kernel,
        out_shape=jax.ShapeDtypeStruct(x.shape, BF16),
        in_specs=[VMEM],
        out_specs=VMEM,
        cost_estimate=cost(x.size, x.size * 4),
        name="sum_copies",
        compiler_params=room(4),
    )(x)


def moment_kernel(y_ref, x_ref, e_ref, o_ref):
    y = jnp.concatenate([y_ref[k, 0] for k in range(y_ref.shape[0])], axis=1)
    o_ref[0] = dot(y, x_ref[0], ((1,), (0,))) + e_ref[0].astype(F32)


def moment_of(grad_t, context, error_in):
    blocks, layers, rows, _ = grad_t.shape
    tokens, width = context.shape[1:]
    step = 512
    return pl.pallas_call(
        moment_kernel,
        out_shape=jax.ShapeDtypeStruct((layers, rows, width), F32),
        grid=(layers, rows // step),
        in_specs=[
            pl.BlockSpec((blocks, 1, step, 128), lambda l, d: (0, l, d, 0)),
            pl.BlockSpec((1, tokens, width), lambda l, d: (l, 0, 0)),
            pl.BlockSpec((1, step, width), lambda l, d: (l, d, 0)),
        ],
        out_specs=pl.BlockSpec((1, step, width), lambda l, d: (l, d, 0)),
        cost_estimate=cost(5e9, 28e6),
        name="moment",
        compiler_params=room(60),
    )(grad_t, context, error_in)


def join_kernel(core_ref, own_ref, other_ref, l_ref):
    core = core_ref[0]
    bands, lanes = l_ref.shape[1] // 16, l_ref.shape[2] // 128
    for which, ref in ((core, own_ref), (1 - core, other_ref)):
        for i in range(bands):
            for j in range(lanes):
                l_ref[which, i * 16 : i * 16 + 16, j * 128 : j * 128 + 128] = ref[i * lanes + j]


def join(core, own, other, rank, rows):
    return pl.pallas_call(
        join_kernel,
        out_shape=jax.ShapeDtypeStruct((2, rank, rows), BF16),
        in_specs=[SMEM, VMEM, VMEM],
        out_specs=VMEM,
        cost_estimate=cost(1e5, 2e6),
        name="join",
        compiler_params=room(4),
    )(core, own, other)


def right_term_kernel(l_ref, m_ref, o_ref, acc_ref):
    layer, d = pl.program_id(0), pl.program_id(1)
    part = dot(l_ref[0], m_ref[0].astype(BF16), ((1,), (0,)))

    @pl.when(d == 0)
    def _():
        acc_ref[...] = part

    @pl.when(d > 0)
    def _():
        acc_ref[...] += part

    @pl.when(d == pl.num_programs(1) - 1)
    def _():
        bands, lanes = acc_ref.shape[0] // 16, acc_ref.shape[1] // 128
        for i in range(bands):
            for j in range(lanes):
                piece = acc_ref[i * 16 : i * 16 + 16, j * 128 : j * 128 + 128]
                o_ref[(layer * bands + i) * lanes + j] = piece.astype(BF16)

    @pl.when((layer == 0) & (d == 0))
    def _():
        bands, lanes = acc_ref.shape[0] // 16, acc_ref.shape[1] // 128
        for p in range(2 * bands * lanes, o_ref.shape[0]):
            o_ref[p] = jnp.zeros(o_ref.shape[1:], BF16)


def right_term(left, moment, pieces):
    layers, rank, rows = left.shape
    width = moment.shape[2]
    step = 768
    return pl.pallas_call(
        right_term_kernel,
        out_shape=jax.ShapeDtypeStruct((pieces, 16, 128), BF16),
        grid=(layers, rows // step),
        in_specs=[
            pl.BlockSpec((1, rank, step), lambda l, d: (l, 0, d)),
            pl.BlockSpec((1, step, width), lambda l, d: (l, d, 0)),
        ],
        out_specs=pl.BlockSpec((pieces, 16, 128), lambda l, d: (0, 0, 0)),
        scratch_shapes=[pltpu.VMEM((rank, width), F32)],
        cost_estimate=cost(4e8, 10e6),
        name="right_term",
        compiler_params=room(50),
    )(left, moment)


def inverse_kernel(l_ref, o_ref):
    rank = l_ref.shape[1]
    row = lax.broadcasted_iota(jnp.int32, (rank, 2 * rank), 0)
    col = lax.broadcasted_iota(jnp.int32, (rank, 2 * rank), 1)
    work = []
    for layer in range(l_ref.shape[0]):
        left = l_ref[layer]
        gram = dot(left, left, ((1,), (1,)))
        wide = jnp.concatenate([gram, jnp.zeros((rank, rank), F32)], axis=1)
        diag = jnp.sum(jnp.where(row == col, wide, 0.0), axis=1, keepdims=True)
        ridge = 1e-6 * (jnp.sum(diag, axis=0, keepdims=True) / rank)
        wide = wide + jnp.where(row == col, ridge, 0.0)
        work.append(jnp.where(col == row + rank, 1.0, wide))
    for k in range(rank):
        for layer in range(len(work)):
            a = work[layer]
            pivot_row = a[k : k + 1, :] / a[k : k + 1, k : k + 1]
            column = a[:, k : k + 1]
            work[layer] = jnp.where(row == k, pivot_row, a - column * pivot_row)
    for layer in range(len(work)):
        o_ref[layer] = work[layer][:, rank:]


def inverse_of_gram(left):
    layers, rank, _ = left.shape
    return pl.pallas_call(
        inverse_kernel,
        out_shape=jax.ShapeDtypeStruct((layers, rank, rank), F32),
        in_specs=[VMEM],
        out_specs=VMEM,
        cost_estimate=cost(5e9, 2e6),
        name="gram_inverse",
        compiler_params=room(4),
    )(left)


def outputs_kernel(r_ref, g_ref, l_ref, own_ref, m_ref, s_ref, e_ref, q_ref, *, replicas):
    layer, d = pl.program_id(0), pl.program_id(1)
    rank, width = g_ref.shape[1], m_ref.shape[2]
    bands, lanes = rank // 16, width // 128

    @pl.when(d == 0)
    def _():
        rows = [
            jnp.concatenate([r_ref[(layer * bands + i) * lanes + j] for j in range(lanes)], axis=1)
            for i in range(bands)
        ]
        right = jnp.concatenate(rows, axis=0).astype(F32)
        q = dot(g_ref[0], right, ((1,), (0,)), precision=HIGHEST)
        q_ref[...] = jnp.concatenate(two_parts(q), axis=0)
        own = own_ref[0]
        s = dot(jnp.concatenate([own, own], axis=0), q_ref[...], ((0,), (0,)))
        s_ref[0] = s.astype(BF16)

    left = l_ref[0]
    both = jnp.concatenate([left, left], axis=0)
    mean = dot(both, q_ref[...], ((0,), (0,))) * (1.0 / replicas)
    e_ref[0] = (m_ref[0] - mean).astype(BF16)


def outputs(right, inverse, left, own_left, moment, replicas):
    layers, rows, width = moment.shape
    rank = left.shape[1]
    share = own_left.shape[2]
    step = 768
    return pl.pallas_call(
        functools.partial(outputs_kernel, replicas=replicas),
        out_shape=(
            jax.ShapeDtypeStruct((layers, share, width), BF16),
            jax.ShapeDtypeStruct((layers, rows, width), BF16),
        ),
        grid=(layers, rows // step),
        in_specs=[
            pl.BlockSpec(right.shape, lambda l, d: (0, 0, 0)),
            pl.BlockSpec((1, rank, rank), lambda l, d: (l, 0, 0)),
            pl.BlockSpec((1, rank, step), lambda l, d: (l, 0, d)),
            pl.BlockSpec((1, rank, share), lambda l, d: (l, 0, 0)),
            pl.BlockSpec((1, step, width), lambda l, d: (l, d, 0)),
        ],
        out_specs=(
            pl.BlockSpec((1, share, width), lambda l, d: (l, 0, 0)),
            pl.BlockSpec((1, step, width), lambda l, d: (l, d, 0)),
        ),
        scratch_shapes=[pltpu.VMEM((2 * rank, width), BF16)],
        cost_estimate=cost(6e8, 15e6),
        name="outputs",
        compiler_params=room(50),
    )(right, inverse, left, own_left, moment)


def exchanged(x, axis):
    return lax.all_to_all(x, axis, 0, 0, tiled=True)


def body(context, out_grad, error_in, right_init):
    rank, rows = right_init.shape[1], out_grad.shape[2]
    core = lax.axis_index("tensor_1").astype(jnp.int32).reshape(1)
    grad_t = lax.all_gather(jnp.swapaxes(out_grad, 1, 2), TENSOR, axis=0, tiled=False)

    z = exchanged(sketch(right_init, context), TENSOR)
    error_part = error_sketch(right_init, error_in)
    send, keep = left_term(core, z, out_grad, error_part)
    swap = [(0, 1), (1, 0)]
    arrived = lax.ppermute(send, "tensor_1", swap)
    terms = exchanged(cut(keep, arrived, lax.axis_size(WIDE)), WIDE)
    own = exchanged(sum_copies(terms), WIDE)
    other = lax.ppermute(own, "tensor_1", swap)
    left = join(core, own, other, rank, rows)

    moment = moment_of(grad_t, context, error_in)
    replicas = lax.axis_size(DP)
    right = exchanged(right_term(left, moment, replicas), DP)
    right = exchanged(sum_copies(right), DP)
    inverse = inverse_of_gram(left)
    share = rows // replicas
    own_left = lax.dynamic_slice_in_dim(left, lax.axis_index(DP) * share, share, 2)
    return outputs(right, inverse, left, own_left, moment, replicas)


def solution(mesh):
    finer = Mesh(mesh.devices.reshape(4, 8, 4, 2), ("dp_0", "dp_1", "tensor_0", "tensor_1"))
    return jax.shard_map(
        body,
        mesh=finer,
        in_specs=(
            P(None, DP, TENSOR),
            P(None, DP_TENSOR, None),
            P(None, DP, TENSOR),
            P(None, None, TENSOR),
        ),
        out_specs=(P(None, DP, TENSOR), P(None, DP, TENSOR)),
        check_vma=False,
    )
```

time: 294 us -> 171 us (0.58)
  waiting for transfers between devices: 108 us -> 26.6 us
  matrix products: 46.4 us -> 0 us
  Pallas kernels: 0 us -> 44.4 us
  other arithmetic: 22.2 us -> 0 us
  blocking collectives: 73.7 us -> 57.9 us
  local copies, waits for them, and re-layouts: 20 us -> 6.78 us
  starting transfers between devices: 8.59 us -> 19.7 us
    all_gather x1, waiting for transfers between devices: 77.6 us -> 8.34 us  [body(): lax.all_gather(jnp.swapaxes(out_grad, 1, 2), TENSOR, axis=0, tiled=False)]
    dot_general x6 -> x0, matrix products: 44.9 us -> none  [the longest x1 12.1 us: compress(): jnp.einsum('lrd,lre->lde', ortho_basis, right_factor / replicas, precisio...]
    pallas_call x0 -> x11, Pallas kernels: none -> 44.4 us  [the longest x1 16.1 us: moment_of(): pl.pallas_call(moment_kernel, out_shape=jax.ShapeDtypeStruct((layers, row...]
    another operation x7 -> x0, other arithmetic: 21.8 us -> none  [the longest x4 11.9 us: solve_rows(): factor_low = jnp.linalg.cholesky(gram_matrix)]
    all_to_all x2 -> x3, waiting for transfers between devices: 30.5 us -> 14.3 us  [exchanged(): return lax.all_to_all(x, axis, 0, 0, tiled=True)]
    all_to_all x4 -> x2, blocking collectives: 73.7 us -> 57.9 us  [exchanged(): return lax.all_to_all(x, axis, 0, 0, tiled=True)]
    all_to_all x2 -> x3, starting transfers between devices: 8.56 us -> 19.6 us  [exchanged(): return lax.all_to_all(x, axis, 0, 0, tiled=True)]
    another operation x5 -> x0, local copies, waits for them, and re-layouts: 4.47 us -> none  [the longest x3 2.65 us: cut_along(): x.reshape(*dims[:dim], devices, dims[dim] // devices, *dims[dim + 1:])]
  transfers between devices with their start and end apart: 3 -> 6, of which waited for: 3 -> 6; matrix products, arithmetic and copies ran while one was open for 0% -> 0% of each run, Pallas kernels for 0% -> 6%
where the time goes in v1:
time: 171 us; the launch traced here: 170 us
  blocking collectives  57.9 us (34%)
  Pallas kernels  44.4 us (26%)
  waiting for transfers between devices  26.6 us (16%)
  starting transfers between devices  19.7 us (12%)
  between operations  14.2 us (8%)
  local copies, waits for them, and re-layouts  6.78 us (4%)
    all_to_all x2, blocking collectives, exchanged(): return lax.all_to_all(x, axis, 0, 0, tiled=True)  57.9 us
    all_to_all x3, starting transfers between devices, exchanged(): return lax.all_to_all(x, axis, 0, 0, tiled=True)  19.6 us
    pallas_call x1, Pallas kernels, moment_of(): pl.pallas_call(moment_kernel, out_shape=jax.ShapeDtypeStruct((layers, row...  16.1 us
    all_to_all x3, waiting for transfers between devices, exchanged(): return lax.all_to_all(x, axis, 0, 0, tiled=True)  14.3 us
    pallas_call x1, Pallas kernels, outputs(): pl.pallas_call(functools.partial(outputs_kernel, replicas=replicas), out_...  9.97 us
    all_gather x1, waiting for transfers between devices, body(): lax.all_gather(jnp.swapaxes(out_grad, 1, 2), TENSOR, axis=0, tiled=False)  8.34 us
    pallas_call x1, Pallas kernels, right_term(): pl.pallas_call(right_term_kernel, out_shape=jax.ShapeDtypeStruct((pieces,...  7.4 us
    unnamed x13, local copies, waits for them, and re-layouts  6.69 us
  transfers between devices with their start and end apart: 6, of which 6 were waited for; matrix products, arithmetic and copies ran while one was open for 0% of the time, Pallas kernels for 6%

profile of v1, /device:TPU:2, one launch (start us, length us, event | category | flops | bytes accessed | tf_op | source)
XLA Modules:
  0.0 169.5 jit_solution(4795096132651552856)
XLA Ops:
  7.2 0.0 copy-start.4
  7.2 0.0 copy-start.2
  7.2 0.0 all-gather.3.cloned.1.call-start
  7.2 2.7 %copy.7 = bf16[2,128,3072]{1,2,0:T(8,128)(2,1)} copy(bf16[2,128,3072]{2,1,0:T(8,128)(2,1)} %y_ref.1) | data formatting | bytes 3145728 | tf_op args[1]
  9.9 0.0 all-gather.3.cloned.1.call-update
  10.0 0.0 copy-done.4
  10.0 0.0 copy-done.2
  10.0 0.0 copy-start.1
  10.0 0.6 sketch.1
  10.6 0.0 copy-start.3
  10.6 0.7 copy-done.3
  11.3 4.5 %all-to-all-start = ((bf16[8,2,64,128]{3,2,1,0:T(8,128)(2,1)}), bf16[8,2,64,128]{3,2,1,0:T(8,128)(2,1)S(1)}, u32[]{:S(2)}, u32[]{:S(2)}) async-start(bf16[8,2,64,128]{3,2,1,0:T(8,128)(2,1)} %copy-done.3), calls=%async_computation | async-start | bytes 524288 | tf_op jit(solution)/shard_map/all_to_all | solution.py:342
  15.8 0.0 copy-start
  15.8 2.3 %copy-done = bf16[2,3072,384]{2,1,0:T(8,128)(2,1)S(1)} copy-done((bf16[2,3072,384]{2,1,0:T(8,128)(2,1)S(1)}, bf16[2,3072,384]{2,1,0:T(8,128)(2,1)}, u32[]{:S(2)}) %copy-start) | copy-done | bytes 4718616
  18.2 0.0 copy-start.5
  18.2 0.9 copy-done.5
  19.1 2.7 %error_sketch.1.e_ref = f32[2,64,3072]{2,1,0:T(8,128)S(1)} custom-call(f32[2,64,384]{2,1,0:T(8,128)S(1)} %copy-done.5, bf16[2,3072,384]{2,1,0:T(8,128)(2,1)S(1)} %copy-done), custom_call_target="tpu_custom_call" | custom-call | flops 600000000 | bytes 7000000 | tf_op jit(solution)/shard_map/error_sketch/pallas_call | solution.py:73
  21.8 1.5 all-to-all-done.z_ref
  23.3 0.0 copy-done.1
  23.3 0.6 left_term.1
  23.9 0.1 collective-permute-start
  24.0 1.7 %collective-permute-done.b_ref = bf16[64,3072]{1,0:T(8,128)(2,1)S(1)} collective-permute-done((bf16[64,3072]{1,0:T(8,128)(2,1)S(1)}, bf16[64,3072]{1,0:T(8,128)(2,1)S(1)}, u32[]{:S(2)}, u32[]{:S(2)}) %collective-permute-start) | collective-permute-done | bytes 393248 | tf_op jit(solution)/shard_map/ppermute | solution.py:354
  25.7 0.1 cut.1
  25.8 32.8 %all_to_all.25.x_ref = bf16[128,16,128]{2,1,0:T(8,128)(2,1)S(1)} all-to-all(bf16[128,16,128]{2,1,0:T(8,128)(2,1)S(1)} %cut.1), channel_id=1, replica_groups=mesh['dp_0'=4,'dp_1'=8,'tensor_0'=4,'tensor_1'=2] {'dp_0','dp_1','tensor..., dimensions={0} | all-to-all | bytes 1048576 | tf_op jit(solution)/shard_map/all_to_all | solution.py:342
  58.7 0.1 sum_copies.2
  58.8 25.1 %all_to_all.26.own_ref = bf16[128,16,128]{2,1,0:T(8,128)(2,1)S(1)} all-to-all(bf16[128,16,128]{2,1,0:T(8,128)(2,1)S(1)} %sum_copies.2), channel_id=1, replica_groups=mesh['dp_0'=4,'dp_1'=8,'tensor_0'=4,'tensor_1'=2] {'dp_0','dp_1','tensor..., dimensions={0} | all-to-all | bytes 1048576 | tf_op jit(solution)/shard_map/all_to_all | solution.py:342
  83.8 0.0 collective-permute-start.1
  83.8 2.1 %collective-permute-done.1.other_ref = bf16[128,16,128]{2,1,0:T(8,128)(2,1)S(1)} collective-permute-done((bf16[128,16,128]{2,1,0:T(8,128)(2,1)S(1)}, bf16[128,16,128]{2,1,0:T(8,128)(2,1)S(1)}, u32[]{:S(2)}, u32[]{:S(2)}) %collective-permute-start.1) | collective-permute-done | bytes 524320 | tf_op jit(solution)/shard_map/ppermute | solution.py:357
  86.0 0.1 join.1.l_ref
  86.1 8.3 %all-gather.3.cloned.1.call-done = bf16[16,3072,128]{2,1,0:T(8,128)(2,1)} async-done(((bf16[2,3072,128]{2,1,0:T(8,128)(2,1)}), bf16[16,3072,128]{2,1,0:T(8,128)(2,1)}) %all-gather.3.cloned.1.call-update) | async-done | bytes 12582928 | tf_op jit(solution)/shard_map/all_gather | solution.py:348
  94.5 16.1 %moment.1.m_ref = f32[2,3072,384]{2,1,0:T(8,128)} custom-call(bf16[8,2,3072,128]{3,2,1,0:T(8,128)(2,1)} %bitcast.3, bf16[2,1024,384]{2,1,0:T(8,128)(2,1)} %x_ref.3, bf16[2,3072,384]{2,1,0:T(8,128)(2,1)} %e_ref.3), custom_call_target="tpu_custom_call" | custom-call | flops 5000000000 | bytes 28000000 | tf_op jit(solution)/shard_map/moment/pallas_call | solution.py:167
  110.6 7.4 %right_term.1 = bf16[32,16,128]{2,1,0:T(8,128)(2,1)} custom-call(bf16[2,64,3072]{2,1,0:T(8,128)(2,1)S(1)} %join.1.l_ref, f32[2,3072,384]{2,1,0:T(8,128)} %moment.1.m_ref), custom_call_target="tpu_custom_call" | custom-call | flops 400000000 | bytes 10000000 | tf_op jit(solution)/shard_map/right_term/pallas_call | solution.py:235
  118.0 10.1 %all-to-all-start.3 = ((bf16[32,16,128]{2,1,0:T(8,128)(2,1)}), bf16[32,16,128]{2,1,0:T(8,128)(2,1)S(1)}, u32[]{:S(2)}, u32[]{:S(2)}) async-start(bf16[32,16,128]{2,1,0:T(8,128)(2,1)} %right_term.1), calls=%async_computation.3 | async-start | bytes 262144 | tf_op jit(solution)/shard_map/all_to_all | solution.py:342
  128.2 9.5 %all-to-all-done.3.x_ref = bf16[32,16,128]{2,1,0:T(8,128)(2,1)S(1)} async-done(((bf16[32,16,128]{2,1,0:T(8,128)(2,1)}), bf16[32,16,128]{2,1,0:T(8,128)(2,1)S(1)}, u32[]{:S(2)}, u32[]{:S(2)}) %all-to-all-start.3) | async-done | bytes 131104 | tf_op jit(solution)/shard_map/all_to_all | solution.py:342
  137.7 0.7 sum_copies.3
  138.4 5.0 %all-to-all-start.4 = ((bf16[32,16,128]{2,1,0:T(8,128)(2,1)}), bf16[32,16,128]{2,1,0:T(8,128)(2,1)S(1)}, u32[]{:S(2)}, u32[]{:S(2)}) async-start(bf16[32,16,128]{2,1,0:T(8,128)(2,1)} %sum_copies.3), calls=%async_computation.4 | async-start | bytes 262144 | tf_op jit(solution)/shard_map/all_to_all | solution.py:342
  143.4 6.0 %gram_inverse.1.g_ref = f32[2,64,64]{2,1,0:T(8,128)S(1)} custom-call(bf16[2,64,3072]{2,1,0:T(8,128)(2,1)S(1)} %join.1.l_ref), custom_call_target="tpu_custom_call" | custom-call | flops 5000000000 | bytes 2000000 | tf_op jit(solution)/shard_map/gram_inverse/pallas_call | solution.py:276
  149.3 0.1 constant_dynamic-slice_fusion.own_ref
  149.4 3.3 %all-to-all-done.4.r_ref = bf16[32,16,128]{2,1,0:T(8,128)(2,1)S(1)} async-done(((bf16[32,16,128]{2,1,0:T(8,128)(2,1)}), bf16[32,16,128]{2,1,0:T(8,128)(2,1)S(1)}, u32[]{:S(2)}, u32[]{:S(2)}) %all-to-all-start.4) | async-done | bytes 131104 | tf_op jit(solution)/shard_map/all_to_all | solution.py:342
  152.7 10.0 %outputs.1 = (bf16[2,96,384]{2,1,0:T(8,128)(2,1)}, bf16[2,3072,384]{2,1,0:T(8,128)(2,1)}) custom-call(bf16[32,16,128]{2,1,0:T(8,128)(2,1)S(1)} %all-to-all-done.4.r_ref, f32[2,64,64]{2,1,0:T(8,128)S(1)} %gram_inverse.1.g_ref, bf16[2,64,3072]{2,1,0:T(8,128)(2,1)S(1)} %join.1.l_ref, bf16[2,64,96]{2,1,0:T(8,128)(2,1)S(1)} %constant_dynamic-slice_fusion.own_ref, ...), custom_call_target="tpu_custom_call" | custom-call | flops 600000000 | bytes 15000000 | tf_op jit(solution)/shard_map/outputs/pallas_call | solution.py:316
Async XLA Ops:
  7.2 2.8 %copy-start.4 = (f32[2,64,384]{2,1,0:T(8,128)S(1)}, f32[2,64,384]{2,1,0:T(8,128)}, u32[]{:S(2)}) copy-start(f32[2,64,384]{2,1,0:T(8,128)} %r_ref.3) | copy-start | bytes 589828
  7.2 2.8 %copy-start.2 = (bf16[2,1024,384]{2,1,0:T(8,128)(2,1)S(1)}, bf16[2,1024,384]{2,1,0:T(8,128)(2,1)}, u32[]{:S(2)}) copy-start(bf16[2,1024,384]{2,1,0:T(8,128)(2,1)} %x_ref.3) | copy-start | bytes 4718596
  7.2 87.3 %all-gather.3.cloned.1.call-start = ((), (), s32[]{:S(2)}) async-start(), calls=%async_computation.5 | async-start | bytes 14155776 | tf_op jit(solution)/shard_map/all_gather | solution.py:348
  10.0 13.3 %copy-start.1 = (bf16[2,128,3072]{2,1,0:T(8,128)(2,1)S(1)}, bf16[2,128,3072]{2,1,0:T(8,128)(2,1)}, u32[]{:S(2)}) copy-start(bf16[2,128,3072]{2,1,0:T(8,128)(2,1)} %y_ref.1) | copy-start | bytes 4718596
  10.6 0.7 copy-start.3
  11.3 12.0 %all-to-all-start = ((bf16[8,2,64,128]{3,2,1,0:T(8,128)(2,1)}), bf16[8,2,64,128]{3,2,1,0:T(8,128)(2,1)S(1)}, u32[]{:S(2)}, u32[]{:S(2)}) async-start(bf16[8,2,64,128]{3,2,1,0:T(8,128)(2,1)} %copy-done.3), calls=%async_computation | async-start | bytes 524288 | tf_op jit(solution)/shard_map/all_to_all | solution.py:342
  15.8 2.3 %copy-start = (bf16[2,3072,384]{2,1,0:T(8,128)(2,1)S(1)}, bf16[2,3072,384]{2,1,0:T(8,128)(2,1)}, u32[]{:S(2)}) copy-start(bf16[2,3072,384]{2,1,0:T(8,128)(2,1)} %e_ref.3) | copy-start | bytes 14155780
  18.2 0.9 copy-start.5
  23.9 1.8 %collective-permute-start = (bf16[64,3072]{1,0:T(8,128)(2,1)S(1)}, bf16[64,3072]{1,0:T(8,128)(2,1)S(1)}, u32[]{:S(2)}, u32[]{:S(2)}) collective-permute-start(bf16[64,3072]{1,0:T(8,128)(2,1)S(1)} %get-tuple-element.5), channel_id=1, source_target_pairs={{0,1},{1,0},{2,3},{3,2},{4,5},{5,4},{6,7},{7,6},{8,9},{9,8},{10,11... | collective-permute-start | bytes 1179656 | tf_op jit(solution)/shard_map/ppermute | solution.py:354
  83.8 2.1 %collective-permute-start.1 = (bf16[128,16,128]{2,1,0:T(8,128)(2,1)S(1)}, bf16[128,16,128]{2,1,0:T(8,128)(2,1)S(1)}, u32[]{:S(2)}, u32[]{:S(2)}) collective-permute-start(bf16[128,16,128]{2,1,0:T(8,128)(2,1)S(1)} %all_to_all.26.own_ref), channel_id=1, source_target_pairs={{0,1},{1,0},{2,3},{3,2},{4,5},{5,4},{6,7},{7,6},{8,9},{9,8},{10,11... | collective-permute-start | bytes 1572872 | tf_op jit(solution)/shard_map/ppermute | solution.py:357
  118.0 19.7 %all-to-all-start.3 = ((bf16[32,16,128]{2,1,0:T(8,128)(2,1)}), bf16[32,16,128]{2,1,0:T(8,128)(2,1)S(1)}, u32[]{:S(2)}, u32[]{:S(2)}) async-start(bf16[32,16,128]{2,1,0:T(8,128)(2,1)} %right_term.1), calls=%async_computation.3 | async-start | bytes 262144 | tf_op jit(solution)/shard_map/all_to_all | solution.py:342
  138.4 14.3 %all-to-all-start.4 = ((bf16[32,16,128]{2,1,0:T(8,128)(2,1)}), bf16[32,16,128]{2,1,0:T(8,128)(2,1)S(1)}, u32[]{:S(2)}, u32[]{:S(2)}) async-start(bf16[32,16,128]{2,1,0:T(8,128)(2,1)} %sum_copies.3), calls=%async_computation.4 | async-start | bytes 262144 | tf_op jit(solution)/shard_map/all_to_all | solution.py:342
Sparse Core Ops, SparseCore 0:
  10.4 84.0 all-gather.2

commit v2 on v1

v2 whole, which is shorter than its diff:
```python
import functools

import jax
import jax.numpy as jnp
from jax import lax
from jax.experimental import pallas as pl
from jax.experimental.pallas import tpu as pltpu
from jax.sharding import Mesh
from jax.sharding import PartitionSpec as P


TENSOR = ("tensor_0", "tensor_1")
DP_TENSOR = ("dp_0", "dp_1", "tensor_0", "tensor_1")
DP = ("dp_0", "dp_1")
WIDE = ("dp_0", "dp_1", "tensor_0")
F32, BF16 = jnp.float32, jnp.bfloat16
HIGHEST = lax.Precision.HIGHEST
VMEM = pl.BlockSpec(memory_space=pltpu.VMEM)
SMEM = pl.BlockSpec(memory_space=pltpu.SMEM)


def room(mib):
    return pltpu.CompilerParams(vmem_limit_bytes=mib * 1024 * 1024)


def cost(flops, nbytes):
    return pl.CostEstimate(flops=int(flops), bytes_accessed=int(nbytes), transcendentals=0)


def two_parts(x):
    high = x.astype(BF16)
    return high, (x - high.astype(F32)).astype(BF16)


def dot(a, b, dims, **kw):
    return lax.dot_general(a, b, (dims, ((), ())), preferred_element_type=F32, **kw)


def sketch_kernel(r_ref, x_ref, o_ref):
    rank = r_ref.shape[1]
    for layer in range(r_ref.shape[0]):
        stacked = jnp.concatenate(two_parts(r_ref[layer]), axis=0)
        z = dot(stacked, x_ref[layer], ((1,), (1,)))
        z = (z[:rank] + z[rank:]).astype(BF16)
        for j in range(o_ref.shape[0]):
            o_ref[j, layer] = z[:, j * 128 : (j + 1) * 128]


def sketch(right_init, context):
    layers, rank, _ = right_init.shape
    tokens = context.shape[1]
    return pl.pallas_call(
        sketch_kernel,
        out_shape=jax.ShapeDtypeStruct((tokens // 128, layers, rank, 128), BF16),
        in_specs=[VMEM, VMEM],
        out_specs=VMEM,
        cost_estimate=cost(4e8, 2e6),
        name="sketch",
        compiler_params=room(56),
    )(right_init, context)


def error_sketch_kernel(r_ref, e_ref, o_ref):
    rank = r_ref.shape[1]
    stacked = jnp.concatenate(two_parts(r_ref[0]), axis=0)
    z = dot(stacked, e_ref[0], ((1,), (1,)))
    o_ref[0] = z[:rank] + z[rank:]


def error_sketch(right_init, error_in):
    layers, rank, width = right_init.shape
    rows = error_in.shape[1]
    step = 768
    return pl.pallas_call(
        error_sketch_kernel,
        out_shape=jax.ShapeDtypeStruct((layers, rank, rows), F32),
        grid=(layers, rows // step),
        in_specs=[
            pl.BlockSpec((1, rank, width), lambda l, d: (l, 0, 0)),
            pl.BlockSpec((1, step, width), lambda l, d: (l, d, 0)),
        ],
        out_specs=pl.BlockSpec((1, rank, step), lambda l, d: (l, 0, d)),
        cost_estimate=cost(6e8, 7e6),
        name="error_sketch",
        compiler_params=room(6),
    )(right_init, error_in)


def left_term_kernel(core_ref, z_ref, y_ref, e_ref, send_ref, keep_ref):
    rank = z_ref.shape[2]
    core = core_ref[0]
    for which, out in ((1 - core, send_ref), (core, keep_ref)):
        z = z_ref[0, which].astype(F32)
        for j in range(1, z_ref.shape[0]):
            z = z + z_ref[j, which].astype(F32)
        t = dot(jnp.concatenate(two_parts(z), axis=0), y_ref[which], ((1,), (0,)))
        out[...] = t[:rank] + t[rank:] + e_ref[which]


def left_term(core, z, own_grad, error_part):
    rank, rows = error_part.shape[1:]
    shape = jax.ShapeDtypeStruct((rank, rows), F32)
    return pl.pallas_call(
        left_term_kernel,
        out_shape=(shape, shape),
        in_specs=[SMEM, VMEM, VMEM, VMEM],
        out_specs=(VMEM, VMEM),
        cost_estimate=cost(2e8, 5e6),
        name="left_term",
        compiler_params=room(12),
    )(core, z, own_grad, error_part)


def cut_kernel(a_ref, b_ref, o_ref):
    bands, lanes = a_ref.shape[0] // 16, a_ref.shape[1] // 128
    for i in range(bands):
        for j in range(lanes):
            rows, cols = slice(i * 16, i * 16 + 16), slice(j * 128, j * 128 + 128)
            both = a_ref[rows, cols] + b_ref[rows, cols]
            o_ref[i * lanes + j] = both.astype(BF16)
    for p in range(bands * lanes, o_ref.shape[0]):
        o_ref[p] = jnp.zeros(o_ref.shape[1:], BF16)


def cut(a, b, pieces):
    return pl.pallas_call(
        cut_kernel,
        out_shape=jax.ShapeDtypeStruct((pieces, 16, 128), BF16),
        in_specs=[VMEM, VMEM],
        out_specs=VMEM,
        cost_estimate=cost(4e5, 1.2e6),
        name="cut",
        compiler_params=room(4),
    )(a, b)


def sum_copies_kernel(x_ref, o_ref):
    parts = [x_ref[p].astype(F32) for p in range(4)]
    for p in range(4, x_ref.shape[0], 4):
        for q in range(4):
            parts[q] = parts[q] + x_ref[p + q].astype(F32)
    total = ((parts[0] + parts[1]) + (parts[2] + parts[3])).astype(o_ref.dtype)
    for p in range(o_ref.shape[0]):
        o_ref[p] = total


def sum_copies(x, dtype):
    return pl.pallas_call(
        sum_copies_kernel,
        out_shape=jax.ShapeDtypeStruct(x.shape, dtype),
        in_specs=[VMEM],
        out_specs=VMEM,
        cost_estimate=cost(x.size, x.size * 4),
        name="sum_copies",
        compiler_params=room(4),
    )(x)


def own_tokens_kernel(core_ref, a_ref, b_ref, y_ref, l_ref, o_ref):
    core = core_ref[0]
    count, lanes = l_ref.shape[1] // 16, l_ref.shape[2] // 128
    for which, ref in ((core, a_ref), (1 - core, b_ref)):
        rows = [jnp.concatenate([ref[i * lanes + j] for j in range(lanes)], axis=1) for i in range(count)]
        left = jnp.concatenate(rows, axis=0)
        l_ref[which] = left
        w = dot(left, y_ref[which], ((1,), (1,))).astype(BF16)
        for k in range(o_ref.shape[0]):
            o_ref[k, which] = w


def own_tokens(core, own, other, own_grad, rank, count):
    rows = own_grad.shape[2]
    return pl.pallas_call(
        own_tokens_kernel,
        out_shape=(
            jax.ShapeDtypeStruct((2, rank, rows), BF16),
            jax.ShapeDtypeStruct((count, 2, rank, 128), BF16),
        ),
        in_specs=[SMEM, VMEM, VMEM, VMEM],
        out_specs=(VMEM, VMEM),
        cost_estimate=cost(2e8, 4e6),
        name="own_tokens",
        compiler_params=room(6),
    )(core, own, other, own_grad)


def left_error_kernel(l_ref, e_ref, o_ref):
    for layer in range(l_ref.shape[0]):
        o_ref[layer] = dot(l_ref[layer], e_ref[layer], ((1,), (0,)))


def left_error(left, error_in):
    layers, rank, _ = left.shape
    return pl.pallas_call(
        left_error_kernel,
        out_shape=jax.ShapeDtypeStruct((layers, rank, error_in.shape[2]), F32),
        in_specs=[VMEM, VMEM],
        out_specs=VMEM,
        cost_estimate=cost(6e8, 6e6),
        name="left_error",
        compiler_params=room(10),
    )(left, error_in)


def right_term_kernel(w_ref, x_ref, e_ref, o_ref):
    layers, rank, width = e_ref.shape
    count, lanes = rank // 16, width // 128
    for layer in range(layers):
        w = jnp.concatenate([w_ref[k, layer] for k in range(w_ref.shape[0])], axis=1)
        right = dot(w, x_ref[layer], ((1,), (0,))) + e_ref[layer]
        for i in range(count):
            for j in range(lanes):
                o_ref[(layer * count + i) * lanes + j] = right[i * 16 : i * 16 + 16, j * 128 : j * 128 + 128]
    for p in range(layers * count * lanes, o_ref.shape[0]):
        o_ref[p] = jnp.zeros(o_ref.shape[1:], o_ref.dtype)


def right_term(w, context, error_part, pieces):
    return pl.pallas_call(
        right_term_kernel,
        out_shape=jax.ShapeDtypeStruct((pieces, 16, 128), F32),
        in_specs=[VMEM, VMEM, VMEM],
        out_specs=VMEM,
        cost_estimate=cost(2e8, 3e6),
        name="right_term",
        compiler_params=room(6),
    )(w, context, error_part)


def turn_kernel(y_ref, *o_refs):
    for layer, o_ref in enumerate(o_refs):
        o_ref[...] = y_ref[layer].T


def turn(own_grad):
    layers, tokens, rows = own_grad.shape
    return pl.pallas_call(
        turn_kernel,
        out_shape=[jax.ShapeDtypeStruct((rows, tokens), BF16)] * layers,
        in_specs=[VMEM],
        out_specs=[VMEM] * layers,
        cost_estimate=cost(1e8, 3e6),
        name="turn",
        compiler_params=room(8),
    )(own_grad)


def moment_kernel(y_ref, x_ref, e_ref, o_ref):
    y = jnp.concatenate([y_ref[k] for k in range(y_ref.shape[0])], axis=1)
    o_ref[...] = dot(y, x_ref[0], ((1,), (0,))) + e_ref[0].astype(F32)


def moment_of(grad_t, context, error_in, layer):
    blocks, rows, _ = grad_t.shape
    tokens, width = context.shape[1:]
    step = 512
    return pl.pallas_call(
        moment_kernel,
        out_shape=jax.ShapeDtypeStruct((rows, width), F32),
        grid=(rows // step,),
        in_specs=[
            pl.BlockSpec((blocks, step, 128), lambda d: (0, d, 0)),
            pl.BlockSpec((1, tokens, width), lambda d: (layer, 0, 0)),
            pl.BlockSpec((1, step, width), lambda d: (layer, d, 0)),
        ],
        out_specs=pl.BlockSpec((step, width), lambda d: (d, 0)),
        cost_estimate=cost(4e9, 14e6),
        compiler_params=room(56),
    )(grad_t, context, error_in)


def inverse_kernel(l_ref, o_ref, t_ref):
    rank = l_ref.shape[1]
    row = lax.broadcasted_iota(jnp.int32, (rank, 2 * rank), 0)
    col = lax.broadcasted_iota(jnp.int32, (rank, 2 * rank), 1)
    work = []
    for layer in range(l_ref.shape[0]):
        left = l_ref[layer]
        turned = left.T
        t_ref[layer] = jnp.concatenate([turned, turned], axis=1)
        gram = dot(left, left, ((1,), (1,)))
        wide = jnp.concatenate([gram, jnp.zeros((rank, rank), F32)], axis=1)
        diag = jnp.sum(jnp.where(row == col, wide, 0.0), axis=1, keepdims=True)
        ridge = 1e-6 * (jnp.sum(diag, axis=0, keepdims=True) / rank)
        wide = wide + jnp.where(row == col, ridge, 0.0)
        work.append(jnp.where(col == row + rank, 1.0, wide))
    for k in range(rank):
        for layer in range(len(work)):
            a = work[layer]
            pivot_row = a[k : k + 1, :] / a[k : k + 1, k : k + 1]
            column = a[:, k : k + 1]
            work[layer] = jnp.where(row == k, pivot_row, a - column * pivot_row)
    for layer in range(len(work)):
        o_ref[layer] = work[layer][:, rank:]


def inverse_of_gram(left):
    layers, rank, rows = left.shape
    return pl.pallas_call(
        inverse_kernel,
        out_shape=(
            jax.ShapeDtypeStruct((layers, rank, rank), F32),
            jax.ShapeDtypeStruct((layers, rows, 2 * rank), BF16),
        ),
        in_specs=[VMEM],
        out_specs=(VMEM, VMEM),
        cost_estimate=cost(5e9, 2e6),
        name="gram_inverse",
        compiler_params=room(6),
    )(left)


def outputs_kernel(r_ref, g_ref, t_ref, own_ref, m0_ref, m1_ref, s_ref, e_ref, q_ref, *, replicas):
    layer, d = pl.program_id(0), pl.program_id(1)
    rank, width = g_ref.shape[1], m0_ref.shape[1]
    count, lanes = rank // 16, width // 128

    @pl.when(d == 0)
    def _():
        rows = [
            jnp.concatenate([r_ref[(layer * count + i) * lanes + j] for j in range(lanes)], axis=1)
            for i in range(count)
        ]
        q = dot(g_ref[0], jnp.concatenate(rows, axis=0), ((1,), (0,)), precision=HIGHEST)
        own = own_ref[0]
        s = dot(jnp.concatenate([own, own], axis=0), jnp.concatenate(two_parts(q), axis=0), ((0,), (0,)))
        s_ref[0] = s.astype(BF16)
        q_ref[...] = jnp.concatenate(two_parts(q * (-1.0 / replicas)), axis=0)

    update = dot(t_ref[0], q_ref[...], ((1,), (0,)))
    for which, m_ref in ((0, m0_ref), (1, m1_ref)):

        @pl.when(layer == which)
        def _():
            e_ref[0] = (m_ref[...] + update).astype(BF16)


def outputs(right, inverse, turned, own_left, moments, replicas):
    rows, width = moments[0].shape
    layers, rank, share = own_left.shape
    step = 768
    last = rows // step - 1
    return pl.pallas_call(
        functools.partial(outputs_kernel, replicas=replicas),
        out_shape=(
            jax.ShapeDtypeStruct((layers, share, width), BF16),
            jax.ShapeDtypeStruct((layers, rows, width), BF16),
        ),
        grid=(layers, rows // step),
        in_specs=[
            pl.BlockSpec(right.shape, lambda l, d: (0, 0, 0)),
            pl.BlockSpec((1, rank, rank), lambda l, d: (l, 0, 0)),
            pl.BlockSpec((1, step, 2 * rank), lambda l, d: (l, d, 0)),
            pl.BlockSpec((1, rank, share), lambda l, d: (l, 0, 0)),
            pl.BlockSpec((step, width), lambda l, d: (d * (1 - l) + last * l, 0)),
            pl.BlockSpec((step, width), lambda l, d: (d * l, 0)),
        ],
        out_specs=(
            pl.BlockSpec((1, share, width), lambda l, d: (l, 0, 0)),
            pl.BlockSpec((1, step, width), lambda l, d: (l, d, 0)),
        ),
        scratch_shapes=[pltpu.VMEM((2 * rank, width), BF16)],
        cost_estimate=cost(6e8, 15e6),
        name="outputs",
        compiler_params=room(50),
    )(right, inverse, turned, own_left, *moments)


def exchanged(x, axis):
    return lax.all_to_all(x, axis, 0, 0, tiled=True)


SWAP = [(0, 1), (1, 0)]


def swapped(x):
    return lax.ppermute(x, "tensor_1", SWAP)


def body(context, out_grad, error_in, right_init):
    rank, rows = right_init.shape[1], out_grad.shape[2]
    replicas = lax.axis_size(DP)
    core = lax.axis_index("tensor_1").astype(jnp.int32).reshape(1)
    z = exchanged(sketch(right_init, context), TENSOR)
    grads = []
    for turned in turn(out_grad):
        grads.append(lax.all_gather(turned, TENSOR, axis=0, tiled=False))
    error_part = error_sketch(right_init, error_in)
    send, keep = left_term(core, z, out_grad, error_part)
    arrived = swapped(send)
    terms = exchanged(cut(keep, arrived, lax.axis_size(WIDE)), WIDE)
    own = exchanged(sum_copies(terms, BF16), WIDE)
    other = swapped(own)
    left, w = own_tokens(core, own, other, out_grad, rank, lax.axis_size(TENSOR))
    w = exchanged(w, TENSOR)
    right = right_term(w, context, left_error(left, error_in), replicas)
    right = exchanged(right, DP)
    right = exchanged(sum_copies(right, F32), DP)
    inverse, turned = inverse_of_gram(left)
    moments = []
    for layer, grad_t in enumerate(grads):
        moments.append(moment_of(grad_t, context, error_in, layer))
    share = rows // replicas
    own_left = lax.dynamic_slice_in_dim(left, lax.axis_index(DP) * share, share, 2)
    return outputs(right, inverse, turned, own_left, moments, replicas)


def solution(mesh):
    finer = Mesh(mesh.devices.reshape(4, 8, 4, 2), ("dp_0", "dp_1", "tensor_0", "tensor_1"))
    return jax.shard_map(
        body,
        mesh=finer,
        in_specs=(
            P(None, DP, TENSOR),
            P(None, DP_TENSOR, None),
            P(None, DP, TENSOR),
            P(None, None, TENSOR),
        ),
        out_specs=(P(None, DP, TENSOR), P(None, DP, TENSOR)),
        check_vma=False,
    )
```

time: 171 us -> 166 us (0.971)
  waiting for transfers between devices: 26.6 us -> 17.5 us
  local copies, waits for them, and re-layouts: 6.78 us -> 9.23 us
  Pallas kernels: 44.4 us -> 46.2 us
    all_gather x1 -> x2, waiting for transfers between devices: 8.34 us -> 0.02 us  [body(): grads.append(lax.all_gather(turned, TENSOR, axis=0, tiled=False))]
    pallas_call x1, Pallas kernels: 7.4 us -> 1.06 us  [right_term(): pl.pallas_call(right_term_kernel, out_shape=jax.ShapeDtypeStruct((pieces,...]
    pallas_call x3 -> x6, Pallas kernels: 22.2 us -> 28.1 us  [the longest x2 17.5 us: moment_of(): pl.pallas_call(moment_kernel, out_shape=jax.ShapeDtypeStruct((rows, width...]
    unnamed x13 -> x18, local copies, waits for them, and re-layouts: 6.69 us -> 9.13 us
    pallas_call x1, Pallas kernels: 0.62 us -> 2.96 us  [sketch(): pl.pallas_call(sketch_kernel, out_shape=jax.ShapeDtypeStruct((tokens // 1...]
    all_to_all x3 -> x4, waiting for transfers between devices: 14.3 us -> 12 us  [exchanged(): return lax.all_to_all(x, axis, 0, 0, tiled=True)]
    all_to_all x3 -> x4, starting transfers between devices: 19.6 us -> 19.4 us  [exchanged(): return lax.all_to_all(x, axis, 0, 0, tiled=True)]
  transfers between devices with their start and end apart: 6 -> 8, of which waited for: 6 -> 5; matrix products, arithmetic and copies ran while one was open for 0% -> 0% of each run, Pallas kernels for 6% -> 21%
where the time goes in v2:
time: 166 us; the launch traced here: 165 us
  blocking collectives  57.9 us (35%)
  Pallas kernels  46.2 us (28%)
  starting transfers between devices  19.6 us (12%)
  waiting for transfers between devices  17.5 us (11%)
  between operations  14.2 us (9%)
  local copies, waits for them, and re-layouts  9.23 us (6%)
    all_to_all x2, blocking collectives, exchanged(): return lax.all_to_all(x, axis, 0, 0, tiled=True)  57.9 us
    all_to_all x4, starting transfers between devices, exchanged(): return lax.all_to_all(x, axis, 0, 0, tiled=True)  19.4 us
    pallas_call x2, Pallas kernels, moment_of(): pl.pallas_call(moment_kernel, out_shape=jax.ShapeDtypeStruct((rows, width...  17.5 us
    all_to_all x4, waiting for transfers between devices, exchanged(): return lax.all_to_all(x, axis, 0, 0, tiled=True)  12 us
    pallas_call x1, Pallas kernels, outputs(): pl.pallas_call(functools.partial(outputs_kernel, replicas=replicas), out_...  9.9 us
    unnamed x18, local copies, waits for them, and re-layouts  9.13 us
    pallas_call x1, Pallas kernels, inverse_of_gram(): pl.pallas_call(inverse_kernel, out_shape=(jax.ShapeDtypeStruct((layers, r...  6.85 us
    ppermute x2, waiting for transfers between devices, swapped(): return lax.ppermute(x, 'tensor_1', SWAP)  4.74 us
  transfers between devices with their start and end apart: 8, of which 5 were waited for; matrix products, arithmetic and copies ran while one was open for 0% of the time, Pallas kernels for 21%

profile of v2, /device:TPU:2, one launch (start us, length us, event | category | flops | bytes accessed | tf_op | source)
XLA Modules:
  0.0 164.6 jit_solution(7902459551577344006)
XLA Ops:
  7.2 0.0 all-gather.5.cloned.1.call-start
  7.2 0.0 copy-start.3
  7.2 1.4 copy-done.3
  8.6 1.4 turn.1
  10.1 0.0 all-gather.5.cloned.1.call-update
  10.1 0.0 all-gather.7.cloned.1.call-start
  10.1 0.7 all-gather.7.cloned.1.call-update
  10.8 0.0 copy-start.4
  10.9 3.0 %sketch.1 = bf16[8,2,64,128]{3,2,1,0:T(8,128)(2,1)} custom-call(f32[2,64,384]{2,1,0:T(8,128)} %r_ref.3, bf16[2,1024,384]{2,1,0:T(8,128)(2,1)} %x_ref.7), custom_call_target="tpu_custom_call" | custom-call | flops 400000000 | bytes 2000000 | tf_op jit(solution)/shard_map/sketch/pallas_call | solution.py:52
  13.8 4.5 %all-to-all-start = ((bf16[8,2,64,128]{3,2,1,0:T(8,128)(2,1)}), bf16[8,2,64,128]{3,2,1,0:T(8,128)(2,1)S(1)}, u32[]{:S(2)}, u32[]{:S(2)}) async-start(bf16[8,2,64,128]{3,2,1,0:T(8,128)(2,1)} %sketch.1), calls=%async_computation | async-start | bytes 524288 | tf_op jit(solution)/shard_map/all_to_all | solution.py:370
  18.3 0.0 copy-start
  18.3 2.3 %copy-done = bf16[2,3072,384]{2,1,0:T(8,128)(2,1)S(1)} copy-done((bf16[2,3072,384]{2,1,0:T(8,128)(2,1)S(1)}, bf16[2,3072,384]{2,1,0:T(8,128)(2,1)}, u32[]{:S(2)}) %copy-start) | copy-done | bytes 4718616
  20.6 0.0 copy-start.8
  20.6 0.9 copy-done.8
  21.5 2.7 %error_sketch.1.e_ref = f32[2,64,3072]{2,1,0:T(8,128)S(1)} custom-call(f32[2,64,384]{2,1,0:T(8,128)S(1)} %copy-done.8, bf16[2,3072,384]{2,1,0:T(8,128)(2,1)S(1)} %copy-done), custom_call_target="tpu_custom_call" | custom-call | flops 600000000 | bytes 7000000 | tf_op jit(solution)/shard_map/error_sketch/pallas_call | solution.py:74
  24.2 1.5 all-to-all-done.z_ref
  25.8 0.0 copy-done.4
  25.8 0.6 left_term.1
  26.3 0.1 collective-permute-start
  26.4 2.8 %collective-permute-done.b_ref = f32[64,3072]{1,0:T(8,128)S(1)} collective-permute-done((f32[64,3072]{1,0:T(8,128)S(1)}, f32[64,3072]{1,0:T(8,128)S(1)}, u32[]{:S(2)}, u32[]{:S(2)}) %collective-permute-start) | collective-permute-done | bytes 786464 | tf_op jit(solution)/shard_map/ppermute | solution.py:377
  29.3 0.1 cut.1
  29.4 32.5 %all_to_all.30.x_ref = bf16[128,16,128]{2,1,0:T(8,128)(2,1)S(1)} all-to-all(bf16[128,16,128]{2,1,0:T(8,128)(2,1)S(1)} %cut.1), channel_id=1, replica_groups=mesh['dp_0'=4,'dp_1'=8,'tensor_0'=4,'tensor_1'=2] {'dp_0','dp_1','tensor..., dimensions={0} | all-to-all | bytes 1048576 | tf_op jit(solution)/shard_map/all_to_all | solution.py:370
  61.9 0.1 sum_copies.2
  62.0 0.0 copy-start.2
  62.0 25.4 %all_to_all.31.a_ref = bf16[128,16,128]{2,1,0:T(8,128)(2,1)S(1)} all-to-all(bf16[128,16,128]{2,1,0:T(8,128)(2,1)S(1)} %sum_copies.2), channel_id=1, replica_groups=mesh['dp_0'=4,'dp_1'=8,'tensor_0'=4,'tensor_1'=2] {'dp_0','dp_1','tensor..., dimensions={0} | all-to-all | bytes 1048576 | tf_op jit(solution)/shard_map/all_to_all | solution.py:370
  87.4 0.0 collective-permute-start.1
  87.4 1.9 %collective-permute-done.1.b_ref = bf16[128,16,128]{2,1,0:T(8,128)(2,1)S(1)} collective-permute-done((bf16[128,16,128]{2,1,0:T(8,128)(2,1)S(1)}, bf16[128,16,128]{2,1,0:T(8,128)(2,1)S(1)}, u32[]{:S(2)}, u32[]{:S(2)}) %collective-permute-start.1) | collective-permute-done | bytes 524320 | tf_op jit(solution)/shard_map/ppermute | solution.py:377
  89.3 1.4 own_tokens.1
  90.7 0.0 copy-start.5
  90.7 0.9 copy-done.5
  91.5 3.4 %all-to-all-start.3 = ((bf16[8,2,64,128]{3,2,1,0:T(8,128)(2,1)}), bf16[8,2,64,128]{3,2,1,0:T(8,128)(2,1)S(1)}, u32[]{:S(2)}, u32[]{:S(2)}) async-start(bf16[8,2,64,128]{3,2,1,0:T(8,128)(2,1)} %get-tuple-element.12), calls=%async_computation.3 | async-start | bytes 524288 | tf_op jit(solution)/shard_map/all_to_all | solution.py:370
  95.0 0.0 copy-start.1
  95.0 2.4 %copy-done.1 = bf16[2,3072,384]{2,1,0:T(8,128)(2,1)S(1)} copy-done((bf16[2,3072,384]{2,1,0:T(8,128)(2,1)S(1)}, bf16[2,3072,384]{2,1,0:T(8,128)(2,1)}, u32[]{:S(2)}) %copy-start.1) | copy-done | bytes 4718616
  97.4 0.0 copy-start.6
  97.4 1.1 copy-done.6
  98.5 0.0 copy-start.7
  98.5 0.9 left_error.1.e_ref
  99.4 6.2 %all-to-all-done.3.w_ref = bf16[8,2,64,128]{3,2,1,0:T(8,128)(2,1)S(1)} async-done(((bf16[8,2,64,128]{3,2,1,0:T(8,128)(2,1)}), bf16[8,2,64,128]{3,2,1,0:T(8,128)(2,1)S(1)}, u32[]{:S(2)}, u32[]{:S(2)}) %all-to-all-start.3) | async-done | bytes 262176 | tf_op jit(solution)/shard_map/all_to_all | solution.py:370
  105.6 0.0 copy-done.2
  105.6 1.1 right_term.1
  106.7 6.0 %all-to-all-start.4 = ((f32[32,16,128]{2,1,0:T(8,128)}), f32[32,16,128]{2,1,0:T(8,128)S(1)}, u32[]{:S(2)}, u32[]{:S(2)}) async-start(f32[32,16,128]{2,1,0:T(8,128)} %right_term.1), calls=%async_computation.4 | async-start | bytes 524288 | tf_op jit(solution)/shard_map/all_to_all | solution.py:370
  112.7 0.0 copy-done.7
  112.7 0.1 constant_dynamic-slice_fusion.own_ref
  112.8 6.9 %gram_inverse.1 = (f32[2,64,64]{2,1,0:T(8,128)S(1)}, bf16[2,3072,128]{2,1,0:T(8,128)(2,1)S(1)}) custom-call(bf16[2,64,3072]{2,1,0:T(8,128)(2,1)S(1)} %copy-done.7), custom_call_target="tpu_custom_call" | custom-call | flops 5000000000 | bytes 2000000 | tf_op jit(solution)/shard_map/gram_inverse/pallas_call | solution.py:299
  119.6 4.3 %all-to-all-done.4.x_ref = f32[32,16,128]{2,1,0:T(8,128)S(1)} async-done(((f32[32,16,128]{2,1,0:T(8,128)}), f32[32,16,128]{2,1,0:T(8,128)S(1)}, u32[]{:S(2)}, u32[]{:S(2)}) %all-to-all-start.4) | async-done | bytes 262176 | tf_op jit(solution)/shard_map/all_to_all | solution.py:370
  123.9 0.7 sum_copies.3
  124.7 5.6 %all-to-all-start.5 = ((f32[32,16,128]{2,1,0:T(8,128)}), f32[32,16,128]{2,1,0:T(8,128)S(1)}, u32[]{:S(2)}, u32[]{:S(2)}) async-start(f32[32,16,128]{2,1,0:T(8,128)} %sum_copies.3), calls=%async_computation.5 | async-start | bytes 524288 | tf_op jit(solution)/shard_map/all_to_all | solution.py:370
  130.3 0.0 all-gather.5.cloned.1.call-done
  130.3 8.8 %shard_map.59.m0_ref = f32[3072,384]{1,0:T(8,128)} custom-call(bf16[8,3072,128]{2,1,0:T(8,128)(2,1)} %bitcast.3, bf16[2,1024,384]{2,1,0:T(8,128)(2,1)} %x_ref.7, bf16[2,3072,384]{2,1,0:T(8,128)(2,1)} %e_ref.7), custom_call_target="tpu_custom_call" | custom-call | flops 4000000000 | bytes 14000000 | tf_op jit(solution)/shard_map/pallas_call | solution.py:257
  139.1 0.0 all-gather.7.cloned.1.call-done
  139.1 8.8 %shard_map.60.m1_ref = f32[3072,384]{1,0:T(8,128)} custom-call(bf16[8,3072,128]{2,1,0:T(8,128)(2,1)} %bitcast.4, bf16[2,1024,384]{2,1,0:T(8,128)(2,1)} %x_ref.7, bf16[2,3072,384]{2,1,0:T(8,128)(2,1)} %e_ref.7), custom_call_target="tpu_custom_call" | custom-call | flops 4000000000 | bytes 14000000 | tf_op jit(solution)/shard_map/pallas_call | solution.py:257
  147.8 0.0 all-to-all-done.5.r_ref
  147.8 9.9 %outputs.1 = (bf16[2,96,384]{2,1,0:T(8,128)(2,1)}, bf16[2,3072,384]{2,1,0:T(8,128)(2,1)}) custom-call(f32[32,16,128]{2,1,0:T(8,128)S(1)} %all-to-all-done.5.r_ref, f32[2,64,64]{2,1,0:T(8,128)S(1)} %get-tuple-element.14.g_ref, bf16[2,3072,128]{2,1,0:T(8,128)(2,1)S(1)} %get-tuple-element.15.t_ref, bf16[2,64,96]{2,1,0:T(8,128)(2,1)S(1)} %constant_dynamic-slice_fusion.own_ref, ...), custom_call_target="tpu_custom_call" | custom-call | flops 600000000 | bytes 15000000 | tf_op jit(solution)/shard_map/outputs/pallas_call | solution.py:343
Async XLA Ops:
  7.2 123.1 %all-gather.5.cloned.1.call-start = ((), (), s32[]{:S(2)}) async-start(), calls=%async_computation.6 | async-start | bytes 7077888 | tf_op jit(solution)/shard_map/all_gather | solution.py:387
  7.2 1.4 copy-start.3
  10.1 129.0 %all-gather.7.cloned.1.call-start = ((), (), s32[]{:S(2)}) async-start(), calls=%async_computation.7 | async-start | bytes 7077888 | tf_op jit(solution)/shard_map/all_gather | solution.py:387
  10.8 14.9 %copy-start.4 = (bf16[2,128,3072]{2,1,0:T(8,128)(2,1)S(1)}, bf16[2,128,3072]{2,1,0:T(8,128)(2,1)}, u32[]{:S(2)}) copy-start(bf16[2,128,3072]{2,1,0:T(8,128)(2,1)} %y_ref.5) | copy-start | bytes 4718596
  13.8 12.0 %all-to-all-start = ((bf16[8,2,64,128]{3,2,1,0:T(8,128)(2,1)}), bf16[8,2,64,128]{3,2,1,0:T(8,128)(2,1)S(1)}, u32[]{:S(2)}, u32[]{:S(2)}) async-start(bf16[8,2,64,128]{3,2,1,0:T(8,128)(2,1)} %sketch.1), calls=%async_computation | async-start | bytes 524288 | tf_op jit(solution)/shard_map/all_to_all | solution.py:370
  18.3 2.3 %copy-start = (bf16[2,3072,384]{2,1,0:T(8,128)(2,1)S(1)}, bf16[2,3072,384]{2,1,0:T(8,128)(2,1)}, u32[]{:S(2)}) copy-start(bf16[2,3072,384]{2,1,0:T(8,128)(2,1)} %e_ref.7) | copy-start | bytes 14155780
  20.6 0.9 copy-start.8
  26.3 2.9 %collective-permute-start = (f32[64,3072]{1,0:T(8,128)S(1)}, f32[64,3072]{1,0:T(8,128)S(1)}, u32[]{:S(2)}, u32[]{:S(2)}) collective-permute-start(f32[64,3072]{1,0:T(8,128)S(1)} %get-tuple-element.11), channel_id=1, source_target_pairs={{0,1},{1,0},{2,3},{3,2},{4,5},{5,4},{6,7},{7,6},{8,9},{9,8},{10,11... | collective-permute-start | bytes 2359304 | tf_op jit(solution)/shard_map/ppermute | solution.py:377
  62.0 43.6 %copy-start.2 = (bf16[2,1024,384]{2,1,0:T(8,128)(2,1)S(1)}, bf16[2,1024,384]{2,1,0:T(8,128)(2,1)}, u32[]{:S(2)}) copy-start(bf16[2,1024,384]{2,1,0:T(8,128)(2,1)} %x_ref.7) | copy-start | bytes 4718596
  87.4 1.9 %collective-permute-start.1 = (bf16[128,16,128]{2,1,0:T(8,128)(2,1)S(1)}, bf16[128,16,128]{2,1,0:T(8,128)(2,1)S(1)}, u32[]{:S(2)}, u32[]{:S(2)}) collective-permute-start(bf16[128,16,128]{2,1,0:T(8,128)(2,1)S(1)} %all_to_all.31.a_ref), channel_id=1, source_target_pairs={{0,1},{1,0},{2,3},{3,2},{4,5},{5,4},{6,7},{7,6},{8,9},{9,8},{10,11... | collective-permute-start | bytes 1572872 | tf_op jit(solution)/shard_map/ppermute | solution.py:377
  90.7 0.9 copy-start.5
  91.5 14.1 %all-to-all-start.3 = ((bf16[8,2,64,128]{3,2,1,0:T(8,128)(2,1)}), bf16[8,2,64,128]{3,2,1,0:T(8,128)(2,1)S(1)}, u32[]{:S(2)}, u32[]{:S(2)}) async-start(bf16[8,2,64,128]{3,2,1,0:T(8,128)(2,1)} %get-tuple-element.12), calls=%async_computation.3 | async-start | bytes 524288 | tf_op jit(solution)/shard_map/all_to_all | solution.py:370
  95.0 2.4 %copy-start.1 = (bf16[2,3072,384]{2,1,0:T(8,128)(2,1)S(1)}, bf16[2,3072,384]{2,1,0:T(8,128)(2,1)}, u32[]{:S(2)}) copy-start(bf16[2,3072,384]{2,1,0:T(8,128)(2,1)} %e_ref.7) | copy-start | bytes 14155780
  97.4 1.1 copy-start.6
  98.5 14.1 %copy-start.7 = (bf16[2,64,3072]{2,1,0:T(8,128)(2,1)S(1)}, bf16[2,64,3072]{2,1,0:T(8,128)(2,1)}, u32[]{:S(2)}) copy-start(bf16[2,64,3072]{2,1,0:T(8,128)(2,1)} %copy-done.5) | copy-start | bytes 2359300
  106.7 17.3 %all-to-all-start.4 = ((f32[32,16,128]{2,1,0:T(8,128)}), f32[32,16,128]{2,1,0:T(8,128)S(1)}, u32[]{:S(2)}, u32[]{:S(2)}) async-start(f32[32,16,128]{2,1,0:T(8,128)} %right_term.1), calls=%async_computation.4 | async-start | bytes 524288 | tf_op jit(solution)/shard_map/all_to_all | solution.py:370
  124.7 23.2 %all-to-all-start.5 = ((f32[32,16,128]{2,1,0:T(8,128)}), f32[32,16,128]{2,1,0:T(8,128)S(1)}, u32[]{:S(2)}, u32[]{:S(2)}) async-start(f32[32,16,128]{2,1,0:T(8,128)} %sum_copies.3), calls=%async_computation.5 | async-start | bytes 524288 | tf_op jit(solution)/shard_map/all_to_all | solution.py:370
Sparse Core Ops, SparseCore 0:
  10.2 51.8 all-gather.4
  63.9 48.5 all-gather.6

commit v3 on v2

--- a/solution.py
+++ b/solution.py
@@ -247,7 +247,7 @@
 
 def moment_kernel(y_ref, x_ref, e_ref, o_ref):
     y = jnp.concatenate([y_ref[k] for k in range(y_ref.shape[0])], axis=1)
-    o_ref[...] = dot(y, x_ref[0], ((1,), (0,))) + e_ref[0].astype(F32)
+    o_ref[...] = (dot(y, x_ref[0], ((1,), (0,))) + e_ref[0].astype(F32)).astype(BF16)
 
 
 def moment_of(grad_t, context, error_in, layer):
@@ -256,7 +256,7 @@
     step = 512
     return pl.pallas_call(
         moment_kernel,
-        out_shape=jax.ShapeDtypeStruct((rows, width), F32),
+        out_shape=jax.ShapeDtypeStruct((rows, width), BF16),
         grid=(rows // step,),
         in_specs=[
             pl.BlockSpec((blocks, step, 128), lambda d: (0, d, 0)),
@@ -332,7 +332,7 @@
 
         @pl.when(layer == which)
         def _():
-            e_ref[0] = (m_ref[...] + update).astype(BF16)
+            e_ref[0] = (m_ref[...].astype(F32) + update).astype(BF16)
 
 
 def outputs(right, inverse, turned, own_left, moments, replicas):
@@ -383,7 +383,8 @@
     core = lax.axis_index("tensor_1").astype(jnp.int32).reshape(1)
     z = exchanged(sketch(right_init, context), TENSOR)
     grads = []
-    for turned in turn(out_grad):
+    turns = turn(out_grad)
+    for turned in turns:
         grads.append(lax.all_gather(turned, TENSOR, axis=0, tiled=False))
     error_part = error_sketch(right_init, error_in)
     send, keep = left_term(core, z, out_grad, error_part)

time: 166 us -> 163 us (0.982)
  Pallas kernels: 46.2 us -> 44.1 us
  local copies, waits for them, and re-layouts: 9.23 us -> 7.15 us
    unnamed x18 -> x12, local copies, waits for them, and re-layouts: 9.13 us -> 7.05 us
where the time goes in v3:
time: 163 us; the launch traced here: 162 us
  blocking collectives  57.8 us (35%)
  Pallas kernels  44.1 us (27%)
  starting transfers between devices  19.6 us (12%)
  waiting for transfers between devices  19 us (12%)
  between operations  14.1 us (9%)
  local copies, waits for them, and re-layouts  7.15 us (4%)
    all_to_all x2, blocking collectives, exchanged(): return lax.all_to_all(x, axis, 0, 0, tiled=True)  57.8 us
    all_to_all x4, starting transfers between devices, exchanged(): return lax.all_to_all(x, axis, 0, 0, tiled=True)  19.5 us
    pallas_call x2, Pallas kernels, moment_of(): pl.pallas_call(moment_kernel, out_shape=jax.ShapeDtypeStruct((rows, width...  16.7 us
    all_to_all x4, waiting for transfers between devices, exchanged(): return lax.all_to_all(x, axis, 0, 0, tiled=True)  13.3 us
    pallas_call x1, Pallas kernels, outputs(): pl.pallas_call(functools.partial(outputs_kernel, replicas=replicas), out_...  8.71 us
    unnamed x12, local copies, waits for them, and re-layouts  7.05 us
    pallas_call x1, Pallas kernels, inverse_of_gram(): pl.pallas_call(inverse_kernel, out_shape=(jax.ShapeDtypeStruct((layers, r...  6.85 us
    ppermute x2, waiting for transfers between devices, swapped(): return lax.ppermute(x, 'tensor_1', SWAP)  4.99 us
  transfers between devices with their start and end apart: 8, of which 5 were waited for; matrix products, arithmetic and copies ran while one was open for 0% of the time, Pallas kernels for 21%

profile of v3, /device:TPU:2, one launch (start us, length us, event | category | flops | bytes accessed | tf_op | source)
XLA Modules:
  0.0 161.8 jit_solution(1165678184516435692)
XLA Ops:
  7.2 0.0 all-gather.5.cloned.1.call-start
  7.2 0.0 copy-start.3
  7.2 1.4 copy-done.3
  8.6 1.4 turn.1
  10.0 0.0 all-gather.5.cloned.1.call-update
  10.1 0.0 all-gather.7.cloned.1.call-start
  10.1 0.7 all-gather.7.cloned.1.call-update
  10.8 2.9 %sketch.1 = bf16[8,2,64,128]{3,2,1,0:T(8,128)(2,1)} custom-call(f32[2,64,384]{2,1,0:T(8,128)} %r_ref.3, bf16[2,1024,384]{2,1,0:T(8,128)(2,1)} %x_ref.7), custom_call_target="tpu_custom_call" | custom-call | flops 400000000 | bytes 2000000 | tf_op jit(solution)/shard_map/sketch/pallas_call | solution.py:52
  13.7 4.5 %all-to-all-start = ((bf16[8,2,64,128]{3,2,1,0:T(8,128)(2,1)}), bf16[8,2,64,128]{3,2,1,0:T(8,128)(2,1)S(1)}, u32[]{:S(2)}, u32[]{:S(2)}) async-start(bf16[8,2,64,128]{3,2,1,0:T(8,128)(2,1)} %sketch.1), calls=%async_computation | async-start | bytes 524288 | tf_op jit(solution)/shard_map/all_to_all | solution.py:370
  18.2 0.0 copy-start
  18.2 2.3 %copy-done = bf16[2,3072,384]{2,1,0:T(8,128)(2,1)S(1)} copy-done((bf16[2,3072,384]{2,1,0:T(8,128)(2,1)S(1)}, bf16[2,3072,384]{2,1,0:T(8,128)(2,1)}, u32[]{:S(2)}) %copy-start) | copy-done | bytes 4718616
  20.5 0.0 copy-start.5
  20.5 0.9 copy-done.5
  21.4 0.0 copy-start.4
  21.4 2.7 %error_sketch.1.e_ref = f32[2,64,3072]{2,1,0:T(8,128)S(1)} custom-call(f32[2,64,384]{2,1,0:T(8,128)S(1)} %copy-done.5, bf16[2,3072,384]{2,1,0:T(8,128)(2,1)S(1)} %copy-done), custom_call_target="tpu_custom_call" | custom-call | flops 600000000 | bytes 7000000 | tf_op jit(solution)/shard_map/error_sketch/pallas_call | solution.py:74
  24.1 1.5 all-to-all-done.z_ref
  25.7 0.0 copy-done.4
  25.7 0.6 left_term.1
  26.2 0.1 collective-permute-start
  26.3 3.1 %collective-permute-done.b_ref = f32[64,3072]{1,0:T(8,128)S(1)} collective-permute-done((f32[64,3072]{1,0:T(8,128)S(1)}, f32[64,3072]{1,0:T(8,128)S(1)}, u32[]{:S(2)}, u32[]{:S(2)}) %collective-permute-start) | collective-permute-done | bytes 786464 | tf_op jit(solution)/shard_map/ppermute | solution.py:377
  29.4 0.1 cut.1
  29.5 32.6 %all_to_all.30.x_ref = bf16[128,16,128]{2,1,0:T(8,128)(2,1)S(1)} all-to-all(bf16[128,16,128]{2,1,0:T(8,128)(2,1)S(1)} %cut.1), channel_id=1, replica_groups=mesh['dp_0'=4,'dp_1'=8,'tensor_0'=4,'tensor_1'=2] {'dp_0','dp_1','tensor..., dimensions={0} | all-to-all | bytes 1048576 | tf_op jit(solution)/shard_map/all_to_all | solution.py:370
  62.1 0.1 sum_copies.2
  62.2 25.2 %all_to_all.31.a_ref = bf16[128,16,128]{2,1,0:T(8,128)(2,1)S(1)} all-to-all(bf16[128,16,128]{2,1,0:T(8,128)(2,1)S(1)} %sum_copies.2), channel_id=1, replica_groups=mesh['dp_0'=4,'dp_1'=8,'tensor_0'=4,'tensor_1'=2] {'dp_0','dp_1','tensor..., dimensions={0} | all-to-all | bytes 1048576 | tf_op jit(solution)/shard_map/all_to_all | solution.py:370
  87.4 0.0 collective-permute-start.1
  87.4 1.9 %collective-permute-done.1.b_ref = bf16[128,16,128]{2,1,0:T(8,128)(2,1)S(1)} collective-permute-done((bf16[128,16,128]{2,1,0:T(8,128)(2,1)S(1)}, bf16[128,16,128]{2,1,0:T(8,128)(2,1)S(1)}, u32[]{:S(2)}, u32[]{:S(2)}) %collective-permute-start.1) | collective-permute-done | bytes 524320 | tf_op jit(solution)/shard_map/ppermute | solution.py:377
  89.3 1.4 own_tokens.1
  90.7 3.4 %all-to-all-start.3 = ((bf16[8,2,64,128]{3,2,1,0:T(8,128)(2,1)}), bf16[8,2,64,128]{3,2,1,0:T(8,128)(2,1)S(1)}, u32[]{:S(2)}, u32[]{:S(2)}) async-start(bf16[8,2,64,128]{3,2,1,0:T(8,128)(2,1)} %get-tuple-element.12), calls=%async_computation.3 | async-start | bytes 524288 | tf_op jit(solution)/shard_map/all_to_all | solution.py:370
  94.2 0.0 copy-start.1
  94.2 2.4 %copy-done.1 = bf16[2,3072,384]{2,1,0:T(8,128)(2,1)S(1)} copy-done((bf16[2,3072,384]{2,1,0:T(8,128)(2,1)S(1)}, bf16[2,3072,384]{2,1,0:T(8,128)(2,1)}, u32[]{:S(2)}) %copy-start.1) | copy-done | bytes 4718616
  96.5 0.0 copy-start.2
  96.5 0.9 left_error.1.e_ref
  97.4 7.4 %all-to-all-done.3.w_ref = bf16[8,2,64,128]{3,2,1,0:T(8,128)(2,1)S(1)} async-done(((bf16[8,2,64,128]{3,2,1,0:T(8,128)(2,1)}), bf16[8,2,64,128]{3,2,1,0:T(8,128)(2,1)S(1)}, u32[]{:S(2)}, u32[]{:S(2)}) %all-to-all-start.3) | async-done | bytes 262176 | tf_op jit(solution)/shard_map/all_to_all | solution.py:370
  104.8 0.0 copy-done.2
  104.8 1.1 right_term.1
  105.9 6.0 %all-to-all-start.4 = ((f32[32,16,128]{2,1,0:T(8,128)}), f32[32,16,128]{2,1,0:T(8,128)S(1)}, u32[]{:S(2)}, u32[]{:S(2)}) async-start(f32[32,16,128]{2,1,0:T(8,128)} %right_term.1), calls=%async_computation.4 | async-start | bytes 524288 | tf_op jit(solution)/shard_map/all_to_all | solution.py:370
  111.9 0.1 constant_dynamic-slice_fusion.own_ref
  112.0 6.9 %gram_inverse.1 = (f32[2,64,64]{2,1,0:T(8,128)S(1)}, bf16[2,3072,128]{2,1,0:T(8,128)(2,1)S(1)}) custom-call(bf16[2,64,3072]{2,1,0:T(8,128)(2,1)S(1)} %get-tuple-element.13.l_ref), custom_call_target="tpu_custom_call" | custom-call | flops 5000000000 | bytes 2000000 | tf_op jit(solution)/shard_map/gram_inverse/pallas_call | solution.py:299
  118.8 4.3 %all-to-all-done.4.x_ref = f32[32,16,128]{2,1,0:T(8,128)S(1)} async-done(((f32[32,16,128]{2,1,0:T(8,128)}), f32[32,16,128]{2,1,0:T(8,128)S(1)}, u32[]{:S(2)}, u32[]{:S(2)}) %all-to-all-start.4) | async-done | bytes 262176 | tf_op jit(solution)/shard_map/all_to_all | solution.py:370
  123.2 0.7 sum_copies.3
  123.9 5.6 %all-to-all-start.5 = ((f32[32,16,128]{2,1,0:T(8,128)}), f32[32,16,128]{2,1,0:T(8,128)S(1)}, u32[]{:S(2)}, u32[]{:S(2)}) async-start(f32[32,16,128]{2,1,0:T(8,128)} %sum_copies.3), calls=%async_computation.5 | async-start | bytes 524288 | tf_op jit(solution)/shard_map/all_to_all | solution.py:370
  129.5 0.0 all-gather.5.cloned.1.call-done
  129.5 8.4 %shard_map.59.m0_ref = bf16[3072,384]{1,0:T(8,128)(2,1)} custom-call(bf16[8,3072,128]{2,1,0:T(8,128)(2,1)} %bitcast.3, bf16[2,1024,384]{2,1,0:T(8,128)(2,1)} %x_ref.7, bf16[2,3072,384]{2,1,0:T(8,128)(2,1)} %e_ref.7), custom_call_target="tpu_custom_call" | custom-call | flops 4000000000 | bytes 14000000 | tf_op jit(solution)/shard_map/pallas_call | solution.py:257
  137.9 0.0 all-gather.7.cloned.1.call-done
  137.9 8.4 %shard_map.60.m1_ref = bf16[3072,384]{1,0:T(8,128)(2,1)} custom-call(bf16[8,3072,128]{2,1,0:T(8,128)(2,1)} %bitcast.4, bf16[2,1024,384]{2,1,0:T(8,128)(2,1)} %x_ref.7, bf16[2,3072,384]{2,1,0:T(8,128)(2,1)} %e_ref.7), custom_call_target="tpu_custom_call" | custom-call | flops 4000000000 | bytes 14000000 | tf_op jit(solution)/shard_map/pallas_call | solution.py:257
  146.3 0.0 all-to-all-done.5.r_ref
  146.3 8.7 %outputs.1 = (bf16[2,96,384]{2,1,0:T(8,128)(2,1)}, bf16[2,3072,384]{2,1,0:T(8,128)(2,1)}) custom-call(f32[32,16,128]{2,1,0:T(8,128)S(1)} %all-to-all-done.5.r_ref, f32[2,64,64]{2,1,0:T(8,128)S(1)} %get-tuple-element.14.g_ref, bf16[2,3072,128]{2,1,0:T(8,128)(2,1)S(1)} %get-tuple-element.15.t_ref, bf16[2,64,96]{2,1,0:T(8,128)(2,1)S(1)} %constant_dynamic-slice_fusion.own_ref, ...), custom_call_target="tpu_custom_call" | custom-call | flops 600000000 | bytes 15000000 | tf_op jit(solution)/shard_map/outputs/pallas_call | solution.py:343
Async XLA Ops:
  7.2 122.4 %all-gather.5.cloned.1.call-start = ((), (), s32[]{:S(2)}) async-start(), calls=%async_computation.6 | async-start | bytes 7077888 | tf_op jit(solution)/shard_map/all_gather | solution.py:388
  7.2 1.4 copy-start.3
  10.1 127.8 %all-gather.7.cloned.1.call-start = ((), (), s32[]{:S(2)}) async-start(), calls=%async_computation.7 | async-start | bytes 7077888 | tf_op jit(solution)/shard_map/all_gather | solution.py:388
  13.7 12.0 %all-to-all-start = ((bf16[8,2,64,128]{3,2,1,0:T(8,128)(2,1)}), bf16[8,2,64,128]{3,2,1,0:T(8,128)(2,1)S(1)}, u32[]{:S(2)}, u32[]{:S(2)}) async-start(bf16[8,2,64,128]{3,2,1,0:T(8,128)(2,1)} %sketch.1), calls=%async_computation | async-start | bytes 524288 | tf_op jit(solution)/shard_map/all_to_all | solution.py:370
  18.2 2.3 %copy-start = (bf16[2,3072,384]{2,1,0:T(8,128)(2,1)S(1)}, bf16[2,3072,384]{2,1,0:T(8,128)(2,1)}, u32[]{:S(2)}) copy-start(bf16[2,3072,384]{2,1,0:T(8,128)(2,1)} %e_ref.7) | copy-start | bytes 14155780
  20.5 0.9 copy-start.5
  21.4 4.2 %copy-start.4 = (bf16[2,128,3072]{2,1,0:T(8,128)(2,1)S(1)}, bf16[2,128,3072]{2,1,0:T(8,128)(2,1)}, u32[]{:S(2)}) copy-start(bf16[2,128,3072]{2,1,0:T(8,128)(2,1)} %y_ref.5) | copy-start | bytes 4718596
  26.2 3.2 %collective-permute-start = (f32[64,3072]{1,0:T(8,128)S(1)}, f32[64,3072]{1,0:T(8,128)S(1)}, u32[]{:S(2)}, u32[]{:S(2)}) collective-permute-start(f32[64,3072]{1,0:T(8,128)S(1)} %get-tuple-element.11), channel_id=1, source_target_pairs={{0,1},{1,0},{2,3},{3,2},{4,5},{5,4},{6,7},{7,6},{8,9},{9,8},{10,11... | collective-permute-start | bytes 2359304 | tf_op jit(solution)/shard_map/ppermute | solution.py:377
  87.4 1.9 %collective-permute-start.1 = (bf16[128,16,128]{2,1,0:T(8,128)(2,1)S(1)}, bf16[128,16,128]{2,1,0:T(8,128)(2,1)S(1)}, u32[]{:S(2)}, u32[]{:S(2)}) collective-permute-start(bf16[128,16,128]{2,1,0:T(8,128)(2,1)S(1)} %all_to_all.31.a_ref), channel_id=1, source_target_pairs={{0,1},{1,0},{2,3},{3,2},{4,5},{5,4},{6,7},{7,6},{8,9},{9,8},{10,11... | collective-permute-start | bytes 1572872 | tf_op jit(solution)/shard_map/ppermute | solution.py:377
  90.7 14.1 %all-to-all-start.3 = ((bf16[8,2,64,128]{3,2,1,0:T(8,128)(2,1)}), bf16[8,2,64,128]{3,2,1,0:T(8,128)(2,1)S(1)}, u32[]{:S(2)}, u32[]{:S(2)}) async-start(bf16[8,2,64,128]{3,2,1,0:T(8,128)(2,1)} %get-tuple-element.12), calls=%async_computation.3 | async-start | bytes 524288 | tf_op jit(solution)/shard_map/all_to_all | solution.py:370
  94.2 2.4 %copy-start.1 = (bf16[2,3072,384]{2,1,0:T(8,128)(2,1)S(1)}, bf16[2,3072,384]{2,1,0:T(8,128)(2,1)}, u32[]{:S(2)}) copy-start(bf16[2,3072,384]{2,1,0:T(8,128)(2,1)} %e_ref.7) | copy-start | bytes 14155780
  96.5 8.3 %copy-start.2 = (bf16[2,1024,384]{2,1,0:T(8,128)(2,1)S(1)}, bf16[2,1024,384]{2,1,0:T(8,128)(2,1)}, u32[]{:S(2)}) copy-start(bf16[2,1024,384]{2,1,0:T(8,128)(2,1)} %x_ref.7) | copy-start | bytes 4718596
  105.9 17.3 %all-to-all-start.4 = ((f32[32,16,128]{2,1,0:T(8,128)}), f32[32,16,128]{2,1,0:T(8,128)S(1)}, u32[]{:S(2)}, u32[]{:S(2)}) async-start(f32[32,16,128]{2,1,0:T(8,128)} %right_term.1), calls=%async_computation.4 | async-start | bytes 524288 | tf_op jit(solution)/shard_map/all_to_all | solution.py:370
  123.9 22.4 %all-to-all-start.5 = ((f32[32,16,128]{2,1,0:T(8,128)}), f32[32,16,128]{2,1,0:T(8,128)S(1)}, u32[]{:S(2)}, u32[]{:S(2)}) async-start(f32[32,16,128]{2,1,0:T(8,128)} %sum_copies.3), calls=%async_computation.5 | async-start | bytes 524288 | tf_op jit(solution)/shard_map/all_to_all | solution.py:370
Sparse Core Ops, SparseCore 0:
  10.4 51.8 all-gather.4
  64.1 48.5 all-gather.6

commit v4 on v3

--- a/solution.py
+++ b/solution.py
@@ -112,25 +112,26 @@
 
 
 def cut_kernel(a_ref, b_ref, o_ref):
-    bands, lanes = a_ref.shape[0] // 16, a_ref.shape[1] // 128
-    for i in range(bands):
-        for j in range(lanes):
-            rows, cols = slice(i * 16, i * 16 + 16), slice(j * 128, j * 128 + 128)
-            both = a_ref[rows, cols] + b_ref[rows, cols]
-            o_ref[i * lanes + j] = both.astype(BF16)
-    for p in range(bands * lanes, o_ref.shape[0]):
-        o_ref[p] = jnp.zeros(o_ref.shape[1:], BF16)
+    high, wide = o_ref.shape[1:]
+    across = a_ref.shape[1] // wide
+    both = (a_ref[...] + b_ref[...]).astype(BF16)
+    for p in range(o_ref.shape[0]):
+        i, j = divmod(p, across)
+        o_ref[p] = both[i * high : i * high + high, j * wide : j * wide + wide]
 
 
 def cut(a, b, pieces):
+    rank, rows = a.shape
+    high, wide = 4, 384
+    assert pieces * high * wide == rank * rows
     return pl.pallas_call(
         cut_kernel,
-        out_shape=jax.ShapeDtypeStruct((pieces, 16, 128), BF16),
+        out_shape=jax.ShapeDtypeStruct((pieces, high, wide), BF16),
         in_specs=[VMEM, VMEM],
         out_specs=VMEM,
         cost_estimate=cost(4e5, 1.2e6),
         name="cut",
-        compiler_params=room(4),
+        compiler_params=room(6),
     )(a, b)
 
 
@@ -158,9 +159,13 @@
 
 def own_tokens_kernel(core_ref, a_ref, b_ref, y_ref, l_ref, o_ref):
     core = core_ref[0]
-    count, lanes = l_ref.shape[1] // 16, l_ref.shape[2] // 128
+    high, wide = a_ref.shape[1:]
+    across = l_ref.shape[2] // wide
     for which, ref in ((core, a_ref), (1 - core, b_ref)):
-        rows = [jnp.concatenate([ref[i * lanes + j] for j in range(lanes)], axis=1) for i in range(count)]
+        rows = [
+            jnp.concatenate([ref[i * across + j] for j in range(across)], axis=1)
+            for i in range(l_ref.shape[1] // high)
+        ]
         left = jnp.concatenate(rows, axis=0)
         l_ref[which] = left
         w = dot(left, y_ref[which], ((1,), (1,))).astype(BF16)
@@ -327,19 +332,20 @@
         s_ref[0] = s.astype(BF16)
         q_ref[...] = jnp.concatenate(two_parts(q * (-1.0 / replicas)), axis=0)
 
-    update = dot(t_ref[0], q_ref[...], ((1,), (0,)))
+    step = e_ref.shape[1]
+    here = pl.ds(pl.multiple_of(d * step, step), step)
+    update = dot(t_ref[layer, here, :], q_ref[...], ((1,), (0,)))
     for which, m_ref in ((0, m0_ref), (1, m1_ref)):
 
         @pl.when(layer == which)
         def _():
-            e_ref[0] = (m_ref[...].astype(F32) + update).astype(BF16)
+            e_ref[0] = (m_ref[here, :].astype(F32) + update).astype(BF16)
 
 
 def outputs(right, inverse, turned, own_left, moments, replicas):
     rows, width = moments[0].shape
     layers, rank, share = own_left.shape
     step = 768
-    last = rows // step - 1
     return pl.pallas_call(
         functools.partial(outputs_kernel, replicas=replicas),
         out_shape=(
@@ -350,10 +356,10 @@
         in_specs=[
             pl.BlockSpec(right.shape, lambda l, d: (0, 0, 0)),
             pl.BlockSpec((1, rank, rank), lambda l, d: (l, 0, 0)),
-            pl.BlockSpec((1, step, 2 * rank), lambda l, d: (l, d, 0)),
+            VMEM,
             pl.BlockSpec((1, rank, share), lambda l, d: (l, 0, 0)),
-            pl.BlockSpec((step, width), lambda l, d: (d * (1 - l) + last * l, 0)),
-            pl.BlockSpec((step, width), lambda l, d: (d * l, 0)),
+            VMEM,
+            VMEM,
         ],
         out_specs=(
             pl.BlockSpec((1, share, width), lambda l, d: (l, 0, 0)),
@@ -362,7 +368,7 @@
         scratch_shapes=[pltpu.VMEM((2 * rank, width), BF16)],
         cost_estimate=cost(6e8, 15e6),
         name="outputs",
-        compiler_params=room(50),
+        compiler_params=room(14),
     )(right, inverse, turned, own_left, *moments)
 
 

time: 163 us -> 159 us (0.975)
  blocking collectives: 57.8 us -> 52.7 us
  local copies, waits for them, and re-layouts: 7.15 us -> 11.4 us
  Pallas kernels: 44.1 us -> 41.8 us
    all_to_all x2, blocking collectives: 57.8 us -> 52.7 us  [exchanged(): return lax.all_to_all(x, axis, 0, 0, tiled=True)]
    unnamed x12 -> x20, local copies, waits for them, and re-layouts: 7.05 us -> 11.3 us
    pallas_call x1, Pallas kernels: 8.71 us -> 6.15 us  [outputs(): pl.pallas_call(functools.partial(outputs_kernel, replicas=replicas), out_...]
  transfers between devices with their start and end apart: 8 -> 8, of which waited for: 5 -> 5; matrix products, arithmetic and copies ran while one was open for 0% -> 0% of each run, Pallas kernels for 21% -> 22%
where the time goes in v4:
time: 159 us; the launch traced here: 158 us
  blocking collectives  52.7 us (33%)
  Pallas kernels  41.8 us (26%)
  starting transfers between devices  20.4 us (13%)
  waiting for transfers between devices  17.7 us (11%)
  between operations  14.2 us (9%)
  local copies, waits for them, and re-layouts  11.4 us (7%)
    all_to_all x2, blocking collectives, exchanged(): return lax.all_to_all(x, axis, 0, 0, tiled=True)  52.7 us
    all_to_all x4, starting transfers between devices, exchanged(): return lax.all_to_all(x, axis, 0, 0, tiled=True)  20.2 us
    pallas_call x2, Pallas kernels, moment_of(): pl.pallas_call(moment_kernel, out_shape=jax.ShapeDtypeStruct((rows, width...  16.9 us
    all_to_all x4, waiting for transfers between devices, exchanged(): return lax.all_to_all(x, axis, 0, 0, tiled=True)  12.2 us
    unnamed x20, local copies, waits for them, and re-layouts  11.3 us
    pallas_call x1, Pallas kernels, inverse_of_gram(): pl.pallas_call(inverse_kernel, out_shape=(jax.ShapeDtypeStruct((layers, r...  6.85 us
    pallas_call x1, Pallas kernels, outputs(): pl.pallas_call(functools.partial(outputs_kernel, replicas=replicas), out_...  6.15 us
    ppermute x2, waiting for transfers between devices, swapped(): return lax.ppermute(x, 'tensor_1', SWAP)  4.83 us
  transfers between devices with their start and end apart: 8, of which 5 were waited for; matrix products, arithmetic and copies ran while one was open for 0% of the time, Pallas kernels for 22%

profile of v4, /device:TPU:2, one launch (start us, length us, event | category | flops | bytes accessed | tf_op | source)
XLA Modules:
  0.0 158.1 jit_solution(8889851274941335495)
XLA Ops:
  7.2 0.0 all-gather.5.cloned.1.call-start
  7.2 0.0 copy-start.3
  7.2 1.4 copy-done.3
  8.6 1.4 turn.1
  10.0 0.0 all-gather.5.cloned.1.call-update
  10.0 0.0 all-gather.7.cloned.1.call-start
  10.1 0.7 all-gather.7.cloned.1.call-update
  10.8 2.9 %sketch.1 = bf16[8,2,64,128]{3,2,1,0:T(8,128)(2,1)} custom-call(f32[2,64,384]{2,1,0:T(8,128)} %r_ref.3, bf16[2,1024,384]{2,1,0:T(8,128)(2,1)} %x_ref.7), custom_call_target="tpu_custom_call" | custom-call | flops 400000000 | bytes 2000000 | tf_op jit(solution)/shard_map/sketch/pallas_call | solution.py:52
  13.7 4.5 %all-to-all-start = ((bf16[8,2,64,128]{3,2,1,0:T(8,128)(2,1)}), bf16[8,2,64,128]{3,2,1,0:T(8,128)(2,1)S(1)}, u32[]{:S(2)}, u32[]{:S(2)}) async-start(bf16[8,2,64,128]{3,2,1,0:T(8,128)(2,1)} %sketch.1), calls=%async_computation | async-start | bytes 524288 | tf_op jit(solution)/shard_map/all_to_all | solution.py:376
  18.1 0.0 copy-start
  18.1 2.3 %copy-done = bf16[2,3072,384]{2,1,0:T(8,128)(2,1)S(1)} copy-done((bf16[2,3072,384]{2,1,0:T(8,128)(2,1)S(1)}, bf16[2,3072,384]{2,1,0:T(8,128)(2,1)}, u32[]{:S(2)}) %copy-start) | copy-done | bytes 4718616
  20.5 0.0 copy-start.9
  20.5 0.9 copy-done.9
  21.4 0.0 copy-start.4
  21.4 2.7 %error_sketch.1.e_ref = f32[2,64,3072]{2,1,0:T(8,128)S(1)} custom-call(f32[2,64,384]{2,1,0:T(8,128)S(1)} %copy-done.9, bf16[2,3072,384]{2,1,0:T(8,128)(2,1)S(1)} %copy-done), custom_call_target="tpu_custom_call" | custom-call | flops 600000000 | bytes 7000000 | tf_op jit(solution)/shard_map/error_sketch/pallas_call | solution.py:74
  24.1 1.5 all-to-all-done.z_ref
  25.6 0.0 copy-done.4
  25.6 0.6 left_term.1
  26.2 0.1 collective-permute-start
  26.3 3.1 %collective-permute-done.b_ref = f32[64,3072]{1,0:T(8,128)S(1)} collective-permute-done((f32[64,3072]{1,0:T(8,128)S(1)}, f32[64,3072]{1,0:T(8,128)S(1)}, u32[]{:S(2)}, u32[]{:S(2)}) %collective-permute-start) | collective-permute-done | bytes 786464 | tf_op jit(solution)/shard_map/ppermute | solution.py:383
  29.4 0.1 cut.1
  29.5 30.1 %all_to_all.30.x_ref = bf16[128,4,384]{2,1,0:T(4,128)(2,1)S(1)} all-to-all(bf16[128,4,384]{2,1,0:T(4,128)(2,1)S(1)} %cut.1), channel_id=1, replica_groups=mesh['dp_0'=4,'dp_1'=8,'tensor_0'=4,'tensor_1'=2] {'dp_0','dp_1','tensor..., dimensions={0} | all-to-all | bytes 786432 | tf_op jit(solution)/shard_map/all_to_all | solution.py:376
  59.6 0.1 sum_copies.2
  59.7 22.6 %all_to_all.31.a_ref = bf16[128,4,384]{2,1,0:T(4,128)(2,1)S(1)} all-to-all(bf16[128,4,384]{2,1,0:T(4,128)(2,1)S(1)} %sum_copies.2), channel_id=1, replica_groups=mesh['dp_0'=4,'dp_1'=8,'tensor_0'=4,'tensor_1'=2] {'dp_0','dp_1','tensor..., dimensions={0} | all-to-all | bytes 786432 | tf_op jit(solution)/shard_map/all_to_all | solution.py:376
  82.4 0.0 collective-permute-start.1
  82.4 1.7 %collective-permute-done.1.b_ref = bf16[128,4,384]{2,1,0:T(4,128)(2,1)S(1)} collective-permute-done((bf16[128,4,384]{2,1,0:T(4,128)(2,1)S(1)}, bf16[128,4,384]{2,1,0:T(4,128)(2,1)S(1)}, u32[]{:S(2)}, u32[]{:S(2)}) %collective-permute-start.1) | collective-permute-done | bytes 393248 | tf_op jit(solution)/shard_map/ppermute | solution.py:383
  84.1 1.5 own_tokens.1
  85.5 3.4 %all-to-all-start.3 = ((bf16[8,2,64,128]{3,2,1,0:T(8,128)(2,1)}), bf16[8,2,64,128]{3,2,1,0:T(8,128)(2,1)S(1)}, u32[]{:S(2)}, u32[]{:S(2)}) async-start(bf16[8,2,64,128]{3,2,1,0:T(8,128)(2,1)} %get-tuple-element.12), calls=%async_computation.3 | async-start | bytes 524288 | tf_op jit(solution)/shard_map/all_to_all | solution.py:376
  89.0 0.0 copy-start.1
  89.0 2.4 %copy-done.1 = bf16[2,3072,384]{2,1,0:T(8,128)(2,1)S(1)} copy-done((bf16[2,3072,384]{2,1,0:T(8,128)(2,1)S(1)}, bf16[2,3072,384]{2,1,0:T(8,128)(2,1)}, u32[]{:S(2)}) %copy-start.1) | copy-done | bytes 4718616
  91.3 0.0 copy-start.2
  91.3 0.9 left_error.1.e_ref
  92.2 7.4 %all-to-all-done.3.w_ref = bf16[8,2,64,128]{3,2,1,0:T(8,128)(2,1)S(1)} async-done(((bf16[8,2,64,128]{3,2,1,0:T(8,128)(2,1)}), bf16[8,2,64,128]{3,2,1,0:T(8,128)(2,1)S(1)}, u32[]{:S(2)}, u32[]{:S(2)}) %all-to-all-start.3) | async-done | bytes 262176 | tf_op jit(solution)/shard_map/all_to_all | solution.py:376
  99.6 0.0 copy-done.2
  99.6 1.1 right_term.1
  100.7 5.7 %all-to-all-start.4 = ((f32[32,16,128]{2,1,0:T(8,128)}), f32[32,16,128]{2,1,0:T(8,128)S(1)}, u32[]{:S(2)}, u32[]{:S(2)}) async-start(f32[32,16,128]{2,1,0:T(8,128)} %right_term.1), calls=%async_computation.4 | async-start | bytes 524288 | tf_op jit(solution)/shard_map/all_to_all | solution.py:376
  106.4 0.1 constant_dynamic-slice_fusion.own_ref
  106.5 6.9 %gram_inverse.1 = (f32[2,64,64]{2,1,0:T(8,128)S(1)}, bf16[2,3072,128]{2,1,0:T(8,128)(2,1)S(1)}) custom-call(bf16[2,64,3072]{2,1,0:T(8,128)(2,1)S(1)} %get-tuple-element.13.l_ref), custom_call_target="tpu_custom_call" | custom-call | flops 5000000000 | bytes 2000000 | tf_op jit(solution)/shard_map/gram_inverse/pallas_call | solution.py:304
  113.4 0.0 copy-start.7
  113.4 1.2 copy-done.7
  114.5 3.3 %all-to-all-done.4.x_ref = f32[32,16,128]{2,1,0:T(8,128)S(1)} async-done(((f32[32,16,128]{2,1,0:T(8,128)}), f32[32,16,128]{2,1,0:T(8,128)S(1)}, u32[]{:S(2)}, u32[]{:S(2)}) %all-to-all-start.4) | async-done | bytes 262176 | tf_op jit(solution)/shard_map/all_to_all | solution.py:376
  117.8 0.7 sum_copies.3
  118.5 6.6 %all-to-all-start.5 = ((f32[32,16,128]{2,1,0:T(8,128)}), f32[32,16,128]{2,1,0:T(8,128)S(1)}, u32[]{:S(2)}, u32[]{:S(2)}) async-start(f32[32,16,128]{2,1,0:T(8,128)} %sum_copies.3), calls=%async_computation.5 | async-start | bytes 524288 | tf_op jit(solution)/shard_map/all_to_all | solution.py:376
  125.1 0.0 all-gather.5.cloned.1.call-done
  125.2 8.4 %shard_map.59.m0_ref = bf16[3072,384]{1,0:T(8,128)(2,1)} custom-call(bf16[8,3072,128]{2,1,0:T(8,128)(2,1)} %bitcast.3, bf16[2,1024,384]{2,1,0:T(8,128)(2,1)} %x_ref.7, bf16[2,3072,384]{2,1,0:T(8,128)(2,1)} %e_ref.7), custom_call_target="tpu_custom_call" | custom-call | flops 4000000000 | bytes 14000000 | tf_op jit(solution)/shard_map/pallas_call | solution.py:262
  133.5 0.0 all-gather.7.cloned.1.call-done
  133.5 0.0 copy-start.5
  133.5 8.5 %shard_map.60.m1_ref = bf16[3072,384]{1,0:T(8,128)(2,1)} custom-call(bf16[8,3072,128]{2,1,0:T(8,128)(2,1)} %bitcast.4, bf16[2,1024,384]{2,1,0:T(8,128)(2,1)} %x_ref.7, bf16[2,3072,384]{2,1,0:T(8,128)(2,1)} %e_ref.7), custom_call_target="tpu_custom_call" | custom-call | flops 4000000000 | bytes 14000000 | tf_op jit(solution)/shard_map/pallas_call | solution.py:262
  142.1 0.0 all-to-all-done.5.r_ref
  142.1 0.0 copy-done.5
  142.1 0.0 copy-start.6
  142.1 1.7 %copy-done.6 = bf16[3072,384]{1,0:T(8,128)(2,1)S(1)} copy-done((bf16[3072,384]{1,0:T(8,128)(2,1)S(1)}, bf16[3072,384]{1,0:T(8,128)(2,1)}, u32[]{:S(2)}) %copy-start.6) | copy-done | bytes 2359320
  143.7 0.0 copy-start.8
  143.7 1.4 copy-done.8
  145.1 6.1 %outputs.1 = (bf16[2,96,384]{2,1,0:T(8,128)(2,1)}, bf16[2,3072,384]{2,1,0:T(8,128)(2,1)}) custom-call(f32[32,16,128]{2,1,0:T(8,128)S(1)} %all-to-all-done.5.r_ref, f32[2,64,64]{2,1,0:T(8,128)S(1)} %get-tuple-element.14.g_ref, bf16[2,3072,128]{2,1,0:T(8,128)(2,1)S(1)} %copy-done.8, bf16[2,64,96]{2,1,0:T(8,128)(2,1)S(1)} %constant_dynamic-slice_fusion.own_ref, ...), custom_call_target="tpu_custom_call" | custom-call | flops 600000000 | bytes 15000000 | tf_op jit(solution)/shard_map/outputs/pallas_call | solution.py:349
Async XLA Ops:
  7.2 118.0 %all-gather.5.cloned.1.call-start = ((), (), s32[]{:S(2)}) async-start(), calls=%async_computation.6 | async-start | bytes 7077888 | tf_op jit(solution)/shard_map/all_gather | solution.py:394
  7.2 1.4 copy-start.3
  10.0 123.5 %all-gather.7.cloned.1.call-start = ((), (), s32[]{:S(2)}) async-start(), calls=%async_computation.7 | async-start | bytes 7077888 | tf_op jit(solution)/shard_map/all_gather | solution.py:394
  13.7 12.0 %all-to-all-start = ((bf16[8,2,64,128]{3,2,1,0:T(8,128)(2,1)}), bf16[8,2,64,128]{3,2,1,0:T(8,128)(2,1)S(1)}, u32[]{:S(2)}, u32[]{:S(2)}) async-start(bf16[8,2,64,128]{3,2,1,0:T(8,128)(2,1)} %sketch.1), calls=%async_computation | async-start | bytes 524288 | tf_op jit(solution)/shard_map/all_to_all | solution.py:376
  18.1 2.3 %copy-start = (bf16[2,3072,384]{2,1,0:T(8,128)(2,1)S(1)}, bf16[2,3072,384]{2,1,0:T(8,128)(2,1)}, u32[]{:S(2)}) copy-start(bf16[2,3072,384]{2,1,0:T(8,128)(2,1)} %e_ref.7) | copy-start | bytes 14155780
  20.5 0.9 copy-start.9
  21.4 4.2 %copy-start.4 = (bf16[2,128,3072]{2,1,0:T(8,128)(2,1)S(1)}, bf16[2,128,3072]{2,1,0:T(8,128)(2,1)}, u32[]{:S(2)}) copy-start(bf16[2,128,3072]{2,1,0:T(8,128)(2,1)} %y_ref.5) | copy-start | bytes 4718596
  26.2 3.2 %collective-permute-start = (f32[64,3072]{1,0:T(8,128)S(1)}, f32[64,3072]{1,0:T(8,128)S(1)}, u32[]{:S(2)}, u32[]{:S(2)}) collective-permute-start(f32[64,3072]{1,0:T(8,128)S(1)} %get-tuple-element.11), channel_id=1, source_target_pairs={{0,1},{1,0},{2,3},{3,2},{4,5},{5,4},{6,7},{7,6},{8,9},{9,8},{10,11... | collective-permute-start | bytes 2359304 | tf_op jit(solution)/shard_map/ppermute | solution.py:383
  82.4 1.7 %collective-permute-start.1 = (bf16[128,4,384]{2,1,0:T(4,128)(2,1)S(1)}, bf16[128,4,384]{2,1,0:T(4,128)(2,1)S(1)}, u32[]{:S(2)}, u32[]{:S(2)}) collective-permute-start(bf16[128,4,384]{2,1,0:T(4,128)(2,1)S(1)} %all_to_all.31.a_ref), channel_id=1, source_target_pairs={{0,1},{1,0},{2,3},{3,2},{4,5},{5,4},{6,7},{7,6},{8,9},{9,8},{10,11... | collective-permute-start | bytes 1179656 | tf_op jit(solution)/shard_map/ppermute | solution.py:383
  85.5 14.1 %all-to-all-start.3 = ((bf16[8,2,64,128]{3,2,1,0:T(8,128)(2,1)}), bf16[8,2,64,128]{3,2,1,0:T(8,128)(2,1)S(1)}, u32[]{:S(2)}, u32[]{:S(2)}) async-start(bf16[8,2,64,128]{3,2,1,0:T(8,128)(2,1)} %get-tuple-element.12), calls=%async_computation.3 | async-start | bytes 524288 | tf_op jit(solution)/shard_map/all_to_all | solution.py:376
  89.0 2.4 %copy-start.1 = (bf16[2,3072,384]{2,1,0:T(8,128)(2,1)S(1)}, bf16[2,3072,384]{2,1,0:T(8,128)(2,1)}, u32[]{:S(2)}) copy-start(bf16[2,3072,384]{2,1,0:T(8,128)(2,1)} %e_ref.7) | copy-start | bytes 14155780
  91.3 8.3 %copy-start.2 = (bf16[2,1024,384]{2,1,0:T(8,128)(2,1)S(1)}, bf16[2,1024,384]{2,1,0:T(8,128)(2,1)}, u32[]{:S(2)}) copy-start(bf16[2,1024,384]{2,1,0:T(8,128)(2,1)} %x_ref.7) | copy-start | bytes 4718596
  100.7 17.1 %all-to-all-start.4 = ((f32[32,16,128]{2,1,0:T(8,128)}), f32[32,16,128]{2,1,0:T(8,128)S(1)}, u32[]{:S(2)}, u32[]{:S(2)}) async-start(f32[32,16,128]{2,1,0:T(8,128)} %right_term.1), calls=%async_computation.4 | async-start | bytes 524288 | tf_op jit(solution)/shard_map/all_to_all | solution.py:376
  113.4 1.2 copy-start.7
  118.5 23.5 %all-to-all-start.5 = ((f32[32,16,128]{2,1,0:T(8,128)}), f32[32,16,128]{2,1,0:T(8,128)S(1)}, u32[]{:S(2)}, u32[]{:S(2)}) async-start(f32[32,16,128]{2,1,0:T(8,128)} %sum_copies.3), calls=%async_computation.5 | async-start | bytes 524288 | tf_op jit(solution)/shard_map/all_to_all | solution.py:376
  133.5 8.5 %copy-start.5 = (bf16[3072,384]{1,0:T(8,128)(2,1)S(1)}, bf16[3072,384]{1,0:T(8,128)(2,1)}, u32[]{:S(2)}) copy-start(bf16[3072,384]{1,0:T(8,128)(2,1)} %shard_map.59.m0_ref) | copy-start | bytes 7077892
  142.1 1.7 %copy-start.6 = (bf16[3072,384]{1,0:T(8,128)(2,1)S(1)}, bf16[3072,384]{1,0:T(8,128)(2,1)}, u32[]{:S(2)}) copy-start(bf16[3072,384]{1,0:T(8,128)(2,1)} %shard_map.60.m1_ref) | copy-start | bytes 7077892
  143.7 1.4 copy-start.8
Sparse Core Ops, SparseCore 0:
  10.4 50.5 all-gather.4
  62.8 46.6 all-gather.6

commit v5 on v4

--- a/solution.py
+++ b/solution.py
@@ -246,32 +246,46 @@
         out_specs=[VMEM] * layers,
         cost_estimate=cost(1e8, 3e6),
         name="turn",
-        compiler_params=room(8),
+        compiler_params=room(58),
     )(own_grad)
 
 
-def moment_kernel(y_ref, x_ref, e_ref, o_ref):
-    y = jnp.concatenate([y_ref[k] for k in range(y_ref.shape[0])], axis=1)
-    o_ref[...] = (dot(y, x_ref[0], ((1,), (0,))) + e_ref[0].astype(F32)).astype(BF16)
-
-
-def moment_of(grad_t, context, error_in, layer):
-    blocks, rows, _ = grad_t.shape
+def moment_kernel(core_ref, a_ref, b_ref, x_ref, e_ref, o_ref, rhs_ref):
+    core = core_ref[0]
+    count = a_ref.shape[0]
+
+    @pl.when(pl.program_id(0) == 0)
+    def _():
+        for first, which in ((0, core), (count, 1 - core)):
+            for y in range(count):
+                rows = pl.ds(pl.multiple_of((2 * y + which) * 128, 128), 128)
+                rhs_ref[(first + y) * 128 : (first + y) * 128 + 128] = x_ref[0, rows, :]
+
+    grad = jnp.concatenate([ref[k] for ref in (a_ref, b_ref) for k in range(count)], axis=1)
+    o_ref[...] = (dot(grad, rhs_ref[...], ((1,), (0,))) + e_ref[0].astype(F32)).astype(BF16)
+
+
+def moment_of(core, own, other, context, error_in, layer):
+    blocks, rows, _ = own.shape
     tokens, width = context.shape[1:]
     step = 512
+    part = pl.BlockSpec((blocks, step, 128), lambda d: (0, d, 0))
     return pl.pallas_call(
         moment_kernel,
         out_shape=jax.ShapeDtypeStruct((rows, width), BF16),
         grid=(rows // step,),
         in_specs=[
-            pl.BlockSpec((blocks, step, 128), lambda d: (0, d, 0)),
+            SMEM,
+            part,
+            part,
             pl.BlockSpec((1, tokens, width), lambda d: (layer, 0, 0)),
             pl.BlockSpec((1, step, width), lambda d: (layer, d, 0)),
         ],
         out_specs=pl.BlockSpec((step, width), lambda d: (d, 0)),
+        scratch_shapes=[pltpu.VMEM((tokens, width), BF16)],
         cost_estimate=cost(4e9, 14e6),
-        compiler_params=room(56),
-    )(grad_t, context, error_in)
+        compiler_params=room(58),
+    )(core, own, other, context, error_in)
 
 
 def inverse_kernel(l_ref, o_ref, t_ref):
@@ -332,20 +346,19 @@
         s_ref[0] = s.astype(BF16)
         q_ref[...] = jnp.concatenate(two_parts(q * (-1.0 / replicas)), axis=0)
 
-    step = e_ref.shape[1]
-    here = pl.ds(pl.multiple_of(d * step, step), step)
-    update = dot(t_ref[layer, here, :], q_ref[...], ((1,), (0,)))
+    update = dot(t_ref[0], q_ref[...], ((1,), (0,)))
     for which, m_ref in ((0, m0_ref), (1, m1_ref)):
 
         @pl.when(layer == which)
         def _():
-            e_ref[0] = (m_ref[here, :].astype(F32) + update).astype(BF16)
+            e_ref[0] = (m_ref[...].astype(F32) + update).astype(BF16)
 
 
 def outputs(right, inverse, turned, own_left, moments, replicas):
     rows, width = moments[0].shape
     layers, rank, share = own_left.shape
     step = 768
+    last = rows // step - 1
     return pl.pallas_call(
         functools.partial(outputs_kernel, replicas=replicas),
         out_shape=(
@@ -356,10 +369,10 @@
         in_specs=[
             pl.BlockSpec(right.shape, lambda l, d: (0, 0, 0)),
             pl.BlockSpec((1, rank, rank), lambda l, d: (l, 0, 0)),
-            VMEM,
+            pl.BlockSpec((1, step, 2 * rank), lambda l, d: (l, d, 0)),
             pl.BlockSpec((1, rank, share), lambda l, d: (l, 0, 0)),
-            VMEM,
-            VMEM,
+            pl.BlockSpec((step, width), lambda l, d: (d * (1 - l) + last * l, 0)),
+            pl.BlockSpec((step, width), lambda l, d: (d * l, 0)),
         ],
         out_specs=(
             pl.BlockSpec((1, share, width), lambda l, d: (l, 0, 0)),
@@ -368,7 +381,7 @@
         scratch_shapes=[pltpu.VMEM((2 * rank, width), BF16)],
         cost_estimate=cost(6e8, 15e6),
         name="outputs",
-        compiler_params=room(14),
+        compiler_params=room(50),
     )(right, inverse, turned, own_left, *moments)
 
 
@@ -391,7 +404,7 @@
     grads = []
     turns = turn(out_grad)
     for turned in turns:
-        grads.append(lax.all_gather(turned, TENSOR, axis=0, tiled=False))
+        grads.append(lax.all_gather(turned, "tensor_0", axis=0, tiled=False))
     error_part = error_sketch(right_init, error_in)
     send, keep = left_term(core, z, out_grad, error_part)
     arrived = swapped(send)
@@ -406,7 +419,8 @@
     inverse, turned = inverse_of_gram(left)
     moments = []
     for layer, grad_t in enumerate(grads):
-        moments.append(moment_of(grad_t, context, error_in, layer))
+        grad_other = swapped(grad_t)
+        moments.append(moment_of(core, grad_t, grad_other, context, error_in, layer))
     share = rows // replicas
     own_left = lax.dynamic_slice_in_dim(left, lax.axis_index(DP) * share, share, 2)
     return outputs(right, inverse, turned, own_left, moments, replicas)

time: 159 us -> 204 us (1.28)
  waiting for transfers between devices: 17.7 us -> 71.8 us
  blocking collectives: 52.7 us -> 28.1 us
  starting transfers between devices: 20.4 us -> 32.2 us
  Pallas kernels: 41.8 us -> 47.2 us
    all_gather x2, waiting for transfers between devices: 0.02 us -> 60.9 us  [body(): grads.append(lax.all_gather(turned, 'tensor_0', axis=0, tiled=False))]
    all_to_all x2 -> x1, blocking collectives: 52.7 us -> 28.1 us  [exchanged(): return lax.all_to_all(x, axis, 0, 0, tiled=True)]
    all_to_all x4 -> x5, starting transfers between devices: 20.2 us -> 32.1 us  [exchanged(): return lax.all_to_all(x, axis, 0, 0, tiled=True)]
    all_to_all x4 -> x5, waiting for transfers between devices: 12.2 us -> 8.5 us  [exchanged(): return lax.all_to_all(x, axis, 0, 0, tiled=True)]
    ppermute x2 -> x4, waiting for transfers between devices: 4.83 us -> 1.73 us  [swapped(): return lax.ppermute(x, 'tensor_1', SWAP)]
    pallas_call x1, Pallas kernels: 6.15 us -> 8.7 us  [outputs(): pl.pallas_call(functools.partial(outputs_kernel, replicas=replicas), out_...]
  transfers between devices with their start and end apart: 8 -> 11, of which waited for: 5 -> 6; matrix products, arithmetic and copies ran while one was open for 0% -> 0% of each run, Pallas kernels for 22% -> 18%
where the time goes in v5:
time: 204 us; the launch traced here: 203 us
  waiting for transfers between devices  71.8 us (35%)
  Pallas kernels  47.2 us (23%)
  starting transfers between devices  32.2 us (16%)
  blocking collectives  28.1 us (14%)
  between operations  14.1 us (7%)
  local copies, waits for them, and re-layouts  9.73 us (5%)
    all_gather x2, waiting for transfers between devices, body(): grads.append(lax.all_gather(turned, 'tensor_0', axis=0, tiled=False))  60.9 us
    all_to_all x5, starting transfers between devices, exchanged(): return lax.all_to_all(x, axis, 0, 0, tiled=True)  32.1 us
    all_to_all x1, blocking collectives, exchanged(): return lax.all_to_all(x, axis, 0, 0, tiled=True)  28.1 us
    pallas_call x2, Pallas kernels, moment_of(): pl.pallas_call(moment_kernel, out_shape=jax.ShapeDtypeStruct((rows, width...  16.9 us
    unnamed x20, local copies, waits for them, and re-layouts  9.63 us
    pallas_call x1, Pallas kernels, outputs(): pl.pallas_call(functools.partial(outputs_kernel, replicas=replicas), out_...  8.7 us
    all_to_all x5, waiting for transfers between devices, exchanged(): return lax.all_to_all(x, axis, 0, 0, tiled=True)  8.5 us
    pallas_call x1, Pallas kernels, inverse_of_gram(): pl.pallas_call(inverse_kernel, out_shape=(jax.ShapeDtypeStruct((layers, r...  6.85 us
  transfers between devices with their start and end apart: 11, of which 6 were waited for; matrix products, arithmetic and copies ran while one was open for 0% of the time, Pallas kernels for 18%

profile of v5, /device:TPU:2, one launch (start us, length us, event | category | flops | bytes accessed | tf_op | source)
XLA Modules:
  0.0 203.2 jit_solution(18224328459060960930)
XLA Ops:
  7.2 0.0 all-gather.5.cloned.1.call-start
  7.2 2.9 %turn.1 = (bf16[3072,128]{1,0:T(8,128)(2,1)}, bf16[3072,128]{1,0:T(8,128)(2,1)}) custom-call(bf16[2,128,3072]{2,1,0:T(8,128)(2,1)} %y_ref.5), custom_call_target="tpu_custom_call" | custom-call | flops 100000000 | bytes 3000000 | tf_op jit(solution)/shard_map/turn/pallas_call | solution.py:242
  10.1 0.0 all-gather.5.cloned.1.call-update
  10.1 0.0 all-gather.7.cloned.1.call-start
  10.1 0.7 all-gather.7.cloned.1.call-update
  10.8 2.9 %sketch.1 = bf16[8,2,64,128]{3,2,1,0:T(8,128)(2,1)} custom-call(f32[2,64,384]{2,1,0:T(8,128)} %r_ref.3, bf16[2,1024,384]{2,1,0:T(8,128)(2,1)} %x_ref.7), custom_call_target="tpu_custom_call" | custom-call | flops 400000000 | bytes 2000000 | tf_op jit(solution)/shard_map/sketch/pallas_call | solution.py:52
  13.7 4.5 %all-to-all-start = ((bf16[8,2,64,128]{3,2,1,0:T(8,128)(2,1)}), bf16[8,2,64,128]{3,2,1,0:T(8,128)(2,1)S(1)}, u32[]{:S(2)}, u32[]{:S(2)}) async-start(bf16[8,2,64,128]{3,2,1,0:T(8,128)(2,1)} %sketch.1), calls=%async_computation | async-start | bytes 524288 | tf_op jit(solution)/shard_map/all_to_all | solution.py:389
  18.2 0.0 copy-start
  18.2 2.3 %copy-done = bf16[2,3072,384]{2,1,0:T(8,128)(2,1)S(1)} copy-done((bf16[2,3072,384]{2,1,0:T(8,128)(2,1)S(1)}, bf16[2,3072,384]{2,1,0:T(8,128)(2,1)}, u32[]{:S(2)}) %copy-start) | copy-done | bytes 4718616
  20.5 0.0 copy-start.7
  20.5 0.9 copy-done.7
  21.4 0.0 copy-start.3
  21.4 2.7 %error_sketch.1.e_ref = f32[2,64,3072]{2,1,0:T(8,128)S(1)} custom-call(f32[2,64,384]{2,1,0:T(8,128)S(1)} %copy-done.7, bf16[2,3072,384]{2,1,0:T(8,128)(2,1)S(1)} %copy-done), custom_call_target="tpu_custom_call" | custom-call | flops 600000000 | bytes 7000000 | tf_op jit(solution)/shard_map/error_sketch/pallas_call | solution.py:74
  24.1 1.5 all-to-all-done.z_ref
  25.7 0.0 copy-done.3
  25.7 1.2 left_term.1
  26.9 0.0 copy-start.8
  26.9 0.9 copy-done.8
  27.8 0.0 collective-permute-start
  27.8 27.5 %all-gather.5.cloned.1.call-done = bf16[12288,128]{1,0:T(8,128)(2,1)} async-done(((bf16[3072,128]{1,0:T(8,128)(2,1)}), bf16[12288,128]{1,0:T(8,128)(2,1)}) %all-gather.5.cloned.1.call-update) | async-done | bytes 3145744 | tf_op jit(solution)/shard_map/all_gather | solution.py:407
  55.3 0.0 collective-permute-start.2
  55.3 0.0 collective-permute-done.b_ref
  55.3 0.0 copy-start.9
  55.3 1.1 copy-done.9
  56.4 0.8 cut.1
  57.2 12.8 %all-to-all-start.1 = ((bf16[128,4,384]{2,1,0:T(4,128)(2,1)}), bf16[128,4,384]{2,1,0:T(4,128)(2,1)S(1)}, u32[]{:S(2)}, u32[]{:S(2)}) async-start(bf16[128,4,384]{2,1,0:T(4,128)(2,1)} %cut.1), calls=%async_computation.1 | async-start | bytes 786432 | tf_op jit(solution)/shard_map/all_to_all | solution.py:389
  70.0 33.4 %all-gather.7.cloned.1.call-done = bf16[12288,128]{1,0:T(8,128)(2,1)} async-done(((bf16[3072,128]{1,0:T(8,128)(2,1)}), bf16[12288,128]{1,0:T(8,128)(2,1)}) %all-gather.7.cloned.1.call-update) | async-done | bytes 3145744 | tf_op jit(solution)/shard_map/all_gather | solution.py:407
  103.4 0.0 collective-permute-start.3
  103.4 0.0 all-to-all-done.1.x_ref
  103.4 0.1 sum_copies.2
  103.5 28.1 %all_to_all.30.a_ref = bf16[128,4,384]{2,1,0:T(4,128)(2,1)S(1)} all-to-all(bf16[128,4,384]{2,1,0:T(4,128)(2,1)S(1)} %sum_copies.2), channel_id=1, replica_groups=mesh['dp_0'=4,'dp_1'=8,'tensor_0'=4,'tensor_1'=2] {'dp_0','dp_1','tensor..., dimensions={0} | all-to-all | bytes 786432 | tf_op jit(solution)/shard_map/all_to_all | solution.py:389
  131.6 0.0 collective-permute-start.1
  131.6 1.7 collective-permute-done.1.b_ref
  133.4 0.0 copy-start.2
  133.4 1.5 own_tokens.1
  134.8 0.0 copy-start.4
  134.8 0.9 copy-done.4
  135.7 3.4 %all-to-all-start.3 = ((bf16[8,2,64,128]{3,2,1,0:T(8,128)(2,1)}), bf16[8,2,64,128]{3,2,1,0:T(8,128)(2,1)S(1)}, u32[]{:S(2)}, u32[]{:S(2)}) async-start(bf16[8,2,64,128]{3,2,1,0:T(8,128)(2,1)} %get-tuple-element.12), calls=%async_computation.3 | async-start | bytes 524288 | tf_op jit(solution)/shard_map/all_to_all | solution.py:389
  139.1 0.0 copy-start.1
  139.1 2.3 %copy-done.1 = bf16[2,3072,384]{2,1,0:T(8,128)(2,1)S(1)} copy-done((bf16[2,3072,384]{2,1,0:T(8,128)(2,1)S(1)}, bf16[2,3072,384]{2,1,0:T(8,128)(2,1)}, u32[]{:S(2)}) %copy-start.1) | copy-done | bytes 4718616
  141.5 0.0 copy-start.5
  141.5 1.1 copy-done.5
  142.6 0.0 copy-start.6
  142.6 0.9 left_error.1.e_ref
  143.5 3.1 %all-to-all-done.3.w_ref = bf16[8,2,64,128]{3,2,1,0:T(8,128)(2,1)S(1)} async-done(((bf16[8,2,64,128]{3,2,1,0:T(8,128)(2,1)}), bf16[8,2,64,128]{3,2,1,0:T(8,128)(2,1)S(1)}, u32[]{:S(2)}, u32[]{:S(2)}) %all-to-all-start.3) | async-done | bytes 262176 | tf_op jit(solution)/shard_map/all_to_all | solution.py:389
  146.6 0.0 copy-done.2
  146.6 1.1 right_term.1
  147.7 5.6 %all-to-all-start.4 = ((f32[32,16,128]{2,1,0:T(8,128)}), f32[32,16,128]{2,1,0:T(8,128)S(1)}, u32[]{:S(2)}, u32[]{:S(2)}) async-start(f32[32,16,128]{2,1,0:T(8,128)} %right_term.1), calls=%async_computation.4 | async-start | bytes 524288 | tf_op jit(solution)/shard_map/all_to_all | solution.py:389
  153.2 0.0 copy-done.6
  153.2 0.1 constant_dynamic-slice_fusion.own_ref
  153.3 6.9 %gram_inverse.1 = (f32[2,64,64]{2,1,0:T(8,128)S(1)}, bf16[2,3072,128]{2,1,0:T(8,128)(2,1)S(1)}) custom-call(bf16[2,64,3072]{2,1,0:T(8,128)(2,1)S(1)} %copy-done.6), custom_call_target="tpu_custom_call" | custom-call | flops 5000000000 | bytes 2000000 | tf_op jit(solution)/shard_map/gram_inverse/pallas_call | solution.py:318
  160.2 3.9 %all-to-all-done.4.x_ref = f32[32,16,128]{2,1,0:T(8,128)S(1)} async-done(((f32[32,16,128]{2,1,0:T(8,128)}), f32[32,16,128]{2,1,0:T(8,128)S(1)}, u32[]{:S(2)}, u32[]{:S(2)}) %all-to-all-start.4) | async-done | bytes 262176 | tf_op jit(solution)/shard_map/all_to_all | solution.py:389
  164.1 0.7 sum_copies.3
  164.8 5.9 %all-to-all-start.5 = ((f32[32,16,128]{2,1,0:T(8,128)}), f32[32,16,128]{2,1,0:T(8,128)S(1)}, u32[]{:S(2)}, u32[]{:S(2)}) async-start(f32[32,16,128]{2,1,0:T(8,128)} %sum_copies.3), calls=%async_computation.5 | async-start | bytes 524288 | tf_op jit(solution)/shard_map/all_to_all | solution.py:389
  170.7 0.0 collective-permute-done.2.b_ref
  170.7 8.5 %shard_map.59.m0_ref = bf16[3072,384]{1,0:T(8,128)(2,1)} custom-call(s32[1]{0:T(128)} %bitcast.core_ref, bf16[4,3072,128]{2,1,0:T(8,128)(2,1)} %bitcast.4, bf16[4,3072,128]{2,1,0:T(8,128)(2,1)} %collective-permute-done.2.b_ref, bf16[2,1024,384]{2,1,0:T(8,128)(2,1)} %x_ref.7, bf16[2,3072,384]{2,1,0:T(8,128)(2,1)} %e_ref.7), custom_call_target="tpu_custom_call" | custom-call | flops 4000000000 | bytes 14000000 | tf_op jit(solution)/shard_map/pallas_call | solution.py:273
  179.2 0.0 collective-permute-done.3.b_ref
  179.2 8.5 %shard_map.60.m1_ref = bf16[3072,384]{1,0:T(8,128)(2,1)} custom-call(s32[1]{0:T(128)} %bitcast.core_ref, bf16[4,3072,128]{2,1,0:T(8,128)(2,1)} %bitcast.6, bf16[4,3072,128]{2,1,0:T(8,128)(2,1)} %collective-permute-done.3.b_ref, bf16[2,1024,384]{2,1,0:T(8,128)(2,1)} %x_ref.7, bf16[2,3072,384]{2,1,0:T(8,128)(2,1)} %e_ref.7), custom_call_target="tpu_custom_call" | custom-call | flops 4000000000 | bytes 14000000 | tf_op jit(solution)/shard_map/pallas_call | solution.py:273
  187.7 0.0 all-to-all-done.5.r_ref
  187.7 8.7 %outputs.1 = (bf16[2,96,384]{2,1,0:T(8,128)(2,1)}, bf16[2,3072,384]{2,1,0:T(8,128)(2,1)}) custom-call(f32[32,16,128]{2,1,0:T(8,128)S(1)} %all-to-all-done.5.r_ref, f32[2,64,64]{2,1,0:T(8,128)S(1)} %get-tuple-element.14.g_ref, bf16[2,3072,128]{2,1,0:T(8,128)(2,1)S(1)} %get-tuple-element.15.t_ref, bf16[2,64,96]{2,1,0:T(8,128)(2,1)S(1)} %constant_dynamic-slice_fusion.own_ref, ...), custom_call_target="tpu_custom_call" | custom-call | flops 600000000 | bytes 15000000 | tf_op jit(solution)/shard_map/outputs/pallas_call | solution.py:362
Async XLA Ops:
  7.2 48.1 %all-gather.5.cloned.1.call-start = ((), (), s32[]{:S(2)}) async-start(), calls=%async_computation.6 | async-start | bytes 3932160 | tf_op jit(solution)/shard_map/all_gather | solution.py:407
  10.1 93.3 %all-gather.7.cloned.1.call-start = ((), (), s32[]{:S(2)}) async-start(), calls=%async_computation.7 | async-start | bytes 3932160 | tf_op jit(solution)/shard_map/all_gather | solution.py:407
  13.7 12.0 %all-to-all-start = ((bf16[8,2,64,128]{3,2,1,0:T(8,128)(2,1)}), bf16[8,2,64,128]{3,2,1,0:T(8,128)(2,1)S(1)}, u32[]{:S(2)}, u32[]{:S(2)}) async-start(bf16[8,2,64,128]{3,2,1,0:T(8,128)(2,1)} %sketch.1), calls=%async_computation | async-start | bytes 524288 | tf_op jit(solution)/shard_map/all_to_all | solution.py:389
  18.2 2.3 %copy-start = (bf16[2,3072,384]{2,1,0:T(8,128)(2,1)S(1)}, bf16[2,3072,384]{2,1,0:T(8,128)(2,1)}, u32[]{:S(2)}) copy-start(bf16[2,3072,384]{2,1,0:T(8,128)(2,1)} %e_ref.7) | copy-start | bytes 14155780
  20.5 0.9 copy-start.7
  21.4 4.2 %copy-start.3 = (bf16[2,128,3072]{2,1,0:T(8,128)(2,1)S(1)}, bf16[2,128,3072]{2,1,0:T(8,128)(2,1)}, u32[]{:S(2)}) copy-start(bf16[2,128,3072]{2,1,0:T(8,128)(2,1)} %y_ref.5) | copy-start | bytes 4718596
  26.9 0.9 copy-start.8
  27.8 27.5 %collective-permute-start = (f32[64,3072]{1,0:T(8,128)}, f32[64,3072]{1,0:T(8,128)S(1)}, u32[]{:S(2)}, u32[]{:S(2)}) collective-permute-start(f32[64,3072]{1,0:T(8,128)} %get-tuple-element.11), channel_id=1, source_target_pairs={{0,1},{1,0},{2,3},{3,2},{4,5},{5,4},{6,7},{7,6},{8,9},{9,8},{10,11... | collective-permute-start | bytes 2359304 | tf_op jit(solution)/shard_map/ppermute | solution.py:396
  55.3 115.5 %collective-permute-start.2 = (bf16[4,3072,128]{2,1,0:T(8,128)(2,1)}, bf16[4,3072,128]{2,1,0:T(8,128)(2,1)}, u32[]{:S(2)}, u32[]{:S(2)}) collective-permute-start(bf16[4,3072,128]{2,1,0:T(8,128)(2,1)} %bitcast.3), channel_id=1, source_target_pairs={{0,1},{1,0},{2,3},{3,2},{4,5},{5,4},{6,7},{7,6},{8,9},{9,8},{10,11... | collective-permute-start | bytes 9437192 | tf_op jit(solution)/shard_map/ppermute | solution.py:396
  55.3 1.1 copy-start.9
  57.2 46.2 %all-to-all-start.1 = ((bf16[128,4,384]{2,1,0:T(4,128)(2,1)}), bf16[128,4,384]{2,1,0:T(4,128)(2,1)S(1)}, u32[]{:S(2)}, u32[]{:S(2)}) async-start(bf16[128,4,384]{2,1,0:T(4,128)(2,1)} %cut.1), calls=%async_computation.1 | async-start | bytes 786432 | tf_op jit(solution)/shard_map/all_to_all | solution.py:389
  103.4 75.8 %collective-permute-start.3 = (bf16[4,3072,128]{2,1,0:T(8,128)(2,1)}, bf16[4,3072,128]{2,1,0:T(8,128)(2,1)}, u32[]{:S(2)}, u32[]{:S(2)}) collective-permute-start(bf16[4,3072,128]{2,1,0:T(8,128)(2,1)} %bitcast.5), channel_id=1, source_target_pairs={{0,1},{1,0},{2,3},{3,2},{4,5},{5,4},{6,7},{7,6},{8,9},{9,8},{10,11... | collective-permute-start | bytes 9437192 | tf_op jit(solution)/shard_map/ppermute | solution.py:396
  131.6 1.7 collective-permute-start.1
  133.4 13.2 %copy-start.2 = (bf16[2,1024,384]{2,1,0:T(8,128)(2,1)S(1)}, bf16[2,1024,384]{2,1,0:T(8,128)(2,1)}, u32[]{:S(2)}) copy-start(bf16[2,1024,384]{2,1,0:T(8,128)(2,1)} %x_ref.7) | copy-start | bytes 4718596
  134.8 0.9 copy-start.4
  135.7 10.8 %all-to-all-start.3 = ((bf16[8,2,64,128]{3,2,1,0:T(8,128)(2,1)}), bf16[8,2,64,128]{3,2,1,0:T(8,128)(2,1)S(1)}, u32[]{:S(2)}, u32[]{:S(2)}) async-start(bf16[8,2,64,128]{3,2,1,0:T(8,128)(2,1)} %get-tuple-element.12), calls=%async_computation.3 | async-start | bytes 524288 | tf_op jit(solution)/shard_map/all_to_all | solution.py:389
  139.1 2.3 %copy-start.1 = (bf16[2,3072,384]{2,1,0:T(8,128)(2,1)S(1)}, bf16[2,3072,384]{2,1,0:T(8,128)(2,1)}, u32[]{:S(2)}) copy-start(bf16[2,3072,384]{2,1,0:T(8,128)(2,1)} %e_ref.7) | copy-start | bytes 14155780
  141.5 1.1 copy-start.5
  142.6 10.6 %copy-start.6 = (bf16[2,64,3072]{2,1,0:T(8,128)(2,1)S(1)}, bf16[2,64,3072]{2,1,0:T(8,128)(2,1)}, u32[]{:S(2)}) copy-start(bf16[2,64,3072]{2,1,0:T(8,128)(2,1)} %copy-done.4) | copy-start | bytes 2359300
  147.7 16.4 %all-to-all-start.4 = ((f32[32,16,128]{2,1,0:T(8,128)}), f32[32,16,128]{2,1,0:T(8,128)S(1)}, u32[]{:S(2)}, u32[]{:S(2)}) async-start(f32[32,16,128]{2,1,0:T(8,128)} %right_term.1), calls=%async_computation.4 | async-start | bytes 524288 | tf_op jit(solution)/shard_map/all_to_all | solution.py:389
  164.8 22.9 %all-to-all-start.5 = ((f32[32,16,128]{2,1,0:T(8,128)}), f32[32,16,128]{2,1,0:T(8,128)S(1)}, u32[]{:S(2)}, u32[]{:S(2)}) async-start(f32[32,16,128]{2,1,0:T(8,128)} %sum_copies.3), calls=%async_computation.5 | async-start | bytes 524288 | tf_op jit(solution)/shard_map/all_to_all | solution.py:389
Sparse Core Ops, SparseCore 0:
  10.2 44.9 all-gather.4
  57.1 46.3 all-gather.6

commit v6 on v4

--- a/solution.py
+++ b/solution.py
@@ -12,7 +12,6 @@
 TENSOR = ("tensor_0", "tensor_1")
 DP_TENSOR = ("dp_0", "dp_1", "tensor_0", "tensor_1")
 DP = ("dp_0", "dp_1")
-WIDE = ("dp_0", "dp_1", "tensor_0")
 F32, BF16 = jnp.float32, jnp.bfloat16
 HIGHEST = lax.Precision.HIGHEST
 VMEM = pl.BlockSpec(memory_space=pltpu.VMEM)
@@ -122,7 +121,7 @@
 
 def cut(a, b, pieces):
     rank, rows = a.shape
-    high, wide = 4, 384
+    high, wide = 16, 384
     assert pieces * high * wide == rank * rows
     return pl.pallas_call(
         cut_kernel,
@@ -145,10 +144,10 @@
         o_ref[p] = total
 
 
-def sum_copies(x, dtype):
+def sum_copies(x, count, dtype):
     return pl.pallas_call(
         sum_copies_kernel,
-        out_shape=jax.ShapeDtypeStruct(x.shape, dtype),
+        out_shape=jax.ShapeDtypeStruct((count, *x.shape[1:]), dtype),
         in_specs=[VMEM],
         out_specs=VMEM,
         cost_estimate=cost(x.size, x.size * 4),
@@ -332,20 +331,19 @@
         s_ref[0] = s.astype(BF16)
         q_ref[...] = jnp.concatenate(two_parts(q * (-1.0 / replicas)), axis=0)
 
-    step = e_ref.shape[1]
-    here = pl.ds(pl.multiple_of(d * step, step), step)
-    update = dot(t_ref[layer, here, :], q_ref[...], ((1,), (0,)))
+    update = dot(t_ref[0], q_ref[...], ((1,), (0,)))
     for which, m_ref in ((0, m0_ref), (1, m1_ref)):
 
         @pl.when(layer == which)
         def _():
-            e_ref[0] = (m_ref[here, :].astype(F32) + update).astype(BF16)
+            e_ref[0] = (m_ref[...].astype(F32) + update).astype(BF16)
 
 
 def outputs(right, inverse, turned, own_left, moments, replicas):
     rows, width = moments[0].shape
     layers, rank, share = own_left.shape
     step = 768
+    last = rows // step - 1
     return pl.pallas_call(
         functools.partial(outputs_kernel, replicas=replicas),
         out_shape=(
@@ -356,10 +354,10 @@
         in_specs=[
             pl.BlockSpec(right.shape, lambda l, d: (0, 0, 0)),
             pl.BlockSpec((1, rank, rank), lambda l, d: (l, 0, 0)),
-            VMEM,
+            pl.BlockSpec((1, step, 2 * rank), lambda l, d: (l, d, 0)),
             pl.BlockSpec((1, rank, share), lambda l, d: (l, 0, 0)),
-            VMEM,
-            VMEM,
+            pl.BlockSpec((step, width), lambda l, d: (d * (1 - l) + last * l, 0)),
+            pl.BlockSpec((step, width), lambda l, d: (d * l, 0)),
         ],
         out_specs=(
             pl.BlockSpec((1, share, width), lambda l, d: (l, 0, 0)),
@@ -368,7 +366,7 @@
         scratch_shapes=[pltpu.VMEM((2 * rank, width), BF16)],
         cost_estimate=cost(6e8, 15e6),
         name="outputs",
-        compiler_params=room(14),
+        compiler_params=room(50),
     )(right, inverse, turned, own_left, *moments)
 
 
@@ -395,14 +393,15 @@
     error_part = error_sketch(right_init, error_in)
     send, keep = left_term(core, z, out_grad, error_part)
     arrived = swapped(send)
-    terms = exchanged(cut(keep, arrived, lax.axis_size(WIDE)), WIDE)
-    own = exchanged(sum_copies(terms, BF16), WIDE)
+    terms = exchanged(cut(keep, arrived, replicas), DP)
+    terms = exchanged(sum_copies(terms, lax.axis_size("tensor_0"), F32), "tensor_0")
+    own = exchanged(sum_copies(terms, replicas, BF16), DP)
     other = swapped(own)
     left, w = own_tokens(core, own, other, out_grad, rank, lax.axis_size(TENSOR))
     w = exchanged(w, TENSOR)
     right = right_term(w, context, left_error(left, error_in), replicas)
     right = exchanged(right, DP)
-    right = exchanged(sum_copies(right, F32), DP)
+    right = exchanged(sum_copies(right, replicas, F32), DP)
     inverse, turned = inverse_of_gram(left)
     moments = []
     for layer, grad_t in enumerate(grads):

time: 159 us -> 157 us (0.987)
  local copies, waits for them, and re-layouts: 11.4 us -> 7.22 us
  Pallas kernels: 41.8 us -> 44.1 us
    unnamed x20 -> x12, local copies, waits for them, and re-layouts: 11.3 us -> 7.12 us
    pallas_call x1, Pallas kernels: 6.15 us -> 8.7 us  [outputs(): pl.pallas_call(functools.partial(outputs_kernel, replicas=replicas), out_...]
    all_to_all x2 -> x3, blocking collectives: 52.7 us -> 51.6 us  [exchanged(): return lax.all_to_all(x, axis, 0, 0, tiled=True)]
where the time goes in v6:
time: 157 us; the launch traced here: 156 us
  blocking collectives  51.6 us (33%)
  Pallas kernels  44.1 us (28%)
  starting transfers between devices  20.1 us (13%)
  waiting for transfers between devices  18.6 us (12%)
  between operations  14.1 us (9%)
  local copies, waits for them, and re-layouts  7.22 us (5%)
    all_to_all x3, blocking collectives, exchanged(): return lax.all_to_all(x, axis, 0, 0, tiled=True)  51.6 us
    all_to_all x4, starting transfers between devices, exchanged(): return lax.all_to_all(x, axis, 0, 0, tiled=True)  19.9 us
    pallas_call x2, Pallas kernels, moment_of(): pl.pallas_call(moment_kernel, out_shape=jax.ShapeDtypeStruct((rows, width...  16.7 us
    all_to_all x4, waiting for transfers between devices, exchanged(): return lax.all_to_all(x, axis, 0, 0, tiled=True)  12.9 us
    pallas_call x1, Pallas kernels, outputs(): pl.pallas_call(functools.partial(outputs_kernel, replicas=replicas), out_...  8.7 us
    unnamed x12, local copies, waits for them, and re-layouts  7.12 us
    pallas_call x1, Pallas kernels, inverse_of_gram(): pl.pallas_call(inverse_kernel, out_shape=(jax.ShapeDtypeStruct((layers, r...  6.85 us
    ppermute x2, waiting for transfers between devices, swapped(): return lax.ppermute(x, 'tensor_1', SWAP)  4.91 us
  transfers between devices with their start and end apart: 8, of which 5 were waited for; matrix products, arithmetic and copies ran while one was open for 0% of the time, Pallas kernels for 22%

profile of v6, /device:TPU:2, one launch (start us, length us, event | category | flops | bytes accessed | tf_op | source)
XLA Modules:
  0.0 155.7 jit_solution(9257935009811724757)
XLA Ops:
  7.2 0.0 all-gather.5.cloned.1.call-start
  7.2 0.0 copy-start.3
  7.2 1.4 copy-done.3
  8.6 1.4 turn.1
  10.0 0.0 all-gather.5.cloned.1.call-update
  10.1 0.0 all-gather.7.cloned.1.call-start
  10.1 0.7 all-gather.7.cloned.1.call-update
  10.8 2.9 %sketch.1 = bf16[8,2,64,128]{3,2,1,0:T(8,128)(2,1)} custom-call(f32[2,64,384]{2,1,0:T(8,128)} %r_ref.3, bf16[2,1024,384]{2,1,0:T(8,128)(2,1)} %x_ref.7), custom_call_target="tpu_custom_call" | custom-call | flops 400000000 | bytes 2000000 | tf_op jit(solution)/shard_map/sketch/pallas_call | solution.py:51
  13.7 4.5 %all-to-all-start = ((bf16[8,2,64,128]{3,2,1,0:T(8,128)(2,1)}), bf16[8,2,64,128]{3,2,1,0:T(8,128)(2,1)S(1)}, u32[]{:S(2)}, u32[]{:S(2)}) async-start(bf16[8,2,64,128]{3,2,1,0:T(8,128)(2,1)} %sketch.1), calls=%async_computation | async-start | bytes 524288 | tf_op jit(solution)/shard_map/all_to_all | solution.py:374
  18.2 0.0 copy-start
  18.2 2.3 %copy-done = bf16[2,3072,384]{2,1,0:T(8,128)(2,1)S(1)} copy-done((bf16[2,3072,384]{2,1,0:T(8,128)(2,1)S(1)}, bf16[2,3072,384]{2,1,0:T(8,128)(2,1)}, u32[]{:S(2)}) %copy-start) | copy-done | bytes 4718616
  20.5 0.0 copy-start.5
  20.5 0.9 copy-done.5
  21.4 0.0 copy-start.4
  21.4 2.7 %error_sketch.1.e_ref = f32[2,64,3072]{2,1,0:T(8,128)S(1)} custom-call(f32[2,64,384]{2,1,0:T(8,128)S(1)} %copy-done.5, bf16[2,3072,384]{2,1,0:T(8,128)(2,1)S(1)} %copy-done), custom_call_target="tpu_custom_call" | custom-call | flops 600000000 | bytes 7000000 | tf_op jit(solution)/shard_map/error_sketch/pallas_call | solution.py:73
  24.1 1.5 all-to-all-done.z_ref
  25.7 0.0 copy-done.4
  25.7 0.6 left_term.1
  26.2 0.1 collective-permute-start
  26.3 3.1 %collective-permute-done.b_ref = f32[64,3072]{1,0:T(8,128)S(1)} collective-permute-done((f32[64,3072]{1,0:T(8,128)S(1)}, f32[64,3072]{1,0:T(8,128)S(1)}, u32[]{:S(2)}, u32[]{:S(2)}) %collective-permute-start) | collective-permute-done | bytes 786464 | tf_op jit(solution)/shard_map/ppermute | solution.py:381
  29.4 0.1 cut.1
  29.5 24.0 %all_to_all.35.x_ref = bf16[32,16,384]{2,1,0:T(8,128)(2,1)S(1)} all-to-all(bf16[32,16,384]{2,1,0:T(8,128)(2,1)S(1)} %cut.1), channel_id=1, replica_groups=mesh['dp_0'=4,'dp_1'=8,'tensor_0'=4,'tensor_1'=2] {'dp_0','dp_1'}, dimensions={0} | all-to-all | bytes 786432 | tf_op jit(solution)/shard_map/all_to_all | solution.py:374
  53.5 0.1 sum_copies.3
  53.6 9.4 %all_to_all.36.x_ref = f32[4,16,384]{2,1,0:T(8,128)S(1)} all-to-all(f32[4,16,384]{2,1,0:T(8,128)S(1)} %sum_copies.3), channel_id=1, replica_groups=mesh['dp_0'=4,'dp_1'=8,'tensor_0'=4,'tensor_1'=2] {'tensor_0'}, dimensions={0} | all-to-all | bytes 196608 | tf_op jit(solution)/shard_map/all_to_all | solution.py:374
  63.0 18.1 %all_to_all.37.a_ref = bf16[32,16,384]{2,1,0:T(8,128)(2,1)S(1)} all-to-all(bf16[32,16,384]{2,1,0:T(8,128)(2,1)S(1)} %sum_copies.4), channel_id=1, replica_groups=mesh['dp_0'=4,'dp_1'=8,'tensor_0'=4,'tensor_1'=2] {'dp_0','dp_1'}, dimensions={0} | all-to-all | bytes 786432 | tf_op jit(solution)/shard_map/all_to_all | solution.py:374
  81.2 0.0 collective-permute-start.1
  81.2 1.8 %collective-permute-done.1.b_ref = bf16[32,16,384]{2,1,0:T(8,128)(2,1)S(1)} collective-permute-done((bf16[32,16,384]{2,1,0:T(8,128)(2,1)S(1)}, bf16[32,16,384]{2,1,0:T(8,128)(2,1)S(1)}, u32[]{:S(2)}, u32[]{:S(2)}) %collective-permute-start.1) | collective-permute-done | bytes 393248 | tf_op jit(solution)/shard_map/ppermute | solution.py:381
  83.0 1.4 own_tokens.1
  84.4 3.4 %all-to-all-start.4 = ((bf16[8,2,64,128]{3,2,1,0:T(8,128)(2,1)}), bf16[8,2,64,128]{3,2,1,0:T(8,128)(2,1)S(1)}, u32[]{:S(2)}, u32[]{:S(2)}) async-start(bf16[8,2,64,128]{3,2,1,0:T(8,128)(2,1)} %get-tuple-element.12), calls=%async_computation.4 | async-start | bytes 524288 | tf_op jit(solution)/shard_map/all_to_all | solution.py:374
  87.9 0.0 copy-start.1
  87.9 2.5 %copy-done.1 = bf16[2,3072,384]{2,1,0:T(8,128)(2,1)S(1)} copy-done((bf16[2,3072,384]{2,1,0:T(8,128)(2,1)S(1)}, bf16[2,3072,384]{2,1,0:T(8,128)(2,1)}, u32[]{:S(2)}) %copy-start.1) | copy-done | bytes 4718616
  90.3 0.0 copy-start.2
  90.3 0.9 left_error.1.e_ref
  91.2 7.3 %all-to-all-done.4.w_ref = bf16[8,2,64,128]{3,2,1,0:T(8,128)(2,1)S(1)} async-done(((bf16[8,2,64,128]{3,2,1,0:T(8,128)(2,1)}), bf16[8,2,64,128]{3,2,1,0:T(8,128)(2,1)S(1)}, u32[]{:S(2)}, u32[]{:S(2)}) %all-to-all-start.4) | async-done | bytes 262176 | tf_op jit(solution)/shard_map/all_to_all | solution.py:374
  98.5 0.0 copy-done.2
  98.5 1.1 right_term.1
  99.6 6.3 %all-to-all-start.5 = ((f32[32,16,128]{2,1,0:T(8,128)}), f32[32,16,128]{2,1,0:T(8,128)S(1)}, u32[]{:S(2)}, u32[]{:S(2)}) async-start(f32[32,16,128]{2,1,0:T(8,128)} %right_term.1), calls=%async_computation.5 | async-start | bytes 524288 | tf_op jit(solution)/shard_map/all_to_all | solution.py:374
  105.9 0.1 constant_dynamic-slice_fusion.own_ref
  106.0 6.9 %gram_inverse.1 = (f32[2,64,64]{2,1,0:T(8,128)S(1)}, bf16[2,3072,128]{2,1,0:T(8,128)(2,1)S(1)}) custom-call(bf16[2,64,3072]{2,1,0:T(8,128)(2,1)S(1)} %get-tuple-element.13.l_ref), custom_call_target="tpu_custom_call" | custom-call | flops 5000000000 | bytes 2000000 | tf_op jit(solution)/shard_map/gram_inverse/pallas_call | solution.py:303
  112.9 4.1 %all-to-all-done.5.x_ref = f32[32,16,128]{2,1,0:T(8,128)S(1)} async-done(((f32[32,16,128]{2,1,0:T(8,128)}), f32[32,16,128]{2,1,0:T(8,128)S(1)}, u32[]{:S(2)}, u32[]{:S(2)}) %all-to-all-start.5) | async-done | bytes 262176 | tf_op jit(solution)/shard_map/all_to_all | solution.py:374
  117.0 0.7 sum_copies.5
  117.7 5.7 %all-to-all-start.6 = ((f32[32,16,128]{2,1,0:T(8,128)}), f32[32,16,128]{2,1,0:T(8,128)S(1)}, u32[]{:S(2)}, u32[]{:S(2)}) async-start(f32[32,16,128]{2,1,0:T(8,128)} %sum_copies.5), calls=%async_computation.6 | async-start | bytes 524288 | tf_op jit(solution)/shard_map/all_to_all | solution.py:374
  123.4 0.0 all-gather.5.cloned.1.call-done
  123.4 8.4 %shard_map.59.m0_ref = bf16[3072,384]{1,0:T(8,128)(2,1)} custom-call(bf16[8,3072,128]{2,1,0:T(8,128)(2,1)} %bitcast.3, bf16[2,1024,384]{2,1,0:T(8,128)(2,1)} %x_ref.7, bf16[2,3072,384]{2,1,0:T(8,128)(2,1)} %e_ref.7), custom_call_target="tpu_custom_call" | custom-call | flops 4000000000 | bytes 14000000 | tf_op jit(solution)/shard_map/pallas_call | solution.py:261
  131.8 0.0 all-gather.7.cloned.1.call-done
  131.8 8.4 %shard_map.60.m1_ref = bf16[3072,384]{1,0:T(8,128)(2,1)} custom-call(bf16[8,3072,128]{2,1,0:T(8,128)(2,1)} %bitcast.4, bf16[2,1024,384]{2,1,0:T(8,128)(2,1)} %x_ref.7, bf16[2,3072,384]{2,1,0:T(8,128)(2,1)} %e_ref.7), custom_call_target="tpu_custom_call" | custom-call | flops 4000000000 | bytes 14000000 | tf_op jit(solution)/shard_map/pallas_call | solution.py:261
  140.2 0.0 all-to-all-done.6.r_ref
  140.2 8.7 %outputs.1 = (bf16[2,96,384]{2,1,0:T(8,128)(2,1)}, bf16[2,3072,384]{2,1,0:T(8,128)(2,1)}) custom-call(f32[32,16,128]{2,1,0:T(8,128)S(1)} %all-to-all-done.6.r_ref, f32[2,64,64]{2,1,0:T(8,128)S(1)} %get-tuple-element.14.g_ref, bf16[2,3072,128]{2,1,0:T(8,128)(2,1)S(1)} %get-tuple-element.15.t_ref, bf16[2,64,96]{2,1,0:T(8,128)(2,1)S(1)} %constant_dynamic-slice_fusion.own_ref, ...), custom_call_target="tpu_custom_call" | custom-call | flops 600000000 | bytes 15000000 | tf_op jit(solution)/shard_map/outputs/pallas_call | solution.py:347
  (1 shorter events, 0.0 us)
Async XLA Ops:
  7.2 116.3 %all-gather.5.cloned.1.call-start = ((), (), s32[]{:S(2)}) async-start(), calls=%async_computation.7 | async-start | bytes 7077888 | tf_op jit(solution)/shard_map/all_gather | solution.py:392
  7.2 1.4 copy-start.3
  10.1 121.7 %all-gather.7.cloned.1.call-start = ((), (), s32[]{:S(2)}) async-start(), calls=%async_computation.8 | async-start | bytes 7077888 | tf_op jit(solution)/shard_map/all_gather | solution.py:392
  13.7 12.0 %all-to-all-start = ((bf16[8,2,64,128]{3,2,1,0:T(8,128)(2,1)}), bf16[8,2,64,128]{3,2,1,0:T(8,128)(2,1)S(1)}, u32[]{:S(2)}, u32[]{:S(2)}) async-start(bf16[8,2,64,128]{3,2,1,0:T(8,128)(2,1)} %sketch.1), calls=%async_computation | async-start | bytes 524288 | tf_op jit(solution)/shard_map/all_to_all | solution.py:374
  18.2 2.3 %copy-start = (bf16[2,3072,384]{2,1,0:T(8,128)(2,1)S(1)}, bf16[2,3072,384]{2,1,0:T(8,128)(2,1)}, u32[]{:S(2)}) copy-start(bf16[2,3072,384]{2,1,0:T(8,128)(2,1)} %e_ref.7) | copy-start | bytes 14155780
  20.5 0.9 copy-start.5
  21.4 4.2 %copy-start.4 = (bf16[2,128,3072]{2,1,0:T(8,128)(2,1)S(1)}, bf16[2,128,3072]{2,1,0:T(8,128)(2,1)}, u32[]{:S(2)}) copy-start(bf16[2,128,3072]{2,1,0:T(8,128)(2,1)} %y_ref.5) | copy-start | bytes 4718596
  26.2 3.2 %collective-permute-start = (f32[64,3072]{1,0:T(8,128)S(1)}, f32[64,3072]{1,0:T(8,128)S(1)}, u32[]{:S(2)}, u32[]{:S(2)}) collective-permute-start(f32[64,3072]{1,0:T(8,128)S(1)} %get-tuple-element.11), channel_id=1, source_target_pairs={{0,1},{1,0},{2,3},{3,2},{4,5},{5,4},{6,7},{7,6},{8,9},{9,8},{10,11... | collective-permute-start | bytes 2359304 | tf_op jit(solution)/shard_map/ppermute | solution.py:381
  81.2 1.8 %collective-permute-start.1 = (bf16[32,16,384]{2,1,0:T(8,128)(2,1)S(1)}, bf16[32,16,384]{2,1,0:T(8,128)(2,1)S(1)}, u32[]{:S(2)}, u32[]{:S(2)}) collective-permute-start(bf16[32,16,384]{2,1,0:T(8,128)(2,1)S(1)} %all_to_all.37.a_ref), channel_id=1, source_target_pairs={{0,1},{1,0},{2,3},{3,2},{4,5},{5,4},{6,7},{7,6},{8,9},{9,8},{10,11... | collective-permute-start | bytes 1179656 | tf_op jit(solution)/shard_map/ppermute | solution.py:381
  84.4 14.1 %all-to-all-start.4 = ((bf16[8,2,64,128]{3,2,1,0:T(8,128)(2,1)}), bf16[8,2,64,128]{3,2,1,0:T(8,128)(2,1)S(1)}, u32[]{:S(2)}, u32[]{:S(2)}) async-start(bf16[8,2,64,128]{3,2,1,0:T(8,128)(2,1)} %get-tuple-element.12), calls=%async_computation.4 | async-start | bytes 524288 | tf_op jit(solution)/shard_map/all_to_all | solution.py:374
  87.9 2.5 %copy-start.1 = (bf16[2,3072,384]{2,1,0:T(8,128)(2,1)S(1)}, bf16[2,3072,384]{2,1,0:T(8,128)(2,1)}, u32[]{:S(2)}) copy-start(bf16[2,3072,384]{2,1,0:T(8,128)(2,1)} %e_ref.7) | copy-start | bytes 14155780
  90.3 8.2 %copy-start.2 = (bf16[2,1024,384]{2,1,0:T(8,128)(2,1)S(1)}, bf16[2,1024,384]{2,1,0:T(8,128)(2,1)}, u32[]{:S(2)}) copy-start(bf16[2,1024,384]{2,1,0:T(8,128)(2,1)} %x_ref.7) | copy-start | bytes 4718596
  99.6 17.3 %all-to-all-start.5 = ((f32[32,16,128]{2,1,0:T(8,128)}), f32[32,16,128]{2,1,0:T(8,128)S(1)}, u32[]{:S(2)}, u32[]{:S(2)}) async-start(f32[32,16,128]{2,1,0:T(8,128)} %right_term.1), calls=%async_computation.5 | async-start | bytes 524288 | tf_op jit(solution)/shard_map/all_to_all | solution.py:374
  117.7 22.5 %all-to-all-start.6 = ((f32[32,16,128]{2,1,0:T(8,128)}), f32[32,16,128]{2,1,0:T(8,128)S(1)}, u32[]{:S(2)}, u32[]{:S(2)}) async-start(f32[32,16,128]{2,1,0:T(8,128)} %sum_copies.5), calls=%async_computation.6 | async-start | bytes 524288 | tf_op jit(solution)/shard_map/all_to_all | solution.py:374
Sparse Core Ops, SparseCore 0:
  10.4 46.3 all-gather.4
  58.6 46.2 all-gather.6

commit v7 on v6

--- a/solution.py
+++ b/solution.py
@@ -207,22 +207,21 @@
 
 
 def right_term_kernel(w_ref, x_ref, e_ref, o_ref):
-    layers, rank, width = e_ref.shape
-    count, lanes = rank // 16, width // 128
+    layers, rank, _ = e_ref.shape
+    high = o_ref.shape[1]
     for layer in range(layers):
         w = jnp.concatenate([w_ref[k, layer] for k in range(w_ref.shape[0])], axis=1)
-        right = dot(w, x_ref[layer], ((1,), (0,))) + e_ref[layer]
-        for i in range(count):
-            for j in range(lanes):
-                o_ref[(layer * count + i) * lanes + j] = right[i * 16 : i * 16 + 16, j * 128 : j * 128 + 128]
-    for p in range(layers * count * lanes, o_ref.shape[0]):
-        o_ref[p] = jnp.zeros(o_ref.shape[1:], o_ref.dtype)
+        right = (dot(w, x_ref[layer], ((1,), (0,))) + e_ref[layer]).astype(BF16)
+        for i in range(rank // high):
+            o_ref[layer * (rank // high) + i] = right[i * high : i * high + high]
 
 
 def right_term(w, context, error_part, pieces):
+    layers, rank, width = error_part.shape
+    high = layers * rank // pieces
     return pl.pallas_call(
         right_term_kernel,
-        out_shape=jax.ShapeDtypeStruct((pieces, 16, 128), F32),
+        out_shape=jax.ShapeDtypeStruct((pieces, high, width), BF16),
         in_specs=[VMEM, VMEM, VMEM],
         out_specs=VMEM,
         cost_estimate=cost(2e8, 3e6),
@@ -316,15 +315,12 @@
 
 def outputs_kernel(r_ref, g_ref, t_ref, own_ref, m0_ref, m1_ref, s_ref, e_ref, q_ref, *, replicas):
     layer, d = pl.program_id(0), pl.program_id(1)
-    rank, width = g_ref.shape[1], m0_ref.shape[1]
-    count, lanes = rank // 16, width // 128
+    rank = g_ref.shape[1]
+    count = rank // r_ref.shape[1]
 
     @pl.when(d == 0)
     def _():
-        rows = [
-            jnp.concatenate([r_ref[(layer * count + i) * lanes + j] for j in range(lanes)], axis=1)
-            for i in range(count)
-        ]
+        rows = [r_ref[layer * count + i] for i in range(count)]
         q = dot(g_ref[0], jnp.concatenate(rows, axis=0), ((1,), (0,)), precision=HIGHEST)
         own = own_ref[0]
         s = dot(jnp.concatenate([own, own], axis=0), jnp.concatenate(two_parts(q), axis=0), ((0,), (0,)))

time: 157 us -> 157 us (level)
  waiting for transfers between devices: 18.6 us -> 16.5 us
  starting transfers between devices: 20.1 us -> 22.1 us
    all_to_all x4, starting transfers between devices: 19.9 us -> 22 us  [exchanged(): return lax.all_to_all(x, axis, 0, 0, tiled=True)]
    all_to_all x4, waiting for transfers between devices: 12.9 us -> 10.9 us  [exchanged(): return lax.all_to_all(x, axis, 0, 0, tiled=True)]
where the time goes in v7:
time: 157 us; the launch traced here: 156 us
  blocking collectives  51.6 us (33%)
  Pallas kernels  44 us (28%)
  starting transfers between devices  22.1 us (14%)
  waiting for transfers between devices  16.5 us (11%)
  between operations  14.1 us (9%)
  local copies, waits for them, and re-layouts  7.21 us (5%)
    all_to_all x3, blocking collectives, exchanged(): return lax.all_to_all(x, axis, 0, 0, tiled=True)  51.6 us
    all_to_all x4, starting transfers between devices, exchanged(): return lax.all_to_all(x, axis, 0, 0, tiled=True)  22 us
    pallas_call x2, Pallas kernels, moment_of(): pl.pallas_call(moment_kernel, out_shape=jax.ShapeDtypeStruct((rows, width...  16.7 us
    all_to_all x4, waiting for transfers between devices, exchanged(): return lax.all_to_all(x, axis, 0, 0, tiled=True)  10.9 us
    pallas_call x1, Pallas kernels, outputs(): pl.pallas_call(functools.partial(outputs_kernel, replicas=replicas), out_...  8.7 us
    unnamed x12, local copies, waits for them, and re-layouts  7.12 us
    pallas_call x1, Pallas kernels, inverse_of_gram(): pl.pallas_call(inverse_kernel, out_shape=(jax.ShapeDtypeStruct((layers, r...  6.85 us
    ppermute x2, waiting for transfers between devices, swapped(): return lax.ppermute(x, 'tensor_1', SWAP)  4.91 us
  transfers between devices with their start and end apart: 8, of which 5 were waited for; matrix products, arithmetic and copies ran while one was open for 0% of the time, Pallas kernels for 22%

profile of v7, /device:TPU:2, one launch (start us, length us, event | category | flops | bytes accessed | tf_op | source)
XLA Modules:
  0.0 155.6 jit_solution(7014183626410834122)
XLA Ops:
  7.2 0.0 all-gather.5.cloned.1.call-start
  7.2 0.0 copy-start.3
  7.2 1.4 copy-done.3
  8.6 1.4 turn.1
  10.0 0.0 all-gather.5.cloned.1.call-update
  10.1 0.0 all-gather.7.cloned.1.call-start
  10.1 0.7 all-gather.7.cloned.1.call-update
  10.8 2.9 %sketch.1 = bf16[8,2,64,128]{3,2,1,0:T(8,128)(2,1)} custom-call(f32[2,64,384]{2,1,0:T(8,128)} %r_ref.3, bf16[2,1024,384]{2,1,0:T(8,128)(2,1)} %x_ref.7), custom_call_target="tpu_custom_call" | custom-call | flops 400000000 | bytes 2000000 | tf_op jit(solution)/shard_map/sketch/pallas_call | solution.py:51
  13.7 4.5 %all-to-all-start = ((bf16[8,2,64,128]{3,2,1,0:T(8,128)(2,1)}), bf16[8,2,64,128]{3,2,1,0:T(8,128)(2,1)S(1)}, u32[]{:S(2)}, u32[]{:S(2)}) async-start(bf16[8,2,64,128]{3,2,1,0:T(8,128)(2,1)} %sketch.1), calls=%async_computation | async-start | bytes 524288 | tf_op jit(solution)/shard_map/all_to_all | solution.py:370
  18.2 0.0 copy-start
  18.2 2.3 %copy-done = bf16[2,3072,384]{2,1,0:T(8,128)(2,1)S(1)} copy-done((bf16[2,3072,384]{2,1,0:T(8,128)(2,1)S(1)}, bf16[2,3072,384]{2,1,0:T(8,128)(2,1)}, u32[]{:S(2)}) %copy-start) | copy-done | bytes 4718616
  20.5 0.0 copy-start.5
  20.5 0.9 copy-done.5
  21.4 0.0 copy-start.4
  21.4 2.7 %error_sketch.1.e_ref = f32[2,64,3072]{2,1,0:T(8,128)S(1)} custom-call(f32[2,64,384]{2,1,0:T(8,128)S(1)} %copy-done.5, bf16[2,3072,384]{2,1,0:T(8,128)(2,1)S(1)} %copy-done), custom_call_target="tpu_custom_call" | custom-call | flops 600000000 | bytes 7000000 | tf_op jit(solution)/shard_map/error_sketch/pallas_call | solution.py:73
  24.1 1.5 all-to-all-done.z_ref
  25.7 0.0 copy-done.4
  25.7 0.6 left_term.1
  26.2 0.1 collective-permute-start
  26.3 3.1 %collective-permute-done.b_ref = f32[64,3072]{1,0:T(8,128)S(1)} collective-permute-done((f32[64,3072]{1,0:T(8,128)S(1)}, f32[64,3072]{1,0:T(8,128)S(1)}, u32[]{:S(2)}, u32[]{:S(2)}) %collective-permute-start) | collective-permute-done | bytes 786464 | tf_op jit(solution)/shard_map/ppermute | solution.py:377
  29.4 0.1 cut.1
  29.5 24.0 %all_to_all.35.x_ref = bf16[32,16,384]{2,1,0:T(8,128)(2,1)S(1)} all-to-all(bf16[32,16,384]{2,1,0:T(8,128)(2,1)S(1)} %cut.1), channel_id=1, replica_groups=mesh['dp_0'=4,'dp_1'=8,'tensor_0'=4,'tensor_1'=2] {'dp_0','dp_1'}, dimensions={0} | all-to-all | bytes 786432 | tf_op jit(solution)/shard_map/all_to_all | solution.py:370
  53.5 0.1 sum_copies.3
  53.6 9.4 %all_to_all.36.x_ref = f32[4,16,384]{2,1,0:T(8,128)S(1)} all-to-all(f32[4,16,384]{2,1,0:T(8,128)S(1)} %sum_copies.3), channel_id=1, replica_groups=mesh['dp_0'=4,'dp_1'=8,'tensor_0'=4,'tensor_1'=2] {'tensor_0'}, dimensions={0} | all-to-all | bytes 196608 | tf_op jit(solution)/shard_map/all_to_all | solution.py:370
  63.0 18.1 %all_to_all.37.a_ref = bf16[32,16,384]{2,1,0:T(8,128)(2,1)S(1)} all-to-all(bf16[32,16,384]{2,1,0:T(8,128)(2,1)S(1)} %sum_copies.4), channel_id=1, replica_groups=mesh['dp_0'=4,'dp_1'=8,'tensor_0'=4,'tensor_1'=2] {'dp_0','dp_1'}, dimensions={0} | all-to-all | bytes 786432 | tf_op jit(solution)/shard_map/all_to_all | solution.py:370
  81.2 0.0 collective-permute-start.1
  81.2 1.8 %collective-permute-done.1.b_ref = bf16[32,16,384]{2,1,0:T(8,128)(2,1)S(1)} collective-permute-done((bf16[32,16,384]{2,1,0:T(8,128)(2,1)S(1)}, bf16[32,16,384]{2,1,0:T(8,128)(2,1)S(1)}, u32[]{:S(2)}, u32[]{:S(2)}) %collective-permute-start.1) | collective-permute-done | bytes 393248 | tf_op jit(solution)/shard_map/ppermute | solution.py:377
  83.0 1.4 own_tokens.1
  84.4 3.4 %all-to-all-start.4 = ((bf16[8,2,64,128]{3,2,1,0:T(8,128)(2,1)}), bf16[8,2,64,128]{3,2,1,0:T(8,128)(2,1)S(1)}, u32[]{:S(2)}, u32[]{:S(2)}) async-start(bf16[8,2,64,128]{3,2,1,0:T(8,128)(2,1)} %get-tuple-element.12), calls=%async_computation.4 | async-start | bytes 524288 | tf_op jit(solution)/shard_map/all_to_all | solution.py:370
  87.9 0.0 copy-start.1
  87.9 2.5 %copy-done.1 = bf16[2,3072,384]{2,1,0:T(8,128)(2,1)S(1)} copy-done((bf16[2,3072,384]{2,1,0:T(8,128)(2,1)S(1)}, bf16[2,3072,384]{2,1,0:T(8,128)(2,1)}, u32[]{:S(2)}) %copy-start.1) | copy-done | bytes 4718616
  90.3 0.0 copy-start.2
  90.3 0.9 left_error.1.e_ref
  91.2 7.3 %all-to-all-done.4.w_ref = bf16[8,2,64,128]{3,2,1,0:T(8,128)(2,1)S(1)} async-done(((bf16[8,2,64,128]{3,2,1,0:T(8,128)(2,1)}), bf16[8,2,64,128]{3,2,1,0:T(8,128)(2,1)S(1)}, u32[]{:S(2)}, u32[]{:S(2)}) %all-to-all-start.4) | async-done | bytes 262176 | tf_op jit(solution)/shard_map/all_to_all | solution.py:370
  98.5 0.0 copy-done.2
  98.5 1.0 right_term.1
  99.5 6.3 %all-to-all-start.5 = ((bf16[32,4,384]{2,1,0:T(4,128)(2,1)}), bf16[32,4,384]{2,1,0:T(4,128)(2,1)S(1)}, u32[]{:S(2)}, u32[]{:S(2)}) async-start(bf16[32,4,384]{2,1,0:T(4,128)(2,1)} %right_term.1), calls=%async_computation.5 | async-start | bytes 196608 | tf_op jit(solution)/shard_map/all_to_all | solution.py:370
  105.9 6.9 %gram_inverse.1 = (f32[2,64,64]{2,1,0:T(8,128)S(1)}, bf16[2,3072,128]{2,1,0:T(8,128)(2,1)S(1)}) custom-call(bf16[2,64,3072]{2,1,0:T(8,128)(2,1)S(1)} %get-tuple-element.13.l_ref), custom_call_target="tpu_custom_call" | custom-call | flops 5000000000 | bytes 2000000 | tf_op jit(solution)/shard_map/gram_inverse/pallas_call | solution.py:302
  112.7 0.1 constant_dynamic-slice_fusion.own_ref
  112.8 2.0 %all-to-all-done.5.x_ref = bf16[32,4,384]{2,1,0:T(4,128)(2,1)S(1)} async-done(((bf16[32,4,384]{2,1,0:T(4,128)(2,1)}), bf16[32,4,384]{2,1,0:T(4,128)(2,1)S(1)}, u32[]{:S(2)}, u32[]{:S(2)}) %all-to-all-start.5) | async-done | bytes 98336 | tf_op jit(solution)/shard_map/all_to_all | solution.py:370
  114.8 0.7 sum_copies.5
  115.5 7.8 %all-to-all-start.6 = ((f32[32,4,384]{2,1,0:T(4,128)}), f32[32,4,384]{2,1,0:T(4,128)S(1)}, u32[]{:S(2)}, u32[]{:S(2)}) async-start(f32[32,4,384]{2,1,0:T(4,128)} %sum_copies.5), calls=%async_computation.6 | async-start | bytes 393216 | tf_op jit(solution)/shard_map/all_to_all | solution.py:370
  123.3 0.0 all-gather.5.cloned.1.call-done
  123.3 8.4 %shard_map.59.m0_ref = bf16[3072,384]{1,0:T(8,128)(2,1)} custom-call(bf16[8,3072,128]{2,1,0:T(8,128)(2,1)} %bitcast.3, bf16[2,1024,384]{2,1,0:T(8,128)(2,1)} %x_ref.7, bf16[2,3072,384]{2,1,0:T(8,128)(2,1)} %e_ref.7), custom_call_target="tpu_custom_call" | custom-call | flops 4000000000 | bytes 14000000 | tf_op jit(solution)/shard_map/pallas_call | solution.py:260
  131.7 0.0 all-gather.7.cloned.1.call-done
  131.7 8.4 %shard_map.60.m1_ref = bf16[3072,384]{1,0:T(8,128)(2,1)} custom-call(bf16[8,3072,128]{2,1,0:T(8,128)(2,1)} %bitcast.4, bf16[2,1024,384]{2,1,0:T(8,128)(2,1)} %x_ref.7, bf16[2,3072,384]{2,1,0:T(8,128)(2,1)} %e_ref.7), custom_call_target="tpu_custom_call" | custom-call | flops 4000000000 | bytes 14000000 | tf_op jit(solution)/shard_map/pallas_call | solution.py:260
  140.1 0.0 all-to-all-done.6.r_ref
  140.1 8.7 %outputs.1 = (bf16[2,96,384]{2,1,0:T(8,128)(2,1)}, bf16[2,3072,384]{2,1,0:T(8,128)(2,1)}) custom-call(f32[32,4,384]{2,1,0:T(4,128)S(1)} %all-to-all-done.6.r_ref, f32[2,64,64]{2,1,0:T(8,128)S(1)} %get-tuple-element.14.g_ref, bf16[2,3072,128]{2,1,0:T(8,128)(2,1)S(1)} %get-tuple-element.15.t_ref, bf16[2,64,96]{2,1,0:T(8,128)(2,1)S(1)} %constant_dynamic-slice_fusion.own_ref, ...), custom_call_target="tpu_custom_call" | custom-call | flops 600000000 | bytes 15000000 | tf_op jit(solution)/shard_map/outputs/pallas_call | solution.py:343
  (1 shorter events, 0.0 us)
Async XLA Ops:
  7.2 116.2 %all-gather.5.cloned.1.call-start = ((), (), s32[]{:S(2)}) async-start(), calls=%async_computation.7 | async-start | bytes 7077888 | tf_op jit(solution)/shard_map/all_gather | solution.py:388
  7.2 1.4 copy-start.3
  10.1 121.6 %all-gather.7.cloned.1.call-start = ((), (), s32[]{:S(2)}) async-start(), calls=%async_computation.8 | async-start | bytes 7077888 | tf_op jit(solution)/shard_map/all_gather | solution.py:388
  13.7 12.0 %all-to-all-start = ((bf16[8,2,64,128]{3,2,1,0:T(8,128)(2,1)}), bf16[8,2,64,128]{3,2,1,0:T(8,128)(2,1)S(1)}, u32[]{:S(2)}, u32[]{:S(2)}) async-start(bf16[8,2,64,128]{3,2,1,0:T(8,128)(2,1)} %sketch.1), calls=%async_computation | async-start | bytes 524288 | tf_op jit(solution)/shard_map/all_to_all | solution.py:370
  18.2 2.3 %copy-start = (bf16[2,3072,384]{2,1,0:T(8,128)(2,1)S(1)}, bf16[2,3072,384]{2,1,0:T(8,128)(2,1)}, u32[]{:S(2)}) copy-start(bf16[2,3072,384]{2,1,0:T(8,128)(2,1)} %e_ref.7) | copy-start | bytes 14155780
  20.5 0.9 copy-start.5
  21.4 4.2 %copy-start.4 = (bf16[2,128,3072]{2,1,0:T(8,128)(2,1)S(1)}, bf16[2,128,3072]{2,1,0:T(8,128)(2,1)}, u32[]{:S(2)}) copy-start(bf16[2,128,3072]{2,1,0:T(8,128)(2,1)} %y_ref.5) | copy-start | bytes 4718596
  26.2 3.2 %collective-permute-start = (f32[64,3072]{1,0:T(8,128)S(1)}, f32[64,3072]{1,0:T(8,128)S(1)}, u32[]{:S(2)}, u32[]{:S(2)}) collective-permute-start(f32[64,3072]{1,0:T(8,128)S(1)} %get-tuple-element.11), channel_id=1, source_target_pairs={{0,1},{1,0},{2,3},{3,2},{4,5},{5,4},{6,7},{7,6},{8,9},{9,8},{10,11... | collective-permute-start | bytes 2359304 | tf_op jit(solution)/shard_map/ppermute | solution.py:377
  81.2 1.8 %collective-permute-start.1 = (bf16[32,16,384]{2,1,0:T(8,128)(2,1)S(1)}, bf16[32,16,384]{2,1,0:T(8,128)(2,1)S(1)}, u32[]{:S(2)}, u32[]{:S(2)}) collective-permute-start(bf16[32,16,384]{2,1,0:T(8,128)(2,1)S(1)} %all_to_all.37.a_ref), channel_id=1, source_target_pairs={{0,1},{1,0},{2,3},{3,2},{4,5},{5,4},{6,7},{7,6},{8,9},{9,8},{10,11... | collective-permute-start | bytes 1179656 | tf_op jit(solution)/shard_map/ppermute | solution.py:377
  84.4 14.1 %all-to-all-start.4 = ((bf16[8,2,64,128]{3,2,1,0:T(8,128)(2,1)}), bf16[8,2,64,128]{3,2,1,0:T(8,128)(2,1)S(1)}, u32[]{:S(2)}, u32[]{:S(2)}) async-start(bf16[8,2,64,128]{3,2,1,0:T(8,128)(2,1)} %get-tuple-element.12), calls=%async_computation.4 | async-start | bytes 524288 | tf_op jit(solution)/shard_map/all_to_all | solution.py:370
  87.9 2.5 %copy-start.1 = (bf16[2,3072,384]{2,1,0:T(8,128)(2,1)S(1)}, bf16[2,3072,384]{2,1,0:T(8,128)(2,1)}, u32[]{:S(2)}) copy-start(bf16[2,3072,384]{2,1,0:T(8,128)(2,1)} %e_ref.7) | copy-start | bytes 14155780
  90.3 8.2 %copy-start.2 = (bf16[2,1024,384]{2,1,0:T(8,128)(2,1)S(1)}, bf16[2,1024,384]{2,1,0:T(8,128)(2,1)}, u32[]{:S(2)}) copy-start(bf16[2,1024,384]{2,1,0:T(8,128)(2,1)} %x_ref.7) | copy-start | bytes 4718596
  99.5 15.3 %all-to-all-start.5 = ((bf16[32,4,384]{2,1,0:T(4,128)(2,1)}), bf16[32,4,384]{2,1,0:T(4,128)(2,1)S(1)}, u32[]{:S(2)}, u32[]{:S(2)}) async-start(bf16[32,4,384]{2,1,0:T(4,128)(2,1)} %right_term.1), calls=%async_computation.5 | async-start | bytes 196608 | tf_op jit(solution)/shard_map/all_to_all | solution.py:370
  115.5 24.6 %all-to-all-start.6 = ((f32[32,4,384]{2,1,0:T(4,128)}), f32[32,4,384]{2,1,0:T(4,128)S(1)}, u32[]{:S(2)}, u32[]{:S(2)}) async-start(f32[32,4,384]{2,1,0:T(4,128)} %sum_copies.5), calls=%async_computation.6 | async-start | bytes 393216 | tf_op jit(solution)/shard_map/all_to_all | solution.py:370
Sparse Core Ops, SparseCore 0:
  10.4 46.3 all-gather.4
  58.6 46.2 all-gather.6
